TPU v7x, 768 devices: a whole 4x8x12 slice. The times are simulated.
768 devices in a mesh: ctx: 384 (over z, y, x), head: 2 (over core).
Axes of the slice: x: 4, y: 8, z: 12, core: 2. Of those that a mesh axis runs over, the one named last changes fastest.
Arguments:
- queries: bfloat16 [98304, 4, 256], P('ctx', 'head'), may hold values from -6 to 6
- token_keys: bfloat16 [98304, 4, 256], P('ctx', 'head'), may hold values from -6 to 6
- token_values: bfloat16 [98304, 4, 256], P('ctx', 'head'), may hold values from -6 to 6
- step_rates: float32 [98304, 4], P('ctx', 'head'), may hold values from 0.1 to 1
- counts: int32 [384], replicated, may hold values from 64 to 256, as said below
- fast_weights: float32 [4, 3, 256, 256], P('head'), may hold values from -0.375 to 0.375
- out_weight: bfloat16 [1024, 4096], P('head'), may hold values from -0.1875 to 0.1875
Outputs:
- layer_output: bfloat16 [98304, 4096], P('ctx', 'head')
Inputs may be any that keep to these rules, and one draw needn't show every extreme that they name: counts[i] tokens at the start of block i are valid, the rest are padding; some block is full and some holds exactly 64.
All inputs are finite; a program needn't handle non-finite values.
Results may differ from a plain program's by a relative error of at most 0.012.
The roundings to bfloat16 on the way count: a program that leaves them out, or rounds other values in their place, can miss the bound.
Values may be sent and summed in bfloat16 or wider, within the bound.
No kernel may reach another device: no remote copies, remote signals or barrier semaphores. Data moves between devices by JAX's collectives and lax.ppermute only.
A program may use at most 32 MiB of HBM per device.

v0:
```python
import math

import jax
import jax.numpy as jnp
from jax import lax
from jax.sharding import PartitionSpec as P

SPAN = 2


def passed_along(value, axis, steps):
    count = lax.axis_size(axis)
    leading, last = (max(0, -steps), min(count, count - steps))
    return lax.ppermute(value, axis, [(source, source + steps) for source in range(leading, last)])


def split_up(x, dim, peers):
    before, after = (x.shape[:dim], x.shape[dim + 1 :])
    return jnp.moveaxis(x.reshape(*before, peers, -1, *after), dim, 0)


def sent_and_summed(x, axis, dim):
    peers = lax.axis_size(axis)
    blocks = lax.all_to_all(split_up(x, dim, peers), axis, 0, 0, tiled=True)
    return jnp.sum(blocks.astype(jnp.float32), axis=0)


def silu_slope(pre_value):
    sigmoid_value = jax.nn.sigmoid(pre_value)
    return sigmoid_value * (1.0 + pre_value * (1.0 - sigmoid_value))


def refresh(old_rows, gradient_rows, token_total):
    updated = old_rows - gradient_rows / math.sqrt(token_total)
    old_norm = jnp.sqrt(jnp.sum(old_rows * old_rows, axis=-1, keepdims=True))
    fresh = (
        updated * old_norm / jnp.sqrt(jnp.sum(updated * updated, axis=-1, keepdims=True) + 1e-06)
    )
    return fresh.astype(jnp.bfloat16)


def shards(queries, token_keys, token_values, step_rates, counts, fast_weights, out_weight):
    tok_rows, head_local, head_width = queries.shape
    device_count = lax.axis_size("ctx")
    device_place = lax.axis_index("ctx")
    positions = jnp.arange(tok_rows, dtype=jnp.int32)
    own_count = lax.dynamic_index_in_dim(counts, device_place, 0, keepdims=False)
    valid_rows = (positions < own_count).astype(jnp.float32)
    weights_low = fast_weights.astype(jnp.bfloat16)
    gate_pre = jnp.einsum(
        "thi,hci->thc", token_keys, weights_low[:, 0], preferred_element_type=jnp.float32
    )
    up_pre = jnp.einsum(
        "thi,hci->thc", token_keys, weights_low[:, 1], preferred_element_type=jnp.float32
    )
    gate_act = jax.nn.silu(gate_pre)
    hidden = (gate_act * up_pre).astype(jnp.bfloat16)
    scaled = (
        (step_rates * valid_rows[:, None])[:, :, None] * token_values.astype(jnp.float32)
    ).astype(jnp.bfloat16)
    grad_down = -jnp.einsum("thd,thc->hdc", scaled, hidden, preferred_element_type=jnp.float32)
    back_hidden = -jnp.einsum(
        "thd,hdc->thc", scaled, weights_low[:, 2], preferred_element_type=jnp.float32
    )
    grad_gate = (back_hidden * up_pre * silu_slope(gate_pre)).astype(jnp.bfloat16)
    grad_up = (back_hidden * gate_act).astype(jnp.bfloat16)
    first_grad = jnp.einsum(
        "thc,thi->hci", grad_gate, token_keys, preferred_element_type=jnp.float32
    )
    second_grad = jnp.einsum(
        "thc,thi->hci", grad_up, token_keys, preferred_element_type=jnp.float32
    )
    local_grad = jnp.stack([first_grad, second_grad, grad_down], axis=1).reshape(-1, head_width)
    old_flat = fast_weights.reshape(-1, head_width)
    token_total = tok_rows * device_count
    grad_whole = lax.psum(local_grad, "ctx")
    new_flat = refresh(old_flat, grad_whole, token_total)
    new_weights = new_flat.reshape(head_local, 3, head_width, head_width)
    query_gate = jnp.einsum(
        "thi,hci->thc", queries, new_weights[:, 0], preferred_element_type=jnp.float32
    )
    query_up = jnp.einsum(
        "thi,hci->thc", queries, new_weights[:, 1], preferred_element_type=jnp.float32
    )
    query_hidden = (jax.nn.silu(query_gate) * query_up).astype(jnp.bfloat16)
    ttt_out = jnp.einsum(
        "thc,hdc->thd", query_hidden, new_weights[:, 2], preferred_element_type=jnp.float32
    )
    key_parts = []
    value_parts = []
    valid_parts = []
    for back_step in range(SPAN, 0, -1):
        moved_keys, moved_values = passed_along((token_keys, token_values), "ctx", back_step)
        source = device_place - back_step
        source_count = lax.dynamic_index_in_dim(counts, jnp.maximum(source, 0), 0, keepdims=False)
        valid_parts.append(((positions < source_count) & (source >= 0)).astype(jnp.float32))
        key_parts.append(moved_keys)
        value_parts.append(moved_values)
    key_parts.append(token_keys)
    value_parts.append(token_values)
    valid_parts.append(valid_rows)
    seen_keys = jnp.concatenate(key_parts, 0)
    seen_values = jnp.concatenate(value_parts, 0)
    seen_valid = jnp.concatenate(valid_parts, 0)
    window_len = SPAN * tok_rows
    distance = (
        window_len
        + positions[:, None]
        - jnp.arange(window_len + tok_rows, dtype=jnp.int32)[None, :]
    )
    scores = jnp.einsum(
        "thi,shi->hts", queries, seen_keys, preferred_element_type=jnp.float32
    ) / math.sqrt(head_width)
    allowed = (distance >= 0) & (distance < window_len) & (seen_valid[None, :] > 0.5)
    scores = jnp.where(allowed[None], scores, -1e30)
    top_score = jnp.max(scores, axis=-1, keepdims=True)
    expo = jnp.exp(scores - top_score)
    attention = (expo / jnp.sum(expo, axis=-1, keepdims=True)).astype(jnp.bfloat16)
    window_out = jnp.einsum(
        "hts,shd->thd", attention, seen_values, preferred_element_type=jnp.float32
    )
    features = ((ttt_out + window_out) * valid_rows[:, None, None]).astype(jnp.bfloat16)
    features = features.reshape(tok_rows, head_local * head_width)
    partial_out = jnp.dot(features, out_weight, preferred_element_type=jnp.float32)
    return sent_and_summed(partial_out.astype(jnp.bfloat16), "head", 1).astype(jnp.bfloat16)


def solution(mesh):
    in_specs = (
        P("ctx", "head", None),
        P("ctx", "head", None),
        P("ctx", "head", None),
        P("ctx", "head"),
        P(),
        P("head", None, None, None),
        P("head", None),
    )
    out_specs = P("ctx", "head")
    return jax.shard_map(shards, mesh=mesh, in_specs=in_specs, out_specs=out_specs, check_vma=False)
```

profile of v0, /device:TPU:1, one launch (start us, length us, event | category | flops | bytes accessed | tf_op | source)
XLA Modules:
  0.0 442.5 jit_solution(5893268447782373406)
XLA Ops:
  6.6 1.5 convolution_bitcast_fusion.4
  8.1 2.2 convolution_bitcast_fusion.5
  10.3 0.7 fusion.60
  11.0 0.6 compare_convert_fusion
  11.8 0.3 multiply_convert_fusion.3
  12.2 0.2 copy.66
  12.4 0.3 fusion.5
  12.7 0.4 convolution_bitcast_fusion.2
  13.0 0.7 copy-done.6
  13.7 0.4 convolution_bitcast_fusion.3
  14.1 0.3 fusion.4
  14.5 0.2 pad_maximum_fusion
  14.7 1.3 copy.67
  16.0 6.2 %collective-permute-start.2 = (bf16[256,2,256]{2,0,1:T(8,128)(2,1)S(1)}, bf16[256,2,256]{2,0,1:T(8,128)(2,1)}, u32[]{:S(2)}, u32[]{:S(2)}) collective-permute-start(bf16[256,2,256]{2,0,1:T(8,128)(2,1)S(1)} %copy.58), channel_id=1, source_target_pairs={{0,4},{2,6},{4,8},{6,10},{8,12},{10,14},{12,16},{14,18},{16,20},{1... | collective-permute-start | bytes 786440 | tf_op jit(solution)/shard_map/ppermute | solution.py:14
  22.2 2.9 collective-permute-start.3
  25.3 3.3 collective-permute-start
  28.5 3.8 collective-permute-start.1
  32.4 1.3 and_convert_fusion
  33.6 0.3 multiply_reduce_fusion.1
  34.0 0.2 fusion.23
  34.2 2.8 fusion.61
  37.1 377.1 %all-reduce.2.cloned.1.call-done = f32[1536,256]{1,0:T(8,128)} async-done(((f32[1536,256]{1,0:T(8,128)}), f32[1536,256]{1,0:T(8,128)}) %all-reduce.2.cloned.1.call-update) | async-done | bytes 1572880 | tf_op jit(solution)/shard_map/psum | solution.py:76
  414.2 1.8 multiply_reduce_fusion
  416.0 0.5 divide_convert_fusion.1
  416.5 0.3 convolution_bitcast_fusion.1
  416.8 0.5 fusion.9
  417.3 2.0 fusion.7
  419.3 0.7 copy-done.3
  420.0 1.3 convolution_convert_fusion
  421.3 0.2 copy.128
  421.6 12.3 %all_to_all.5 = bf16[2,256,2048]{2,1,0:T(8,128)(2,1)S(1)} all-to-all(bf16[2,256,2048]{2,1,0:T(8,128)(2,1)S(1)} %bitcast.81), channel_id=1, replica_groups=mesh['ctx'=384,'head'=2] {'head'}, dimensions={0} | all-to-all | bytes 4194304 | tf_op jit(solution)/shard_map/all_to_all | solution.py:24
  433.9 1.7 reduce_sum.42
  (31 shorter events, 0.5 us)
Async XLA Ops:
  6.5 27.7 %copy-start = (bf16[256,2,256]{2,1,0:T(2,128)(2,1)S(1)}, bf16[256,2,256]{2,1,0:T(2,128)(2,1)}, u32[]{:S(2)}) copy-start(bf16[256,2,256]{2,1,0:T(2,128)(2,1)} %param.7) | copy-start | bytes 786436
  6.5 3.8 copy-start.8
  6.5 5.1 %copy-start.7 = (f32[256,2]{0,1:T(2,128)S(1)}, f32[256,2]{0,1:T(2,128)}, u32[]{:S(2)}) copy-start(f32[256,2]{0,1:T(2,128)} %param.10) | copy-start | bytes 6148
  6.5 5.3 %copy-start.5 = (bf16[256,2,256]{2,1,0:T(2,128)(2,1)S(1)}, bf16[256,2,256]{2,1,0:T(2,128)(2,1)}, u32[]{:S(2)}) copy-start(bf16[256,2,256]{2,1,0:T(2,128)(2,1)} %param.9) | copy-start | bytes 786436
  6.5 407.6 %all-reduce.2.cloned.1.call-start = ((), (), s32[]{:S(2)}) async-start(), calls=%async_computation.1 | async-start | bytes 3145728 | tf_op jit(solution)/shard_map/psum | solution.py:76
  6.6 5.8 %copy-start.1 = (f32[2,3,256,256]{3,2,1,0:T(8,128)S(1)}, f32[2,3,256,256]{3,2,1,0:T(8,128)}, u32[]{:S(2)}) copy-start(f32[2,3,256,256]{3,2,1,0:T(8,128)} %param.12) | copy-start | bytes 4718596
  8.1 4.5 %copy-start.4 = (bf16[256,2,256]{2,1,0:T(2,128)(2,1)S(1)}, bf16[256,2,256]{2,1,0:T(2,128)(2,1)}, u32[]{:S(2)}) copy-start(bf16[256,2,256]{2,1,0:T(2,128)(2,1)} %param.8) | copy-start | bytes 786436
  12.7 1.0 copy-start.6
  16.0 18.2 %collective-permute-start.2 = (bf16[256,2,256]{2,0,1:T(8,128)(2,1)S(1)}, bf16[256,2,256]{2,0,1:T(8,128)(2,1)}, u32[]{:S(2)}, u32[]{:S(2)}) collective-permute-start(bf16[256,2,256]{2,0,1:T(8,128)(2,1)S(1)} %copy.58), channel_id=1, source_target_pairs={{0,4},{2,6},{4,8},{6,10},{8,12},{10,14},{12,16},{14,18},{16,20},{1... | collective-permute-start | bytes 786440 | tf_op jit(solution)/shard_map/ppermute | solution.py:14
  22.2 12.1 %collective-permute-start.3 = (bf16[256,2,256]{2,0,1:T(8,128)(2,1)S(1)}, bf16[256,2,256]{2,0,1:T(8,128)(2,1)}, u32[]{:S(2)}, u32[]{:S(2)}) collective-permute-start(bf16[256,2,256]{2,0,1:T(8,128)(2,1)S(1)} %copy.58), channel_id=1, source_target_pairs={{0,2},{2,4},{4,6},{6,8},{8,10},{10,12},{12,14},{14,16},{16,18},{18... | collective-permute-start | bytes 786440 | tf_op jit(solution)/shard_map/ppermute | solution.py:14
  25.3 392.0 %collective-permute-start = (bf16[256,2,256]{0,2,1:T(8,128)(2,1)S(1)}, bf16[256,2,256]{0,2,1:T(8,128)(2,1)S(1)}, u32[]{:S(2)}, u32[]{:S(2)}) collective-permute-start(bf16[256,2,256]{0,2,1:T(8,128)(2,1)S(1)} %copy.75), channel_id=1, source_target_pairs={{0,4},{2,6},{4,8},{6,10},{8,12},{10,14},{12,16},{14,18},{16,20},{1... | collective-permute-start | bytes 786440 | tf_op jit(solution)/shard_map/ppermute | solution.py:14
  28.5 388.7 %collective-permute-start.1 = (bf16[256,2,256]{0,2,1:T(8,128)(2,1)S(1)}, bf16[256,2,256]{0,2,1:T(8,128)(2,1)}, u32[]{:S(2)}, u32[]{:S(2)}) collective-permute-start(bf16[256,2,256]{0,2,1:T(8,128)(2,1)S(1)} %copy.75), channel_id=1, source_target_pairs={{0,2},{2,4},{4,6},{6,8},{8,10},{10,12},{12,14},{14,16},{16,18},{18... | collective-permute-start | bytes 786440 | tf_op jit(solution)/shard_map/ppermute | solution.py:14
  414.2 1.9 copy-start.2
  417.3 2.7 copy-start.3
Sparse Core Ops, SparseCore 0:
  16.1 398.0 all-reduce.1
where the time goes:
time: 443 us; the launch traced here: 442 us
  waiting for transfers between devices  377 us (85%)
  starting transfers between devices  16.2 us (4%)
  between operations  13.7 us (3%)
  blocking collectives  12.3 us (3%)
  matrix products  12 us (3%)
  other arithmetic  6.95 us (2%)
    psum x1, waiting for transfers between devices, shards(): grad_whole = lax.psum(local_grad, 'ctx')  377 us
    ppermute x4, starting transfers between devices, passed_along(): lax.ppermute(value, axis, [(source, source + steps) for source in range(l...  16.2 us
    all_to_all x1, blocking collectives, sent_and_summed(): blocks = lax.all_to_all(split_up(x, dim, peers), axis, 0, 0, tiled=True)  12.3 us
  transfers between devices with their start and end apart: 5, of which 1 were waited for; matrix products, arithmetic and copies ran while one was open for 2% of the time, Pallas kernels for 0%

commit v1 on v0

v1 whole, which is shorter than its diff:
```python
import math

import jax
import jax.numpy as jnp
from jax import lax
from jax.experimental import pallas as pl
from jax.experimental.pallas import tpu as pltpu
from jax.sharding import Mesh, PartitionSpec as P


RING = 4
CTX = ("z", "p")
VMEM = pl.BlockSpec(memory_space=pltpu.VMEM)
SMEM = pl.BlockSpec(memory_space=pltpu.SMEM)
LOWEST = -1e30
VMEM_BYTES = 24 << 20


def passed_along(value, steps):
    count = lax.axis_size(CTX)
    return lax.ppermute(value, CTX, [(source, source + steps) for source in range(count - steps)])


def product(left, right, left_dim, right_dim):
    return lax.dot_general(
        left,
        right,
        (((left_dim,), (right_dim,)), ((), ())),
        preferred_element_type=jnp.float32,
    )


def gradient_kernel(count_ref, keys_ref, values_ref, rates_ref, weights_ref, grad_ref):
    tokens, heads, width = keys_ref.shape
    valid = lax.broadcasted_iota(jnp.int32, (tokens, 1), 0) < count_ref[0]
    for head in range(heads):
        keys = keys_ref[:, head, :]
        values = values_ref[:, head, :].astype(jnp.float32)
        rates = jnp.where(valid, rates_ref[:, head : head + 1], 0.0)
        scaled = (rates * values).astype(jnp.bfloat16)
        gate_weight = weights_ref[head, 0].astype(jnp.bfloat16)
        up_weight = weights_ref[head, 1].astype(jnp.bfloat16)
        down_weight = weights_ref[head, 2].astype(jnp.bfloat16)
        gate_pre = product(keys, gate_weight, 1, 1)
        up_pre = product(keys, up_weight, 1, 1)
        back = -product(scaled, down_weight, 1, 0)
        sigmoid = jax.nn.sigmoid(gate_pre)
        gate_act = gate_pre * sigmoid
        hidden = (gate_act * up_pre).astype(jnp.bfloat16)
        slope = sigmoid * (1.0 + gate_pre * (1.0 - sigmoid))
        grad_gate = (back * up_pre * slope).astype(jnp.bfloat16)
        grad_up = (back * gate_act).astype(jnp.bfloat16)
        first = head * 3 * width
        grad_ref[first : first + width, :] = product(grad_gate, keys, 0, 0).astype(jnp.bfloat16)
        grad_ref[first + width : first + 2 * width, :] = product(grad_up, keys, 0, 0).astype(
            jnp.bfloat16
        )
        grad_ref[first + 2 * width : first + 3 * width, :] = (
            -product(scaled, hidden, 0, 0)
        ).astype(jnp.bfloat16)


def local_gradient(own_count, token_keys, token_values, step_rates, fast_weights):
    heads, mats, width, _ = fast_weights.shape
    return pl.pallas_call(
        gradient_kernel,
        out_shape=jax.ShapeDtypeStruct((heads * mats * width, width), jnp.bfloat16),
        in_specs=[SMEM, VMEM, VMEM, VMEM, VMEM],
        out_specs=VMEM,
        name="gradient",
        compiler_params=pltpu.CompilerParams(vmem_limit_bytes=VMEM_BYTES),
        cost_estimate=pl.CostEstimate(
            flops=14 * 256 * width * width * heads, transcendentals=131072, bytes_accessed=3000000
        ),
    )(own_count, token_keys, token_values, step_rates, fast_weights)


def near_kernel(counts_ref, queries_ref, own_keys_ref, own_values_ref, near_ref, sum_ref, top_ref, mass_ref):
    tokens, heads, width = queries_ref.shape
    row = lax.broadcasted_iota(jnp.int32, (tokens, tokens), 0)
    column = lax.broadcasted_iota(jnp.int32, (tokens, tokens), 1)
    own_allowed = (column <= row) & (column < counts_ref[0])
    near_allowed = column < counts_ref[1]
    scale = 1.0 / math.sqrt(width)
    for head in range(heads):
        queries = queries_ref[:, head, :]
        own = product(queries, own_keys_ref[:, head, :], 1, 1) * scale
        near = product(queries, near_ref[0, :, head, :], 1, 1) * scale
        own = jnp.where(own_allowed, own, LOWEST)
        near = jnp.where(near_allowed, near, LOWEST)
        top = jnp.max(jnp.maximum(own, near), axis=1, keepdims=True)
        own, near = jnp.exp(own - top), jnp.exp(near - top)
        mass = jnp.sum(own + near, axis=1, keepdims=True)
        sum_ref[:, head * width : (head + 1) * width] = product(
            own.astype(jnp.bfloat16), own_values_ref[:, head, :], 1, 0
        ) + product(near.astype(jnp.bfloat16), near_ref[1, :, head, :], 1, 0)
        top_ref[head] = jnp.broadcast_to(top, top_ref.shape[1:])
        mass_ref[head] = jnp.broadcast_to(mass, mass_ref.shape[1:])


def near_attention(seen_counts, queries, token_keys, token_values, near):
    tokens, heads, width = queries.shape
    side = jax.ShapeDtypeStruct((heads, tokens, 128), jnp.float32)
    return pl.pallas_call(
        near_kernel,
        out_shape=(jax.ShapeDtypeStruct((tokens, heads * width), jnp.float32), side, side),
        in_specs=[SMEM, VMEM, VMEM, VMEM, VMEM],
        out_specs=(VMEM, VMEM, VMEM),
        name="near_attention",
        compiler_params=pltpu.CompilerParams(vmem_limit_bytes=VMEM_BYTES),
        cost_estimate=pl.CostEstimate(
            flops=8 * tokens * tokens * width * heads, transcendentals=262144, bytes_accessed=3000000
        ),
    )(seen_counts, queries, token_keys, token_values, near)


def feature_kernel(
    counts_ref, queries_ref, far_ref, sum_ref, top_ref, mass_ref, weights_ref, features_ref
):
    tokens, heads, width = queries_ref.shape
    row = lax.broadcasted_iota(jnp.int32, (tokens, tokens), 0)
    column = lax.broadcasted_iota(jnp.int32, (tokens, tokens), 1)
    far_allowed = (column > row) & (column < counts_ref[2])
    valid = lax.broadcasted_iota(jnp.int32, (tokens, 1), 0) < counts_ref[0]
    scale = 1.0 / math.sqrt(width)
    for head in range(heads):
        queries = queries_ref[:, head, :]
        far = product(queries, far_ref[0, :, head, :], 1, 1) * scale
        far = jnp.where(far_allowed, far, LOWEST)
        near_top = top_ref[head][:, :1]
        top = jnp.maximum(near_top, jnp.max(far, axis=1, keepdims=True))
        far = jnp.exp(far - top)
        kept = jnp.exp(near_top - top)
        mass = kept * mass_ref[head][:, :1] + jnp.sum(far, axis=1, keepdims=True)
        near_sum = sum_ref[:, head * width : (head + 1) * width]
        total = kept * near_sum + product(far.astype(jnp.bfloat16), far_ref[1, :, head, :], 1, 0)
        window = total / mass
        first = head * 3 * width
        gate = product(queries, weights_ref[first : first + width, :], 1, 1)
        up = product(queries, weights_ref[first + width : first + 2 * width, :], 1, 1)
        hidden = (gate * jax.nn.sigmoid(gate) * up).astype(jnp.bfloat16)
        learned = product(hidden, weights_ref[first + 2 * width : first + 3 * width, :], 1, 1)
        features_ref[:, head * width : (head + 1) * width] = jnp.where(
            valid, learned + window, 0.0
        ).astype(jnp.bfloat16)


def features_of(seen_counts, queries, far, near_sum, near_top, near_mass, new_flat):
    tokens, heads, width = queries.shape
    return pl.pallas_call(
        feature_kernel,
        out_shape=jax.ShapeDtypeStruct((tokens, heads * width), jnp.bfloat16),
        in_specs=[SMEM] + [VMEM] * 6,
        out_specs=VMEM,
        name="features",
        compiler_params=pltpu.CompilerParams(vmem_limit_bytes=VMEM_BYTES),
        cost_estimate=pl.CostEstimate(
            flops=10 * tokens * tokens * width * heads, transcendentals=262144, bytes_accessed=3000000
        ),
    )(seen_counts, queries, far, near_sum, near_top, near_mass, new_flat)


def project_kernel(place_ref, own_ref, other_ref, own_weight_ref, other_weight_ref, out_ref):
    out_ref[...] = (
        jnp.dot(own_ref[...], own_weight_ref[...], preferred_element_type=jnp.float32)
        + jnp.dot(other_ref[...], other_weight_ref[...], preferred_element_type=jnp.float32)
    ).astype(jnp.bfloat16)


def projected(head_place, own, other, own_weight, other_weight):
    tokens, depth = own.shape
    columns = other_weight.shape[1]
    tile = 512
    tiles = columns // tile
    return pl.pallas_call(
        project_kernel,
        out_shape=jax.ShapeDtypeStruct((tokens, columns), jnp.bfloat16),
        grid_spec=pltpu.PrefetchScalarGridSpec(
            num_scalar_prefetch=1,
            grid=(tiles,),
            in_specs=[
                pl.BlockSpec((tokens, depth), lambda step, place: (0, 0)),
                pl.BlockSpec((tokens, depth), lambda step, place: (0, 0)),
                pl.BlockSpec((depth, tile), lambda step, place: (0, place[0] * tiles + step)),
                pl.BlockSpec((depth, tile), lambda step, place: (0, step)),
            ],
            out_specs=pl.BlockSpec((tokens, tile), lambda step, place: (0, step)),
        ),
        name="project",
        cost_estimate=pl.CostEstimate(
            flops=4 * tokens * depth * columns, transcendentals=0, bytes_accessed=6000000
        ),
    )(head_place, own, other, own_weight, other_weight)


def refresh(old_rows, gradient_rows, token_total):
    updated = old_rows - gradient_rows / math.sqrt(token_total)
    old_norm = jnp.sqrt(jnp.sum(old_rows * old_rows, axis=-1, keepdims=True))
    fresh = (
        updated * old_norm / jnp.sqrt(jnp.sum(updated * updated, axis=-1, keepdims=True) + 1e-06)
    )
    return fresh.astype(jnp.bfloat16)


def shards(queries, token_keys, token_values, step_rates, counts, fast_weights, out_weight):
    tok_rows, _, head_width = queries.shape
    device_count, plane_count = lax.axis_size(CTX), lax.axis_size("p")
    device_place, head_place = lax.axis_index(CTX), lax.axis_index("head")
    places = device_place - jnp.arange(3, dtype=jnp.int32)
    seen_counts = jnp.where(places >= 0, counts[jnp.maximum(places, 0)], 0)
    pairs = jnp.stack([token_keys, token_values], 0)
    near = passed_along(pairs, 1)
    local_grad = local_gradient(
        seen_counts, token_keys, token_values, step_rates, fast_weights
    )
    blocks = lax.all_to_all(local_grad.reshape(device_count, -1, head_width), CTX, 0, 0, tiled=True)
    out_parts = out_weight.reshape(out_weight.shape[0], 2, -1)
    out_other = lax.ppermute(
        lax.dynamic_index_in_dim(out_parts, 1 - head_place, 1, keepdims=False),
        "head",
        [(0, 1), (1, 0)],
    )
    near_sum, near_top, near_mass = near_attention(
        seen_counts, queries, token_keys, token_values, near
    )
    grad_rows = jnp.sum(blocks.astype(jnp.float32), axis=0)
    own_rows = grad_rows.shape[0]
    old_rows = lax.dynamic_slice_in_dim(
        fast_weights.reshape(-1, head_width), device_place * own_rows, own_rows, 0
    )
    new_rows = refresh(old_rows, grad_rows, tok_rows * device_count)
    held = lax.all_to_all(
        jnp.broadcast_to(new_rows[None], (plane_count, *new_rows.shape)), "p", 0, 0, tiled=True
    )
    held = held.reshape(-1, head_width)
    pairs, held = lax.optimization_barrier((pairs, held))
    far = passed_along(pairs, 2)
    new_flat = lax.all_gather(held, "z", axis=0, tiled=True)
    features = features_of(
        seen_counts, queries, far, near_sum, near_top, near_mass, new_flat
    )
    other = lax.ppermute(features, "head", [(0, 1), (1, 0)])
    return projected(head_place.reshape(1), features, other, out_weight, out_other)


def solution(mesh):
    fine = Mesh(mesh.devices.reshape(RING, -1, 2), ("z", "p", "head"))
    in_specs = (
        P(CTX, "head", None),
        P(CTX, "head", None),
        P(CTX, "head", None),
        P(CTX, "head"),
        P(),
        P("head", None, None, None),
        P("head", None),
    )
    return jax.shard_map(
        shards, mesh=fine, in_specs=in_specs, out_specs=P(CTX, "head"), check_vma=False
    )
```

time: 443 us -> 153 us (0.35)
  the two profiles are of different devices: /device:TPU:1 before, /device:TPU:127 now
where the time goes in v1:
time: 153 us; the launch traced here: 152 us
  starting transfers between devices  67.7 us (44%)
  local copies, waits for them, and re-layouts  29.2 us (19%)
  blocking collectives  21.7 us (14%)
  waiting for transfers between devices  16.7 us (11%)
  Pallas kernels  14.2 us (9%)
  other arithmetic  2.82 us (2%)
    all_to_all x1, starting transfers between devices, shards(): lax.all_to_all(local_grad.reshape(device_count, -1, head_width), CTX, 0,...  25.7 us
    all_gather x1, blocking collectives, shards(): new_flat = lax.all_gather(held, 'z', axis=0, tiled=True)  21.7 us
    ppermute x1, starting transfers between devices, shards(): other = lax.ppermute(features, 'head', [(0, 1), (1, 0)])  18.8 us
    unnamed x20, local copies, waits for them, and re-layouts  10.3 us
    all_to_all x1, starting transfers between devices, shards(): lax.all_to_all(jnp.broadcast_to(new_rows[None], (plane_count, *new_rows.s...  9.98 us
    ppermute x2, starting transfers between devices, passed_along(): lax.ppermute(value, CTX, [(source, source + steps) for source in range(co...  9.91 us
    dynamic_slice x1, local copies, waits for them, and re-layouts, shards(): lax.dynamic_index_in_dim(out_parts, 1 - head_place, 1, keepdims=False)  8.45 us
    reshape x1, local copies, waits for them, and re-layouts, shards(): out_parts = out_weight.reshape(out_weight.shape[0], 2, -1)  7.87 us
  transfers between devices with their start and end apart: 6, of which 4 were waited for; matrix products, arithmetic and copies ran while one was open for 16% of the time, Pallas kernels for 5%

profile of v1, /device:TPU:127, one launch (start us, length us, event | category | flops | bytes accessed | tf_op | source)
XLA Modules:
  0.0 152.4 jit_solution(6343349495769123271)
XLA Ops:
  0.0 0.7 copy-done
  0.7 0.6 gather_fusion
  1.3 0.8 copy.10.rates_ref
  2.2 0.9 copy-done.1
  3.1 0.9 copy-done.3
  4.1 1.4 copy-done.5
  5.5 2.4 %gradient.1 = bf16[1536,256]{1,0:T(8,128)(2,1)S(1)} custom-call(s32[3]{0:T(128)S(1)} %compare_select_fusion.count_ref.counts_ref, bf16[256,2,256]{2,1,0:T(2,128)(2,1)S(1)} %copy-done.3, bf16[256,2,256]{2,1,0:T(2,128)(2,1)S(1)} %copy-done.1, f32[256,2]{1,0:T(8,128)S(1)} %copy.10.rates_ref, f32[2,3,256,256]{3,2,1,0:T(8,128)S(1)} %copy-done.5), custom_call_target="tpu_custom_call" | custom-call | flops 469762048 | bytes 3000000 | tf_op jit(solution)/shard_map/gradient/pallas_call | solution.py:65
  7.8 1.1 reshape.38
  8.9 25.7 %all-to-all-start = ((bf16[384,4,256]{2,1,0:T(4,128)(2,1)}), bf16[384,4,256]{2,1,0:T(4,128)(2,1)S(1)}, u32[]{:S(2)}, u32[]{:S(2)}) async-start(bf16[384,4,256]{2,1,0:T(4,128)(2,1)} %reshape.38), calls=%async_computation | async-start | bytes 1572864 | tf_op jit(solution)/shard_map/all_to_all | solution.py:216
  34.6 7.9 %reshape.40 = bf16[512,2,2048]{2,1,0:T(2,128)(2,1)} reshape(bf16[512,4096]{1,0:T(8,128)(2,1)} %own_weight_ref.1) | data formatting | bytes 8388608 | tf_op jit(solution)/shard_map/reshape | solution.py:217
  42.5 8.5 %constant_dynamic-slice_fusion = bf16[512,1,2048]{2,1,0:T(2,128)(2,1)} fusion(bf16[512,2,2048]{2,1,0:T(2,128)(2,1)} %reshape.40, s32[]{:T(128)S(6)} %select_n.14), kind=kLoop, calls=%fused_computation.13 | loop fusion | bytes 4194308 | tf_op jit(solution)/shard_map/jit(dynamic_index_in_dim)/dynamic_slice | solution.py:219
  50.9 4.8 %copy.14 = bf16[512,1,2048]{2,0,1:T(8,128)(2,1)} copy(bf16[512,1,2048]{2,1,0:T(2,128)(2,1)} %constant_dynamic-slice_fusion) | data formatting | bytes 4194304
  55.8 3.3 %collective-permute-start.3 = (bf16[512,2048]{1,0:T(8,128)(2,1)}, bf16[512,2048]{1,0:T(8,128)(2,1)}, u32[]{:S(2)}, u32[]{:S(2)}) collective-permute-start(bf16[512,2048]{1,0:T(8,128)(2,1)} %bitcast.8), channel_id=1, source_target_pairs={{0,1},{1,0},{2,3},{3,2},{4,5},{5,4},{6,7},{7,6},{8,9},{9,8},{10,11... | collective-permute-start | bytes 6291464 | tf_op jit(solution)/shard_map/ppermute | solution.py:218
  59.1 7.2 %all-to-all-done = bf16[384,4,256]{2,1,0:T(4,128)(2,1)S(1)} async-done(((bf16[384,4,256]{2,1,0:T(4,128)(2,1)}), bf16[384,4,256]{2,1,0:T(4,128)(2,1)S(1)}, u32[]{:S(2)}, u32[]{:S(2)}) %all-to-all-start) | async-done | bytes 786464 | tf_op jit(solution)/shard_map/all_to_all | solution.py:216
  66.2 0.4 convert_reduce_fusion
  66.7 0.8 multiply_reduce_fusion.1
  67.5 0.8 fusion
  68.3 0.7 broadcast_in_dim.4
  69.0 10.0 %all-to-all-start.1 = ((bf16[96,4,256]{2,1,0:T(4,128)(2,1)}), bf16[96,4,256]{2,1,0:T(4,128)(2,1)S(1)}, u32[]{:S(2)}, u32[]{:S(2)}) async-start(bf16[96,4,256]{2,1,0:T(4,128)(2,1)} %broadcast_in_dim.4), calls=%async_computation.1 | async-start | bytes 393216 | tf_op jit(solution)/shard_map/all_to_all | solution.py:232
  79.1 0.7 pad_maximum_fusion
  79.8 3.1 %collective-permute-start.1 = (bf16[2,256,2,256]{3,2,1,0:T(2,128)(2,1)S(1)}, bf16[2,256,2,256]{3,2,1,0:T(2,128)(2,1)S(1)}, u32[]{:S(2)}, u32[]{:S(2)}) collective-permute-start(bf16[2,256,2,256]{3,2,1,0:T(2,128)(2,1)S(1)} %pad_maximum_fusion), channel_id=1, source_target_pairs={{0,2},{2,4},{4,6},{6,8},{8,10},{10,12},{12,14},{14,16},{16,18},{18... | collective-permute-start | bytes 1572872 | tf_op jit(solution)/shard_map/ppermute | solution.py:21
  82.9 2.3 %all-to-all-done.1 = bf16[96,4,256]{2,1,0:T(4,128)(2,1)S(1)} async-done(((bf16[96,4,256]{2,1,0:T(4,128)(2,1)}), bf16[96,4,256]{2,1,0:T(4,128)(2,1)S(1)}, u32[]{:S(2)}, u32[]{:S(2)}) %all-to-all-start.1) | async-done | bytes 196640 | tf_op jit(solution)/shard_map/all_to_all | solution.py:232
  85.2 0.1 reshape.39
  85.2 6.8 %collective-permute-start = (bf16[2,256,2,256]{3,2,1,0:T(2,128)(2,1)S(1)}, bf16[2,256,2,256]{3,2,1,0:T(2,128)(2,1)S(1)}, u32[]{:S(2)}, u32[]{:S(2)}) collective-permute-start(bf16[2,256,2,256]{3,2,1,0:T(2,128)(2,1)S(1)} %pad_maximum_fusion), channel_id=1, source_target_pairs={{0,4},{2,6},{4,8},{6,10},{8,12},{10,14},{12,16},{14,18},{16,20},{1... | collective-permute-start | bytes 1572872 | tf_op jit(solution)/shard_map/ppermute | solution.py:21
  92.1 6.1 %collective-permute-done.1.near_ref = bf16[2,256,2,256]{3,2,1,0:T(2,128)(2,1)S(1)} collective-permute-done((bf16[2,256,2,256]{3,2,1,0:T(2,128)(2,1)S(1)}, bf16[2,256,2,256]{3,2,1,0:T(2,128)(2,1)S(1)}, u32[]{:S(2)}, u32[]{:S(2)}) %collective-permute-start.1) | collective-permute-done | bytes 524320 | tf_op jit(solution)/shard_map/ppermute | solution.py:21
  98.2 3.8 %near_attention.1 = (f32[256,512]{1,0:T(8,128)S(1)}, f32[2,256,128]{2,1,0:T(8,128)S(1)}, f32[2,256,128]{2,1,0:T(8,128)S(1)}) custom-call(s32[3]{0:T(128)S(1)} %compare_select_fusion.count_ref.counts_ref, bf16[256,2,256]{2,1,0:T(2,128)(2,1)S(1)} %copy-done.6, bf16[256,2,256]{2,1,0:T(2,128)(2,1)S(1)} %copy-done.4, bf16[256,2,256]{2,1,0:T(2,128)(2,1)S(1)} %copy-done.2, ...), custom_call_target="tpu_custom_call" | custom-call | flops 268435456 | bytes 3000000 | tf_op jit(solution)/shard_map/near_attention/pallas_call | solution.py:104
  102.0 21.7 %all_gather.3.weights_ref = bf16[1536,256]{1,0:T(8,128)(2,1)S(1)} all-gather(bf16[384,256]{1,0:T(8,128)(2,1)S(1)} %reshape.39), channel_id=1, replica_groups=mesh['z'=4,'p'=96,'head'=2] {'z'}, dimensions={0}, use_global_device_ids=true | all-gather | bytes 983040 | tf_op jit(solution)/shard_map/all_gather | solution.py:238
  123.7 3.0 %features.1.own_ref = bf16[256,512]{1,0:T(8,128)(2,1)S(1)} custom-call(s32[3]{0:T(128)S(1)} %compare_select_fusion.count_ref.counts_ref, bf16[256,2,256]{2,1,0:T(2,128)(2,1)S(1)} %copy-done.6, bf16[2,256,2,256]{3,2,1,0:T(2,128)(2,1)S(1)} %collective-permute-done.far_ref, f32[256,512]{1,0:T(8,128)S(1)} %get-tuple-element.11.sum_ref, ...), custom_call_target="tpu_custom_call" | custom-call | flops 335544320 | bytes 3000000 | tf_op jit(solution)/shard_map/features/pallas_call | solution.py:150
  126.8 18.8 %collective-permute-start.2 = (bf16[256,512]{1,0:T(8,128)(2,1)S(1)}, bf16[256,512]{1,0:T(8,128)(2,1)S(1)}, u32[]{:S(2)}, u32[]{:S(2)}) collective-permute-start(bf16[256,512]{1,0:T(8,128)(2,1)S(1)} %features.1.own_ref), channel_id=1, source_target_pairs={{0,1},{1,0},{2,3},{3,2},{4,5},{5,4},{6,7},{7,6},{8,9},{9,8},{10,11... | collective-permute-start | bytes 786440 | tf_op jit(solution)/shard_map/ppermute | solution.py:242
  145.6 1.1 collective-permute-done.2.other_ref
  146.7 0.7 copy-done.8
  147.4 4.9 %project.1 = bf16[256,2048]{1,0:T(8,128)(2,1)} custom-call(s32[1]{0:T(128)} %bitcast.place_ref, bf16[256,512]{1,0:T(8,128)(2,1)} %copy-done.7, bf16[256,512]{1,0:T(8,128)(2,1)} %copy-done.8, bf16[512,4096]{1,0:T(8,128)(2,1)} %own_weight_ref.1, bf16[512,2048]{1,0:T(8,128)(2,1)} %collective-permute-done.3.other_weight_ref), custom_call_target="tpu_custom_call" | custom-call | flops 1073741824 | bytes 6000000 | tf_op jit(solution)/shard_map/project/pallas_call | solution.py:175
  (20 shorter events, 0.1 us)
Async XLA Ops:
  0.0 0.7 copy-start
  2.1 1.0 copy-start.1
  3.1 0.9 copy-start.3
  4.1 1.4 copy-start.5
  8.9 57.3 %all-to-all-start = ((bf16[384,4,256]{2,1,0:T(4,128)(2,1)}), bf16[384,4,256]{2,1,0:T(4,128)(2,1)S(1)}, u32[]{:S(2)}, u32[]{:S(2)}) async-start(bf16[384,4,256]{2,1,0:T(4,128)(2,1)} %reshape.38), calls=%async_computation | async-start | bytes 1572864 | tf_op jit(solution)/shard_map/all_to_all | solution.py:216
  50.9 28.1 %copy-start.2 = (bf16[256,2,256]{2,1,0:T(2,128)(2,1)S(1)}, bf16[256,2,256]{2,1,0:T(2,128)(2,1)}, u32[]{:S(2)}) copy-start(bf16[256,2,256]{2,1,0:T(2,128)(2,1)} %own_values_ref.1) | copy-start | bytes 786436
  50.9 28.1 %copy-start.4 = (bf16[256,2,256]{2,1,0:T(2,128)(2,1)S(1)}, bf16[256,2,256]{2,1,0:T(2,128)(2,1)}, u32[]{:S(2)}) copy-start(bf16[256,2,256]{2,1,0:T(2,128)(2,1)} %own_keys_ref.1) | copy-start | bytes 786436
  55.8 42.4 %copy-start.6 = (bf16[256,2,256]{2,1,0:T(2,128)(2,1)S(1)}, bf16[256,2,256]{2,1,0:T(2,128)(2,1)}, u32[]{:S(2)}) copy-start(bf16[256,2,256]{2,1,0:T(2,128)(2,1)} %queries_ref.3) | copy-start | bytes 786436
  55.8 89.8 %collective-permute-start.3 = (bf16[512,2048]{1,0:T(8,128)(2,1)}, bf16[512,2048]{1,0:T(8,128)(2,1)}, u32[]{:S(2)}, u32[]{:S(2)}) collective-permute-start(bf16[512,2048]{1,0:T(8,128)(2,1)} %bitcast.8), channel_id=1, source_target_pairs={{0,1},{1,0},{2,3},{3,2},{4,5},{5,4},{6,7},{7,6},{8,9},{9,8},{10,11... | collective-permute-start | bytes 6291464 | tf_op jit(solution)/shard_map/ppermute | solution.py:218
  69.0 16.1 %all-to-all-start.1 = ((bf16[96,4,256]{2,1,0:T(4,128)(2,1)}), bf16[96,4,256]{2,1,0:T(4,128)(2,1)S(1)}, u32[]{:S(2)}, u32[]{:S(2)}) async-start(bf16[96,4,256]{2,1,0:T(4,128)(2,1)} %broadcast_in_dim.4), calls=%async_computation.1 | async-start | bytes 393216 | tf_op jit(solution)/shard_map/all_to_all | solution.py:232
  79.8 18.4 %collective-permute-start.1 = (bf16[2,256,2,256]{3,2,1,0:T(2,128)(2,1)S(1)}, bf16[2,256,2,256]{3,2,1,0:T(2,128)(2,1)S(1)}, u32[]{:S(2)}, u32[]{:S(2)}) collective-permute-start(bf16[2,256,2,256]{3,2,1,0:T(2,128)(2,1)S(1)} %pad_maximum_fusion), channel_id=1, source_target_pairs={{0,2},{2,4},{4,6},{6,8},{8,10},{10,12},{12,14},{14,16},{16,18},{18... | collective-permute-start | bytes 1572872 | tf_op jit(solution)/shard_map/ppermute | solution.py:21
  85.2 38.5 %collective-permute-start = (bf16[2,256,2,256]{3,2,1,0:T(2,128)(2,1)S(1)}, bf16[2,256,2,256]{3,2,1,0:T(2,128)(2,1)S(1)}, u32[]{:S(2)}, u32[]{:S(2)}) collective-permute-start(bf16[2,256,2,256]{3,2,1,0:T(2,128)(2,1)S(1)} %pad_maximum_fusion), channel_id=1, source_target_pairs={{0,4},{2,6},{4,8},{6,10},{8,12},{10,14},{12,16},{14,18},{16,20},{1... | collective-permute-start | bytes 1572872 | tf_op jit(solution)/shard_map/ppermute | solution.py:21
  126.8 20.0 %copy-start.7 = (bf16[256,512]{1,0:T(8,128)(2,1)}, bf16[256,512]{1,0:T(8,128)(2,1)S(1)}, u32[]{:S(2)}) copy-start(bf16[256,512]{1,0:T(8,128)(2,1)S(1)} %features.1.own_ref) | copy-start | bytes 786436
  126.8 20.0 %collective-permute-start.2 = (bf16[256,512]{1,0:T(8,128)(2,1)S(1)}, bf16[256,512]{1,0:T(8,128)(2,1)S(1)}, u32[]{:S(2)}, u32[]{:S(2)}) collective-permute-start(bf16[256,512]{1,0:T(8,128)(2,1)S(1)} %features.1.own_ref), channel_id=1, source_target_pairs={{0,1},{1,0},{2,3},{3,2},{4,5},{5,4},{6,7},{7,6},{8,9},{9,8},{10,11... | collective-permute-start | bytes 786440 | tf_op jit(solution)/shard_map/ppermute | solution.py:242
  146.7 0.7 copy-start.8

commit v2 on v1

v2 whole, which is shorter than its diff:
```python
import functools
import math

import jax
import jax.numpy as jnp
from jax import lax
from jax.experimental import pallas as pl
from jax.experimental.pallas import tpu as pltpu
from jax.sharding import Mesh, PartitionSpec as P


RING = 4
CTX = ("z", "p")
VMEM = pl.BlockSpec(memory_space=pltpu.VMEM)
SMEM = pl.BlockSpec(memory_space=pltpu.SMEM)
LOWEST = -1e30
VMEM_BYTES = 24 << 20


def passed_along(value, steps):
    count = lax.axis_size(CTX)
    return lax.ppermute(value, CTX, [(source, source + steps) for source in range(count - steps)])


def product(left, right, left_dim, right_dim):
    return lax.dot_general(
        left,
        right,
        (((left_dim,), (right_dim,)), ((), ())),
        preferred_element_type=jnp.float32,
    )


def place_count(counts_ref, place_ref, back_step):
    place = place_ref[0] - back_step
    return jnp.where(place >= 0, counts_ref[jnp.maximum(place, 0)], 0)


def chunked(rows):
    blocks = rows.shape[0] // 8
    left = rows[:, :128].reshape(blocks, 8, 128)
    right = rows[:, 128:].reshape(blocks, 8, 128)
    ahead = lax.broadcasted_iota(jnp.int32, (blocks, 8, 128), 1) < 4
    even = jnp.where(ahead, left, pltpu.roll(right, 4, 1))
    odd = jnp.where(ahead, pltpu.roll(left, 4, 1), right)
    return even.astype(jnp.bfloat16), odd.astype(jnp.bfloat16)


def gradient_kernel(place_ref, counts_ref, keys_ref, values_ref, rates_ref, weights_ref, grad_ref):
    tokens, heads, width = keys_ref.shape
    valid = lax.broadcasted_iota(jnp.int32, (tokens, 1), 0) < place_count(counts_ref, place_ref, 0)
    rates_all = jnp.concatenate(
        [rates_ref[...], jnp.zeros((8 - heads, tokens), jnp.float32)], 0
    ).T
    for head in range(heads):
        keys = keys_ref[:, head, :]
        values = values_ref[:, head, :].astype(jnp.float32)
        rates = jnp.where(valid, rates_all[:, head : head + 1], 0.0)
        scaled = (rates * values).astype(jnp.bfloat16)
        gate_weight = weights_ref[head, 0].astype(jnp.bfloat16)
        up_weight = weights_ref[head, 1].astype(jnp.bfloat16)
        down_weight = weights_ref[head, 2].astype(jnp.bfloat16)
        gate_pre = product(keys, gate_weight, 1, 1)
        up_pre = product(keys, up_weight, 1, 1)
        back = -product(scaled, down_weight, 1, 0)
        sigmoid = jax.nn.sigmoid(gate_pre)
        gate_act = gate_pre * sigmoid
        hidden = (gate_act * up_pre).astype(jnp.bfloat16)
        slope = sigmoid * (1.0 + gate_pre * (1.0 - sigmoid))
        grad_gate = (back * up_pre * slope).astype(jnp.bfloat16)
        grad_up = (back * gate_act).astype(jnp.bfloat16)
        mats = (
            product(grad_gate, keys, 0, 0),
            product(grad_up, keys, 0, 0),
            -product(scaled, hidden, 0, 0),
        )
        blocks = width // 8
        for index, mat in enumerate(mats):
            first = (head * 3 + index) * blocks
            even, odd = chunked(mat)
            grad_ref[first : first + blocks, 0] = even
            grad_ref[first : first + blocks, 1] = odd


def local_gradient(place, counts, token_keys, token_values, step_rates, fast_weights):
    heads, mats, width, _ = fast_weights.shape
    return pl.pallas_call(
        gradient_kernel,
        out_shape=jax.ShapeDtypeStruct((heads * mats * width // 8, 2, 8, 128), jnp.bfloat16),
        in_specs=[SMEM, SMEM, VMEM, VMEM, VMEM, VMEM],
        out_specs=VMEM,
        name="gradient",
        cost_estimate=pl.CostEstimate(
            flops=14 * 256 * width * width * heads, transcendentals=131072, bytes_accessed=3000000
        ),
    )(place, counts, token_keys, token_values, step_rates.T, fast_weights)


def own_kernel(
    place_ref, counts_ref, queries_ref, keys_ref, values_ref, pairs_ref, sum_ref, top_ref, mass_ref
):
    tokens, heads, width = queries_ref.shape
    row = lax.broadcasted_iota(jnp.int32, (tokens, tokens), 0)
    column = lax.broadcasted_iota(jnp.int32, (tokens, tokens), 1)
    allowed = (column <= row) & (column < place_count(counts_ref, place_ref, 0))
    scale = 1.0 / math.sqrt(width)
    for head in range(heads):
        keys, values = keys_ref[:, head, :], values_ref[:, head, :]
        pairs_ref[head] = keys
        pairs_ref[heads + head] = values
        own = product(queries_ref[:, head, :], keys, 1, 1) * scale
        own = jnp.where(allowed, own, LOWEST)
        top = jnp.max(own, axis=1, keepdims=True)
        own = jnp.exp(own - top)
        mass = jnp.sum(own, axis=1, keepdims=True)
        sum_ref[:, head * width : (head + 1) * width] = product(
            own.astype(jnp.bfloat16), values, 1, 0
        )
        top_ref[head] = jnp.broadcast_to(top, top_ref.shape[1:])
        mass_ref[head] = jnp.broadcast_to(mass, mass_ref.shape[1:])


def own_attention(place, counts, queries, token_keys, token_values):
    tokens, heads, width = queries.shape
    side = jax.ShapeDtypeStruct((heads, tokens, 128), jnp.float32)
    return pl.pallas_call(
        own_kernel,
        out_shape=(
            jax.ShapeDtypeStruct((2 * heads, tokens, width), jnp.bfloat16),
            jax.ShapeDtypeStruct((tokens, heads * width), jnp.float32),
            side,
            side,
        ),
        in_specs=[SMEM, SMEM, VMEM, VMEM, VMEM],
        out_specs=(VMEM, VMEM, VMEM, VMEM),
        name="own_attention",
        compiler_params=pltpu.CompilerParams(vmem_limit_bytes=VMEM_BYTES),
        cost_estimate=pl.CostEstimate(
            flops=4 * tokens * tokens * width * heads, transcendentals=131072, bytes_accessed=3000000
        ),
    )(place, counts, queries, token_keys, token_values)


def feature_kernel(
    place_ref,
    counts_ref,
    queries_ref,
    near_ref,
    far_ref,
    sum_ref,
    top_ref,
    mass_ref,
    weights_ref,
    features_ref,
):
    tokens, heads, width = queries_ref.shape
    row = lax.broadcasted_iota(jnp.int32, (tokens, tokens), 0)
    column = lax.broadcasted_iota(jnp.int32, (tokens, tokens), 1)
    near_allowed = column < place_count(counts_ref, place_ref, 1)
    far_allowed = (column > row) & (column < place_count(counts_ref, place_ref, 2))
    valid = lax.broadcasted_iota(jnp.int32, (tokens, 1), 0) < place_count(counts_ref, place_ref, 0)
    scale = 1.0 / math.sqrt(width)
    for head in range(heads):
        queries = queries_ref[:, head, :]
        near = product(queries, near_ref[head], 1, 1) * scale
        far = product(queries, far_ref[head], 1, 1) * scale
        near = jnp.where(near_allowed, near, LOWEST)
        far = jnp.where(far_allowed, far, LOWEST)
        own_top = top_ref[head][:, :1]
        top = jnp.maximum(own_top, jnp.max(jnp.maximum(near, far), axis=1, keepdims=True))
        near, far = jnp.exp(near - top), jnp.exp(far - top)
        kept = jnp.exp(own_top - top)
        mass = kept * mass_ref[head][:, :1] + jnp.sum(near + far, axis=1, keepdims=True)
        total = (
            kept * sum_ref[:, head * width : (head + 1) * width]
            + product(near.astype(jnp.bfloat16), near_ref[heads + head], 1, 0)
            + product(far.astype(jnp.bfloat16), far_ref[heads + head], 1, 0)
        )
        window = total / mass
        first = head * 3 * width
        gate = product(queries, weights_ref[first : first + width, :], 1, 1)
        up = product(queries, weights_ref[first + width : first + 2 * width, :], 1, 1)
        hidden = (gate * jax.nn.sigmoid(gate) * up).astype(jnp.bfloat16)
        learned = product(hidden, weights_ref[first + 2 * width : first + 3 * width, :], 1, 1)
        features_ref[:, head * width : (head + 1) * width] = jnp.where(
            valid, learned + window, 0.0
        ).astype(jnp.bfloat16)


def features_of(place, counts, queries, near, far, own_parts, new_flat):
    tokens, heads, width = queries.shape
    return pl.pallas_call(
        feature_kernel,
        out_shape=jax.ShapeDtypeStruct((tokens, heads * width), jnp.bfloat16),
        in_specs=[SMEM, SMEM] + [VMEM] * 7,
        out_specs=VMEM,
        name="features",
        compiler_params=pltpu.CompilerParams(vmem_limit_bytes=VMEM_BYTES),
        cost_estimate=pl.CostEstimate(
            flops=14 * tokens * tokens * width * heads,
            transcendentals=262144,
            bytes_accessed=3000000,
        ),
    )(place, counts, queries, near, far, *own_parts, new_flat)


def split_kernel(place_ref, mine_in_ref, theirs_in_ref, mine_ref, theirs_ref):
    mine_ref[...] = mine_in_ref[...]
    theirs_ref[...] = theirs_in_ref[...]


def column_halves(head_place, out_weight):
    depth, columns = out_weight.shape
    half = columns // 2
    tile = half // 2
    piece = jax.ShapeDtypeStruct((depth, half), out_weight.dtype)
    return pl.pallas_call(
        split_kernel,
        out_shape=(piece, piece),
        grid_spec=pltpu.PrefetchScalarGridSpec(
            num_scalar_prefetch=1,
            grid=(half // tile,),
            in_specs=[
                pl.BlockSpec((depth, tile), lambda step, place: (0, place[0] * 2 + step)),
                pl.BlockSpec((depth, tile), lambda step, place: (0, (1 - place[0]) * 2 + step)),
            ],
            out_specs=(
                pl.BlockSpec((depth, tile), lambda step, place: (0, step)),
                pl.BlockSpec((depth, tile), lambda step, place: (0, step)),
            ),
        ),
        name="split",
        compiler_params=pltpu.CompilerParams(vmem_limit_bytes=VMEM_BYTES),
        cost_estimate=pl.CostEstimate(flops=0, transcendentals=0, bytes_accessed=8000000),
    )(head_place, out_weight, out_weight)


def project_kernel(own_ref, other_ref, own_weight_ref, other_weight_ref, out_ref):
    out_ref[...] = (
        jnp.dot(own_ref[...], own_weight_ref[...], preferred_element_type=jnp.float32)
        + jnp.dot(other_ref[...], other_weight_ref[...], preferred_element_type=jnp.float32)
    ).astype(jnp.bfloat16)


def projected(own, other, own_weight, other_weight):
    tokens, depth = own.shape
    columns = other_weight.shape[1]
    tile = 512
    whole = pl.BlockSpec((tokens, depth), lambda step: (0, 0))
    piece = pl.BlockSpec((depth, tile), lambda step: (0, step))
    return pl.pallas_call(
        project_kernel,
        out_shape=jax.ShapeDtypeStruct((tokens, columns), jnp.bfloat16),
        grid=(columns // tile,),
        in_specs=[whole, whole, piece, piece],
        out_specs=pl.BlockSpec((tokens, tile), lambda step: (0, step)),
        name="project",
        compiler_params=pltpu.CompilerParams(vmem_limit_bytes=VMEM_BYTES),
        cost_estimate=pl.CostEstimate(
            flops=4 * tokens * depth * columns, transcendentals=0, bytes_accessed=6000000
        ),
    )(own, other, own_weight, other_weight)


def refresh_kernel(total, blocks_ref, old_ref, rows_ref):
    gradient = jnp.sum(blocks_ref[...].astype(jnp.float32), axis=0)
    gradient = jnp.concatenate([gradient[:4], gradient[4:]], 1)
    old = old_ref[...]
    updated = old - gradient / math.sqrt(total)
    old_norm = jnp.sqrt(jnp.sum(old * old, axis=1, keepdims=True))
    fresh = updated * old_norm / jnp.sqrt(jnp.sum(updated * updated, axis=1, keepdims=True) + 1e-06)
    rows_ref[...] = jnp.broadcast_to(fresh.astype(jnp.bfloat16)[None], rows_ref.shape)


def refreshed(total, copies, blocks, old_rows):
    return pl.pallas_call(
        functools.partial(refresh_kernel, total),
        out_shape=jax.ShapeDtypeStruct((copies, *old_rows.shape), jnp.bfloat16),
        in_specs=[VMEM, VMEM],
        out_specs=VMEM,
        name="refresh",
        compiler_params=pltpu.CompilerParams(vmem_limit_bytes=VMEM_BYTES),
        cost_estimate=pl.CostEstimate(flops=400000, transcendentals=0, bytes_accessed=1600000),
    )(blocks, old_rows)


def shards(queries, token_keys, token_values, step_rates, counts, fast_weights, out_weight):
    tok_rows, _, head_width = queries.shape
    device_count, plane_count = lax.axis_size(CTX), lax.axis_size("p")
    device_place, head_place = lax.axis_index(CTX), lax.axis_index("head")
    place = device_place.reshape(1).astype(jnp.int32)
    local_grad = local_gradient(place, counts, token_keys, token_values, step_rates, fast_weights)
    blocks = lax.all_to_all(local_grad.reshape(device_count, 8, 128), CTX, 0, 0, tiled=True)
    out_own, out_theirs = column_halves(
        head_place.reshape(1).astype(jnp.int32), out_weight
    )
    out_other = lax.ppermute(out_theirs, "head", [(0, 1), (1, 0)])
    pairs, *own_parts = own_attention(place, counts, queries, token_keys, token_values)
    old_flat = fast_weights.reshape(-1, head_width)
    own_rows = old_flat.shape[0] // device_count
    old_rows = lax.dynamic_slice_in_dim(old_flat, device_place * own_rows, own_rows, 0)
    new_rows = refreshed(tok_rows * device_count, plane_count, blocks, old_rows)
    held = lax.all_to_all(new_rows, "p", 0, 0, tiled=True)
    near = passed_along(pairs, 1)
    far = passed_along(pairs, 2)
    new_flat = lax.all_gather(held.reshape(-1, head_width), "z", axis=0, tiled=True)
    features = features_of(place, counts, queries, near, far, own_parts, new_flat)
    other = lax.ppermute(features, "head", [(0, 1), (1, 0)])
    return projected(features, other, out_own, out_other)


def solution(mesh):
    fine = Mesh(mesh.devices.reshape(RING, -1, 2), ("z", "p", "head"))
    in_specs = (
        P(CTX, "head", None),
        P(CTX, "head", None),
        P(CTX, "head", None),
        P(CTX, "head"),
        P(),
        P("head", None, None, None),
        P("head", None),
    )
    return jax.shard_map(
        shards, mesh=fine, in_specs=in_specs, out_specs=P(CTX, "head"), check_vma=False
    )
```

time: 153 us -> 148 us (0.967)
  local copies, waits for them, and re-layouts: 29.2 us -> 11.4 us
  blocking collectives: 21.7 us -> 35.3 us
  starting transfers between devices: 67.7 us -> 59 us
  waiting for transfers between devices: 16.7 us -> 24.9 us
  other arithmetic: 2.82 us -> 0 us
  Pallas kernels: 14.2 us -> 16.7 us
    all_to_all x2, waiting for transfers between devices: 9.43 us -> 23.7 us  [the longest x1 23.7 us: shards(): lax.all_to_all(local_grad.reshape(device_count, 8, 128), CTX, 0, 0, tiled...]
    all_gather x1, blocking collectives: 21.7 us -> 35.3 us  [shards(): lax.all_gather(held.reshape(-1, head_width), 'z', axis=0, tiled=True)]
    dynamic_slice x1, local copies, waits for them, and re-layouts: 8.45 us -> 0.71 us  [shards(): lax.dynamic_slice_in_dim(old_flat, device_place * own_rows, own_rows, 0)]
    reshape x3 -> x1, local copies, waits for them, and re-layouts: 8.98 us -> 1.67 us  [shards(): held.reshape(-1, head_width)]
    ppermute x1, starting transfers between devices: 18.8 us -> 12 us  [shards(): other = lax.ppermute(features, 'head', [(0, 1), (1, 0)])]
    ppermute x2, waiting for transfers between devices: 6.11 us -> 0.01 us  [passed_along(): lax.ppermute(value, CTX, [(source, source + steps) for source in range(co...]
    ppermute x2, starting transfers between devices: 9.91 us -> 7.69 us  [passed_along(): lax.ppermute(value, CTX, [(source, source + steps) for source in range(co...]
    pallas_call x1, Pallas kernels: 2.37 us -> 4.27 us  [local_gradient(): pl.pallas_call(gradient_kernel, out_shape=jax.ShapeDtypeStruct((heads * m...]
  transfers between devices with their start and end apart: 6 -> 6, of which waited for: 4 -> 2; matrix products, arithmetic and copies ran while one was open for 16% -> 2% of each run, Pallas kernels for 5% -> 5%
where the time goes in v2:
time: 148 us; the launch traced here: 147 us
  starting transfers between devices  59 us (40%)
  blocking collectives  35.3 us (24%)
  waiting for transfers between devices  24.9 us (17%)
  Pallas kernels  16.7 us (11%)
  local copies, waits for them, and re-layouts  11.4 us (8%)
    all_gather x1, blocking collectives, shards(): lax.all_gather(held.reshape(-1, head_width), 'z', axis=0, tiled=True)  35.3 us
    all_to_all x1, starting transfers between devices, shards(): lax.all_to_all(local_grad.reshape(device_count, 8, 128), CTX, 0, 0, tiled...  25.7 us
    all_to_all x1, waiting for transfers between devices, shards(): lax.all_to_all(local_grad.reshape(device_count, 8, 128), CTX, 0, 0, tiled...  23.7 us
    ppermute x1, starting transfers between devices, shards(): other = lax.ppermute(features, 'head', [(0, 1), (1, 0)])  12 us
    all_to_all x1, starting transfers between devices, shards(): held = lax.all_to_all(new_rows, 'p', 0, 0, tiled=True)  10.5 us
    unnamed x26, local copies, waits for them, and re-layouts  8.99 us
    ppermute x2, starting transfers between devices, passed_along(): lax.ppermute(value, CTX, [(source, source + steps) for source in range(co...  7.69 us
    pallas_call x1, Pallas kernels, projected(): pl.pallas_call(project_kernel, out_shape=jax.ShapeDtypeStruct((tokens, co...  4.48 us
  transfers between devices with their start and end apart: 6, of which 2 were waited for; matrix products, arithmetic and copies ran while one was open for 2% of the time, Pallas kernels for 5%

profile of v2, /device:TPU:127, one launch (start us, length us, event | category | flops | bytes accessed | tf_op | source)
XLA Modules:
  0.0 147.3 jit_solution(8873985324503538982)
XLA Ops:
  0.0 4.3 %gradient.1 = bf16[192,2,8,128]{3,2,1,0:T(8,128)(2,1)} custom-call(s32[1]{0:T(128)} %bitcast.place_ref, s32[384]{0:T(512)} %counts_ref.5, bf16[256,2,256]{2,1,0:T(2,128)(2,1)} %keys_ref.3, bf16[256,2,256]{2,1,0:T(2,128)(2,1)} %values_ref.3, f32[2,256]{1,0:T(2,128)} %bitcast.7, f32[2,3,256,256]{3,2,1,0:T(8,128)} %weights_ref.1), custom_call_target="tpu_custom_call" | custom-call | flops 469762048 | bytes 3000000 | tf_op jit(solution)/shard_map/gradient/pallas_call | solution.py:87
  4.3 25.7 %all-to-all-start = ((bf16[384,8,128]{2,1,0:T(8,128)(2,1)}), bf16[384,8,128]{2,1,0:T(8,128)(2,1)S(1)}, u32[]{:S(2)}, u32[]{:S(2)}) async-start(bf16[384,8,128]{2,1,0:T(8,128)(2,1)} %bitcast.5), calls=%async_computation | async-start | bytes 1572864 | tf_op jit(solution)/shard_map/all_to_all | solution.py:293
  30.0 0.0 copy-start
  30.0 2.2 %copy-done = bf16[512,4096]{1,0:T(8,128)(2,1)S(1)} copy-done((bf16[512,4096]{1,0:T(8,128)(2,1)S(1)}, bf16[512,4096]{1,0:T(8,128)(2,1)}, u32[]{:S(2)}) %copy-start) | copy-done | bytes 4194328
  32.2 1.8 %split.1 = (bf16[512,2048]{1,0:T(8,128)(2,1)S(1)}, bf16[512,2048]{1,0:T(8,128)(2,1)}) custom-call(s32[1]{0:T(128)} %bitcast.4.place_ref, bf16[512,4096]{1,0:T(8,128)(2,1)S(1)} %copy-done, bf16[512,4096]{1,0:T(8,128)(2,1)S(1)} %copy-done), custom_call_target="tpu_custom_call" | custom-call | bytes 8000000 | tf_op jit(solution)/shard_map/split/pallas_call | solution.py:217
  34.0 3.1 %collective-permute-start.3 = (bf16[512,2048]{1,0:T(8,128)(2,1)}, bf16[512,2048]{1,0:T(8,128)(2,1)}, u32[]{:S(2)}, u32[]{:S(2)}) collective-permute-start(bf16[512,2048]{1,0:T(8,128)(2,1)} %get-tuple-element.16), channel_id=1, source_target_pairs={{0,1},{1,0},{2,3},{3,2},{4,5},{5,4},{6,7},{7,6},{8,9},{9,8},{10,11... | collective-permute-start | bytes 6291464 | tf_op jit(solution)/shard_map/ppermute | solution.py:297
  37.2 0.7 constant_dynamic-slice_fusion.old_ref
  37.9 23.7 %all-to-all-done.blocks_ref = bf16[384,8,128]{2,1,0:T(8,128)(2,1)S(1)} async-done(((bf16[384,8,128]{2,1,0:T(8,128)(2,1)}), bf16[384,8,128]{2,1,0:T(8,128)(2,1)S(1)}, u32[]{:S(2)}, u32[]{:S(2)}) %all-to-all-start) | async-done | bytes 786464 | tf_op jit(solution)/shard_map/all_to_all | solution.py:293
  61.6 0.6 refresh.1
  62.2 0.7 copy-done.5
  62.9 10.5 %all-to-all-start.1 = ((bf16[96,4,256]{2,1,0:T(4,128)(2,1)}), bf16[96,4,256]{2,1,0:T(4,128)(2,1)}, u32[]{:S(2)}, u32[]{:S(2)}) async-start(bf16[96,4,256]{2,1,0:T(4,128)(2,1)} %copy-done.5), calls=%async_computation.1 | async-start | bytes 393216 | tf_op jit(solution)/shard_map/all_to_all | solution.py:303
  73.4 0.0 copy-start.3
  73.4 0.9 copy-done.3
  74.3 3.3 %own_attention.1 = (bf16[4,256,256]{2,1,0:T(8,128)(2,1)}, f32[256,512]{1,0:T(8,128)S(1)}, f32[2,256,128]{2,1,0:T(8,128)S(1)}, f32[2,256,128]{2,1,0:T(8,128)S(1)}) custom-call(s32[1]{0:T(128)} %bitcast.place_ref, s32[384]{0:T(512)S(1)} %copy-done.12, bf16[256,2,256]{2,1,0:T(2,128)(2,1)S(1)} %copy-done.3, bf16[256,2,256]{2,1,0:T(2,128)(2,1)S(1)} %copy-done.1, ...), custom_call_target="tpu_custom_call" | custom-call | flops 134217728 | bytes 3000000 | tf_op jit(solution)/shard_map/own_attention/pallas_call | solution.py:126
  77.6 0.8 copy-done.6
  78.4 0.7 copy-done.8
  79.2 0.7 copy-done.10
  79.9 4.0 %collective-permute-start.1 = (bf16[4,256,256]{2,1,0:T(8,128)(2,1)}, bf16[4,256,256]{2,1,0:T(8,128)(2,1)S(1)}, u32[]{:S(2)}, u32[]{:S(2)}) collective-permute-start(bf16[4,256,256]{2,1,0:T(8,128)(2,1)} %get-tuple-element.11), channel_id=1, source_target_pairs={{0,4},{2,6},{4,8},{6,10},{8,12},{10,14},{12,16},{14,18},{16,20},{1... | collective-permute-start | bytes 1572872 | tf_op jit(solution)/shard_map/ppermute | solution.py:22
  83.9 3.7 %collective-permute-start = (bf16[4,256,256]{2,1,0:T(8,128)(2,1)}, bf16[4,256,256]{2,1,0:T(8,128)(2,1)S(1)}, u32[]{:S(2)}, u32[]{:S(2)}) collective-permute-start(bf16[4,256,256]{2,1,0:T(8,128)(2,1)} %get-tuple-element.11), channel_id=1, source_target_pairs={{0,2},{2,4},{4,6},{6,8},{8,10},{10,12},{12,14},{14,16},{16,18},{18... | collective-permute-start | bytes 1572872 | tf_op jit(solution)/shard_map/ppermute | solution.py:22
  87.6 0.0 all-to-all-done.1
  87.6 1.7 %reshape.18 = bf16[384,256]{1,0:T(8,128)(2,1)} reshape(bf16[96,4,256]{2,1,0:T(4,128)(2,1)} %all-to-all-done.1) | data formatting | bytes 393216 | tf_op jit(solution)/shard_map/reshape | solution.py:306
  89.3 35.3 %all_gather.3.weights_ref = bf16[1536,256]{1,0:T(8,128)(2,1)S(1)} all-gather(bf16[384,256]{1,0:T(8,128)(2,1)} %reshape.18), channel_id=1, replica_groups=mesh['z'=4,'p'=96,'head'=2] {'z'}, dimensions={0}, use_global_device_ids=true | all-gather | bytes 983040 | tf_op jit(solution)/shard_map/all_gather | solution.py:306
  124.5 0.0 collective-permute-done.1.far_ref
  124.5 0.0 collective-permute-done.near_ref
  124.6 1.0 copy-done.7
  125.6 0.9 copy-done.9
  126.6 0.9 copy-done.11
  127.5 2.2 %features.1.own_ref = bf16[256,512]{1,0:T(8,128)(2,1)S(1)} custom-call(s32[1]{0:T(128)} %bitcast.place_ref, s32[384]{0:T(512)S(1)} %copy-done.12, bf16[256,2,256]{2,1,0:T(2,128)(2,1)S(1)} %copy-done.4, bf16[4,256,256]{2,1,0:T(8,128)(2,1)S(1)} %collective-permute-done.near_ref, bf16[4,256,256]{2,1,0:T(8,128)(2,1)S(1)} %collective-permute-done.1.far_ref, ...), custom_call_target="tpu_custom_call" | custom-call | flops 469762048 | bytes 3000000 | tf_op jit(solution)/shard_map/features/pallas_call | solution.py:192
  129.7 12.0 %collective-permute-start.2 = (bf16[256,512]{1,0:T(8,128)(2,1)S(1)}, bf16[256,512]{1,0:T(8,128)(2,1)S(1)}, u32[]{:S(2)}, u32[]{:S(2)}) collective-permute-start(bf16[256,512]{1,0:T(8,128)(2,1)S(1)} %features.1.own_ref), channel_id=1, source_target_pairs={{0,1},{1,0},{2,3},{3,2},{4,5},{5,4},{6,7},{7,6},{8,9},{9,8},{10,11... | collective-permute-start | bytes 786440 | tf_op jit(solution)/shard_map/ppermute | solution.py:308
  141.7 0.0 collective-permute-done.3.other_weight_ref
  141.7 1.1 collective-permute-done.2.other_ref
  142.8 4.5 %project.1 = bf16[256,2048]{1,0:T(8,128)(2,1)} custom-call(bf16[256,512]{1,0:T(8,128)(2,1)S(1)} %features.1.own_ref, bf16[256,512]{1,0:T(8,128)(2,1)S(1)} %collective-permute-done.2.other_ref, bf16[512,2048]{1,0:T(8,128)(2,1)S(1)} %get-tuple-element.15.own_weight_ref, bf16[512,2048]{1,0:T(8,128)(2,1)} %collective-permute-done.3.other_weight_ref), custom_call_target="tpu_custom_call" | custom-call | flops 1073741824 | bytes 6000000 | tf_op jit(solution)/shard_map/project/pallas_call | solution.py:251
  (15 shorter events, 0.0 us)
Async XLA Ops:
  4.3 57.3 %all-to-all-start = ((bf16[384,8,128]{2,1,0:T(8,128)(2,1)}), bf16[384,8,128]{2,1,0:T(8,128)(2,1)S(1)}, u32[]{:S(2)}, u32[]{:S(2)}) async-start(bf16[384,8,128]{2,1,0:T(8,128)(2,1)} %bitcast.5), calls=%async_computation | async-start | bytes 1572864 | tf_op jit(solution)/shard_map/all_to_all | solution.py:293
  30.0 2.2 %copy-start = (bf16[512,4096]{1,0:T(8,128)(2,1)S(1)}, bf16[512,4096]{1,0:T(8,128)(2,1)}, u32[]{:S(2)}) copy-start(bf16[512,4096]{1,0:T(8,128)(2,1)} %theirs_in_ref.1) | copy-start | bytes 12582916
  32.2 41.2 %copy-start.1 = (bf16[256,2,256]{2,1,0:T(2,128)(2,1)S(1)}, bf16[256,2,256]{2,1,0:T(2,128)(2,1)}, u32[]{:S(2)}) copy-start(bf16[256,2,256]{2,1,0:T(2,128)(2,1)} %keys_ref.3) | copy-start | bytes 786436
  32.2 41.2 %copy-start.2 = (bf16[256,2,256]{2,1,0:T(2,128)(2,1)S(1)}, bf16[256,2,256]{2,1,0:T(2,128)(2,1)}, u32[]{:S(2)}) copy-start(bf16[256,2,256]{2,1,0:T(2,128)(2,1)} %values_ref.3) | copy-start | bytes 786436
  32.2 41.2 %copy-start.12 = (s32[384]{0:T(512)S(1)}, s32[384]{0:T(512)}, u32[]{:S(2)}) copy-start(s32[384]{0:T(512)} %counts_ref.5) | copy-start | bytes 4612
  34.0 107.7 %collective-permute-start.3 = (bf16[512,2048]{1,0:T(8,128)(2,1)}, bf16[512,2048]{1,0:T(8,128)(2,1)}, u32[]{:S(2)}, u32[]{:S(2)}) collective-permute-start(bf16[512,2048]{1,0:T(8,128)(2,1)} %get-tuple-element.16), channel_id=1, source_target_pairs={{0,1},{1,0},{2,3},{3,2},{4,5},{5,4},{6,7},{7,6},{8,9},{9,8},{10,11... | collective-permute-start | bytes 6291464 | tf_op jit(solution)/shard_map/ppermute | solution.py:297
  62.2 0.7 copy-start.5
  62.9 61.7 %copy-start.4 = (bf16[256,2,256]{2,1,0:T(2,128)(2,1)S(1)}, bf16[256,2,256]{2,1,0:T(2,128)(2,1)}, u32[]{:S(2)}) copy-start(bf16[256,2,256]{2,1,0:T(2,128)(2,1)} %queries_ref.3) | copy-start | bytes 786436
  62.9 24.7 %all-to-all-start.1 = ((bf16[96,4,256]{2,1,0:T(4,128)(2,1)}), bf16[96,4,256]{2,1,0:T(4,128)(2,1)}, u32[]{:S(2)}, u32[]{:S(2)}) async-start(bf16[96,4,256]{2,1,0:T(4,128)(2,1)} %copy-done.5), calls=%async_computation.1 | async-start | bytes 393216 | tf_op jit(solution)/shard_map/all_to_all | solution.py:303
  73.4 1.0 copy-start.3
  77.6 0.8 copy-start.6
  78.4 0.7 copy-start.8
  79.2 0.7 copy-start.10
  79.9 44.7 %collective-permute-start.1 = (bf16[4,256,256]{2,1,0:T(8,128)(2,1)}, bf16[4,256,256]{2,1,0:T(8,128)(2,1)S(1)}, u32[]{:S(2)}, u32[]{:S(2)}) collective-permute-start(bf16[4,256,256]{2,1,0:T(8,128)(2,1)} %get-tuple-element.11), channel_id=1, source_target_pairs={{0,4},{2,6},{4,8},{6,10},{8,12},{10,14},{12,16},{14,18},{16,20},{1... | collective-permute-start | bytes 1572872 | tf_op jit(solution)/shard_map/ppermute | solution.py:22
  83.9 40.7 %collective-permute-start = (bf16[4,256,256]{2,1,0:T(8,128)(2,1)}, bf16[4,256,256]{2,1,0:T(8,128)(2,1)S(1)}, u32[]{:S(2)}, u32[]{:S(2)}) collective-permute-start(bf16[4,256,256]{2,1,0:T(8,128)(2,1)} %get-tuple-element.11), channel_id=1, source_target_pairs={{0,2},{2,4},{4,6},{6,8},{8,10},{10,12},{12,14},{14,16},{16,18},{18... | collective-permute-start | bytes 1572872 | tf_op jit(solution)/shard_map/ppermute | solution.py:22
  124.6 1.0 copy-start.7
  125.6 0.9 copy-start.9
  126.5 0.9 copy-start.11
  129.7 13.1 %collective-permute-start.2 = (bf16[256,512]{1,0:T(8,128)(2,1)S(1)}, bf16[256,512]{1,0:T(8,128)(2,1)S(1)}, u32[]{:S(2)}, u32[]{:S(2)}) collective-permute-start(bf16[256,512]{1,0:T(8,128)(2,1)S(1)} %features.1.own_ref), channel_id=1, source_target_pairs={{0,1},{1,0},{2,3},{3,2},{4,5},{5,4},{6,7},{7,6},{8,9},{9,8},{10,11... | collective-permute-start | bytes 786440 | tf_op jit(solution)/shard_map/ppermute | solution.py:308

commit v3 on v2

--- a/solution.py
+++ b/solution.py
@@ -20,6 +20,14 @@
 def passed_along(value, steps):
     count = lax.axis_size(CTX)
     return lax.ppermute(value, CTX, [(source, source + steps) for source in range(count - steps)])
+
+
+def passed_in_plane(value):
+    return lax.ppermute(value, "p", [(place, place + 1) for place in range(lax.axis_size("p") - 1)])
+
+
+def turned(value, steps):
+    return lax.ppermute(value, "z", [(place, (place + steps) % RING) for place in range(RING)])
 
 
 def product(left, right, left_dim, right_dim):
@@ -46,8 +54,12 @@
     return even.astype(jnp.bfloat16), odd.astype(jnp.bfloat16)
 
 
-def gradient_kernel(place_ref, counts_ref, keys_ref, values_ref, rates_ref, weights_ref, grad_ref):
+def gradient_kernel(
+    place_ref, counts_ref, keys_ref, values_ref, rates_ref, weights_ref, *parts
+):
+    quarter_refs, (held_ref, sems) = parts[:RING], parts[RING:]
     tokens, heads, width = keys_ref.shape
+    pieces = held_ref.shape[1]
     valid = lax.broadcasted_iota(jnp.int32, (tokens, 1), 0) < place_count(counts_ref, place_ref, 0)
     rates_all = jnp.concatenate(
         [rates_ref[...], jnp.zeros((8 - heads, tokens), jnp.float32)], 0
@@ -74,21 +86,40 @@
             product(grad_up, keys, 0, 0),
             -product(scaled, hidden, 0, 0),
         )
-        blocks = width // 8
+        half = width // 16
         for index, mat in enumerate(mats):
-            first = (head * 3 + index) * blocks
             even, odd = chunked(mat)
-            grad_ref[first : first + blocks, 0] = even
-            grad_ref[first : first + blocks, 1] = odd
+            for side in range(2):
+                piece = (head * 3 + index) * 2 + side
+                rows = slice(side * half, (side + 1) * half)
+                held_ref[piece // pieces, piece % pieces, :, 0] = even[rows]
+                held_ref[piece // pieces, piece % pieces, :, 1] = odd[rows]
+    ring_place = place_ref[1]
+    copies = [
+        pltpu.make_async_copy(
+            held_ref.at[lax.rem(ring_place + steps, RING)], quarter_refs[steps], sems.at[steps]
+        )
+        for steps in range(RING)
+    ]
+    for copy in copies:
+        copy.start()
+    for copy in copies:
+        copy.wait()
 
 
 def local_gradient(place, counts, token_keys, token_values, step_rates, fast_weights):
     heads, mats, width, _ = fast_weights.shape
+    shape = (2 * heads * mats // RING, width // 16, 2, 8, 128)
+    quarter = jax.ShapeDtypeStruct(shape, jnp.bfloat16)
     return pl.pallas_call(
         gradient_kernel,
-        out_shape=jax.ShapeDtypeStruct((heads * mats * width // 8, 2, 8, 128), jnp.bfloat16),
+        out_shape=(quarter,) * RING,
         in_specs=[SMEM, SMEM, VMEM, VMEM, VMEM, VMEM],
-        out_specs=VMEM,
+        out_specs=(pl.BlockSpec(memory_space=pl.ANY),) * RING,
+        scratch_shapes=[
+            pltpu.VMEM((RING, *shape), jnp.bfloat16),
+            pltpu.SemaphoreType.DMA((RING,)),
+        ],
         name="gradient",
         cost_estimate=pl.CostEstimate(
             flops=14 * 256 * width * width * heads, transcendentals=131072, bytes_accessed=3000000
@@ -96,49 +127,57 @@
     )(place, counts, token_keys, token_values, step_rates.T, fast_weights)
 
 
-def own_kernel(
-    place_ref, counts_ref, queries_ref, keys_ref, values_ref, pairs_ref, sum_ref, top_ref, mass_ref
-):
+def pair_kernel(keys_ref, values_ref, pairs_ref):
+    heads = keys_ref.shape[1]
+    for head in range(heads):
+        pairs_ref[head] = keys_ref[:, head, :]
+        pairs_ref[heads + head] = values_ref[:, head, :]
+
+
+def paired(token_keys, token_values):
+    tokens, heads, width = token_keys.shape
+    return pl.pallas_call(
+        pair_kernel,
+        out_shape=jax.ShapeDtypeStruct((2 * heads, tokens, width), jnp.bfloat16),
+        in_specs=[VMEM, VMEM],
+        out_specs=VMEM,
+        name="pair",
+        cost_estimate=pl.CostEstimate(flops=0, transcendentals=0, bytes_accessed=2000000),
+    )(token_keys, token_values)
+
+
+def own_kernel(place_ref, counts_ref, queries_ref, pairs_ref, state_ref):
     tokens, heads, width = queries_ref.shape
     row = lax.broadcasted_iota(jnp.int32, (tokens, tokens), 0)
     column = lax.broadcasted_iota(jnp.int32, (tokens, tokens), 1)
     allowed = (column <= row) & (column < place_count(counts_ref, place_ref, 0))
     scale = 1.0 / math.sqrt(width)
     for head in range(heads):
-        keys, values = keys_ref[:, head, :], values_ref[:, head, :]
-        pairs_ref[head] = keys
-        pairs_ref[heads + head] = values
-        own = product(queries_ref[:, head, :], keys, 1, 1) * scale
+        own = product(queries_ref[:, head, :], pairs_ref[head], 1, 1) * scale
         own = jnp.where(allowed, own, LOWEST)
         top = jnp.max(own, axis=1, keepdims=True)
         own = jnp.exp(own - top)
         mass = jnp.sum(own, axis=1, keepdims=True)
-        sum_ref[:, head * width : (head + 1) * width] = product(
-            own.astype(jnp.bfloat16), values, 1, 0
+        state_ref[head, :, :width] = product(
+            own.astype(jnp.bfloat16), pairs_ref[heads + head], 1, 0
         )
-        top_ref[head] = jnp.broadcast_to(top, top_ref.shape[1:])
-        mass_ref[head] = jnp.broadcast_to(mass, mass_ref.shape[1:])
-
-
-def own_attention(place, counts, queries, token_keys, token_values):
+        state_ref[head, :, width : width + 128] = jnp.broadcast_to(top, (tokens, 128))
+        state_ref[head, :, width + 128 :] = jnp.broadcast_to(mass, (tokens, 128))
+
+
+def own_attention(place, counts, queries, pairs):
     tokens, heads, width = queries.shape
-    side = jax.ShapeDtypeStruct((heads, tokens, 128), jnp.float32)
     return pl.pallas_call(
         own_kernel,
-        out_shape=(
-            jax.ShapeDtypeStruct((2 * heads, tokens, width), jnp.bfloat16),
-            jax.ShapeDtypeStruct((tokens, heads * width), jnp.float32),
-            side,
-            side,
-        ),
-        in_specs=[SMEM, SMEM, VMEM, VMEM, VMEM],
-        out_specs=(VMEM, VMEM, VMEM, VMEM),
+        out_shape=jax.ShapeDtypeStruct((heads, tokens, width + 256), jnp.float32),
+        in_specs=[SMEM, SMEM, VMEM, VMEM],
+        out_specs=VMEM,
         name="own_attention",
         compiler_params=pltpu.CompilerParams(vmem_limit_bytes=VMEM_BYTES),
         cost_estimate=pl.CostEstimate(
             flops=4 * tokens * tokens * width * heads, transcendentals=131072, bytes_accessed=3000000
         ),
-    )(place, counts, queries, token_keys, token_values)
+    )(place, counts, queries, pairs)
 
 
 def feature_kernel(
@@ -146,10 +185,9 @@
     counts_ref,
     queries_ref,
     near_ref,
+    first_ref,
     far_ref,
-    sum_ref,
-    top_ref,
-    mass_ref,
+    state_ref,
     weights_ref,
     features_ref,
 ):
@@ -160,20 +198,24 @@
     far_allowed = (column > row) & (column < place_count(counts_ref, place_ref, 2))
     valid = lax.broadcasted_iota(jnp.int32, (tokens, 1), 0) < place_count(counts_ref, place_ref, 0)
     scale = 1.0 / math.sqrt(width)
+    at_start = place_ref[2] == 0
     for head in range(heads):
         queries = queries_ref[:, head, :]
-        near = product(queries, near_ref[head], 1, 1) * scale
+        near_keys = jnp.where(at_start, first_ref[head], near_ref[head])
+        near_values = jnp.where(at_start, first_ref[heads + head], near_ref[heads + head])
+        near = product(queries, near_keys, 1, 1) * scale
         far = product(queries, far_ref[head], 1, 1) * scale
         near = jnp.where(near_allowed, near, LOWEST)
         far = jnp.where(far_allowed, far, LOWEST)
-        own_top = top_ref[head][:, :1]
+        own_top = state_ref[head, :, width : width + 1]
+        own_mass = state_ref[head, :, width + 128 : width + 129]
         top = jnp.maximum(own_top, jnp.max(jnp.maximum(near, far), axis=1, keepdims=True))
         near, far = jnp.exp(near - top), jnp.exp(far - top)
         kept = jnp.exp(own_top - top)
-        mass = kept * mass_ref[head][:, :1] + jnp.sum(near + far, axis=1, keepdims=True)
+        mass = kept * own_mass + jnp.sum(near + far, axis=1, keepdims=True)
         total = (
-            kept * sum_ref[:, head * width : (head + 1) * width]
-            + product(near.astype(jnp.bfloat16), near_ref[heads + head], 1, 0)
+            kept * state_ref[head, :, :width]
+            + product(near.astype(jnp.bfloat16), near_values, 1, 0)
             + product(far.astype(jnp.bfloat16), far_ref[heads + head], 1, 0)
         )
         window = total / mass
@@ -187,12 +229,12 @@
         ).astype(jnp.bfloat16)
 
 
-def features_of(place, counts, queries, near, far, own_parts, new_flat):
+def features_of(place, counts, queries, near, first, far, state, new_flat):
     tokens, heads, width = queries.shape
     return pl.pallas_call(
         feature_kernel,
         out_shape=jax.ShapeDtypeStruct((tokens, heads * width), jnp.bfloat16),
-        in_specs=[SMEM, SMEM] + [VMEM] * 7,
+        in_specs=[SMEM, SMEM] + [VMEM] * 6,
         out_specs=VMEM,
         name="features",
         compiler_params=pltpu.CompilerParams(vmem_limit_bytes=VMEM_BYTES),
@@ -201,7 +243,7 @@
             transcendentals=262144,
             bytes_accessed=3000000,
         ),
-    )(place, counts, queries, near, far, *own_parts, new_flat)
+    )(place, counts, queries, near, first, far, state, new_flat)
 
 
 def split_kernel(place_ref, mine_in_ref, theirs_in_ref, mine_ref, theirs_ref):
@@ -235,31 +277,51 @@
     )(head_place, out_weight, out_weight)
 
 
-def project_kernel(own_ref, other_ref, own_weight_ref, other_weight_ref, out_ref):
+def own_project_kernel(own_ref, weight_ref, out_ref):
+    out_ref[...] = jnp.dot(own_ref[...], weight_ref[...], preferred_element_type=jnp.float32)
+
+
+def own_projected(own, weight):
+    return pl.pallas_call(
+        own_project_kernel,
+        out_shape=jax.ShapeDtypeStruct((own.shape[0], weight.shape[1]), jnp.float32),
+        in_specs=[VMEM, VMEM],
+        out_specs=VMEM,
+        name="own_project",
+        compiler_params=pltpu.CompilerParams(vmem_limit_bytes=VMEM_BYTES),
+        cost_estimate=pl.CostEstimate(
+            flops=2 * own.shape[0] * weight.size, transcendentals=0, bytes_accessed=4000000
+        ),
+    )(own, weight)
+
+
+def project_kernel(other_ref, weight_ref, own_ref, out_ref):
     out_ref[...] = (
-        jnp.dot(own_ref[...], own_weight_ref[...], preferred_element_type=jnp.float32)
-        + jnp.dot(other_ref[...], other_weight_ref[...], preferred_element_type=jnp.float32)
+        own_ref[...]
+        + jnp.dot(other_ref[...], weight_ref[...], preferred_element_type=jnp.float32)
     ).astype(jnp.bfloat16)
 
 
-def projected(own, other, own_weight, other_weight):
-    tokens, depth = own.shape
-    columns = other_weight.shape[1]
-    tile = 512
-    whole = pl.BlockSpec((tokens, depth), lambda step: (0, 0))
-    piece = pl.BlockSpec((depth, tile), lambda step: (0, step))
+def projected(other, weight, own_product):
+    tokens, depth = other.shape
+    columns = weight.shape[1]
+    tile = columns // 2
     return pl.pallas_call(
         project_kernel,
         out_shape=jax.ShapeDtypeStruct((tokens, columns), jnp.bfloat16),
         grid=(columns // tile,),
-        in_specs=[whole, whole, piece, piece],
+        in_specs=[
+            pl.BlockSpec((tokens, depth), lambda step: (0, 0)),
+            pl.BlockSpec((depth, tile), lambda step: (0, step)),
+            pl.BlockSpec((tokens, tile), lambda step: (0, step)),
+        ],
         out_specs=pl.BlockSpec((tokens, tile), lambda step: (0, step)),
         name="project",
         compiler_params=pltpu.CompilerParams(vmem_limit_bytes=VMEM_BYTES),
         cost_estimate=pl.CostEstimate(
-            flops=4 * tokens * depth * columns, transcendentals=0, bytes_accessed=6000000
-        ),
-    )(own, other, own_weight, other_weight)
+            flops=2 * tokens * depth * columns, transcendentals=0, bytes_accessed=6000000
+        ),
+    )(other, weight, own_product)
 
 
 def refresh_kernel(total, blocks_ref, old_ref, rows_ref):
@@ -288,25 +350,36 @@
     tok_rows, _, head_width = queries.shape
     device_count, plane_count = lax.axis_size(CTX), lax.axis_size("p")
     device_place, head_place = lax.axis_index(CTX), lax.axis_index("head")
-    place = device_place.reshape(1).astype(jnp.int32)
-    local_grad = local_gradient(place, counts, token_keys, token_values, step_rates, fast_weights)
-    blocks = lax.all_to_all(local_grad.reshape(device_count, 8, 128), CTX, 0, 0, tiled=True)
-    out_own, out_theirs = column_halves(
-        head_place.reshape(1).astype(jnp.int32), out_weight
+    place = jnp.stack([device_place, lax.axis_index("z"), lax.axis_index("p"), head_place])
+    place = place.astype(jnp.int32)
+    pairs = paired(token_keys, token_values)
+    far = passed_along(pairs, 2)
+    quarters = local_gradient(
+        place, counts, token_keys, token_values, step_rates, fast_weights
     )
+    arrived = []
+    for steps in range(1, RING):
+        arrived.append(turned(quarters[steps], steps))
+    summed = quarters[0].astype(jnp.float32)
+    for part in arrived:
+        summed = summed + part.astype(jnp.float32)
+    summed = summed.astype(jnp.bfloat16).reshape(plane_count, 8, 128)
+    blocks = lax.all_to_all(summed, "p", 0, 0, tiled=True)
+    out_own, out_theirs = column_halves(place[3:], out_weight)
     out_other = lax.ppermute(out_theirs, "head", [(0, 1), (1, 0)])
-    pairs, *own_parts = own_attention(place, counts, queries, token_keys, token_values)
+    state = own_attention(place, counts, queries, pairs)
     old_flat = fast_weights.reshape(-1, head_width)
     own_rows = old_flat.shape[0] // device_count
     old_rows = lax.dynamic_slice_in_dim(old_flat, device_place * own_rows, own_rows, 0)
     new_rows = refreshed(tok_rows * device_count, plane_count, blocks, old_rows)
     held = lax.all_to_all(new_rows, "p", 0, 0, tiled=True)
-    near = passed_along(pairs, 1)
-    far = passed_along(pairs, 2)
+    first = lax.ppermute(far, "p", [(1, 0)])
+    near = passed_in_plane(pairs)
     new_flat = lax.all_gather(held.reshape(-1, head_width), "z", axis=0, tiled=True)
-    features = features_of(place, counts, queries, near, far, own_parts, new_flat)
+    features = features_of(place, counts, queries, near, first, far, state, new_flat)
     other = lax.ppermute(features, "head", [(0, 1), (1, 0)])
-    return projected(features, other, out_own, out_other)
+    own_product = own_projected(features, out_own)
+    return projected(other, out_other, own_product)
 
 
 def solution(mesh):

time: 148 us -> 139 us (0.939)
  the two profiles are of different devices: /device:TPU:127 before, /device:TPU:1 now
where the time goes in v3:
time: 139 us; the launch traced here: 138 us
  starting transfers between devices  65.8 us (47%)
  blocking collectives  27.8 us (20%)
  waiting for transfers between devices  18.5 us (13%)
  Pallas kernels  17.5 us (13%)
  local copies, waits for them, and re-layouts  6.9 us (5%)
  other arithmetic  1.45 us (1%)
    all_gather x1, blocking collectives, shards(): lax.all_gather(held.reshape(-1, head_width), 'z', axis=0, tiled=True)  27.8 us
    ppermute x3, starting transfers between devices, turned(): lax.ppermute(value, 'z', [(place, (place + steps) % RING) for place in ra...  23.4 us
    ppermute x3, waiting for transfers between devices, turned(): lax.ppermute(value, 'z', [(place, (place + steps) % RING) for place in ra...  13.6 us
    all_to_all x1, starting transfers between devices, shards(): blocks = lax.all_to_all(summed, 'p', 0, 0, tiled=True)  13.1 us
    all_to_all x1, starting transfers between devices, shards(): held = lax.all_to_all(new_rows, 'p', 0, 0, tiled=True)  8.63 us
    ppermute x1, starting transfers between devices, shards(): other = lax.ppermute(features, 'head', [(0, 1), (1, 0)])  7.44 us
    ppermute x1, starting transfers between devices, passed_along(): lax.ppermute(value, CTX, [(source, source + steps) for source in range(co...  5 us
    unnamed x16, local copies, waits for them, and re-layouts  4.54 us
  transfers between devices with their start and end apart: 10, of which 4 were waited for; matrix products, arithmetic and copies ran while one was open for 2% of the time, Pallas kernels for 8%

profile of v3, /device:TPU:1, one launch (start us, length us, event | category | flops | bytes accessed | tf_op | source)
XLA Modules:
  0.0 138.2 jit_solution(1492828148854082882)
XLA Ops:
  0.0 0.7 pad_add_fusion.place_ref
  0.7 4.3 %gradient.1 = (bf16[3,16,2,8,128]{4,3,2,1,0:T(8,128)(2,1)}, bf16[3,16,2,8,128]{4,3,2,1,0:T(8,128)(2,1)}, bf16[3,16,2,8,128]{4,3,2,1,0:T(8,128)(2,1)}, bf16[3,16,2,8,128]{4,3,2,1,0:T(8,128)(2,1)}) custom-call(s32[4]{0:T(128)} %pad_add_fusion.place_ref, s32[384]{0:T(512)} %counts_ref.5, bf16[256,2,256]{2,1,0:T(2,128)(2,1)} %keys_ref.3, ...), custom_call_target="tpu_custom_call" | custom-call | flops 469762048 | bytes 3000000 | tf_op jit(solution)/shard_map/gradient/pallas_call | solution.py:114
  5.0 8.4 %collective-permute-start.3 = (bf16[3,16,2,8,128]{4,3,2,1,0:T(8,128)(2,1)}, bf16[3,16,2,8,128]{4,3,2,1,0:T(8,128)(2,1)S(1)}, u32[]{:S(2)}, u32[]{:S(2)}) collective-permute-start(bf16[3,16,2,8,128]{4,3,2,1,0:T(8,128)(2,1)} %get-tuple-element.12), channel_id=1, source_target_pairs={{0,192},{192,384},{384,576},{576,0},{1,193},{193,385},{385,577},{5... | collective-permute-start | bytes 589832 | tf_op jit(solution)/shard_map/ppermute | solution.py:30
  13.4 12.8 %collective-permute-start.4 = (bf16[3,16,2,8,128]{4,3,2,1,0:T(8,128)(2,1)}, bf16[3,16,2,8,128]{4,3,2,1,0:T(8,128)(2,1)S(1)}, u32[]{:S(2)}, u32[]{:S(2)}) collective-permute-start(bf16[3,16,2,8,128]{4,3,2,1,0:T(8,128)(2,1)} %get-tuple-element.13), channel_id=1, source_target_pairs={{0,384},{192,576},{384,0},{576,192},{1,385},{193,577},{385,1},{577... | collective-permute-start | bytes 589832 | tf_op jit(solution)/shard_map/ppermute | solution.py:30
  26.2 2.2 %collective-permute-start.5 = (bf16[3,16,2,8,128]{4,3,2,1,0:T(8,128)(2,1)}, bf16[3,16,2,8,128]{4,3,2,1,0:T(8,128)(2,1)S(1)}, u32[]{:S(2)}, u32[]{:S(2)}) collective-permute-start(bf16[3,16,2,8,128]{4,3,2,1,0:T(8,128)(2,1)} %get-tuple-element.14), channel_id=1, source_target_pairs={{0,576},{192,0},{384,192},{576,384},{1,577},{193,1},{385,193},{577... | collective-permute-start | bytes 589832 | tf_op jit(solution)/shard_map/ppermute | solution.py:30
  28.4 0.0 copy-start
  28.4 2.2 %copy-done = bf16[512,4096]{1,0:T(8,128)(2,1)S(1)} copy-done((bf16[512,4096]{1,0:T(8,128)(2,1)S(1)}, bf16[512,4096]{1,0:T(8,128)(2,1)}, u32[]{:S(2)}) %copy-start) | copy-done | bytes 4194328
  30.6 1.9 %split.1 = (bf16[512,2048]{1,0:T(8,128)(2,1)S(1)}, bf16[512,2048]{1,0:T(8,128)(2,1)}) custom-call(s32[1]{0:T(128)} %bitcast.3.place_ref, bf16[512,4096]{1,0:T(8,128)(2,1)S(1)} %copy-done, bf16[512,4096]{1,0:T(8,128)(2,1)S(1)} %copy-done), custom_call_target="tpu_custom_call" | custom-call | bytes 8000000 | tf_op jit(solution)/shard_map/split/pallas_call | solution.py:259
  32.4 1.3 copy-done.2
  33.7 3.5 %collective-permute-start.7 = (bf16[512,2048]{1,0:T(8,128)(2,1)}, bf16[512,2048]{1,0:T(8,128)(2,1)S(1)}, u32[]{:S(2)}, u32[]{:S(2)}) collective-permute-start(bf16[512,2048]{1,0:T(8,128)(2,1)} %get-tuple-element.15), channel_id=1, source_target_pairs={{0,1},{1,0},{2,3},{3,2},{4,5},{5,4},{6,7},{7,6},{8,9},{9,8},{10,11... | collective-permute-start | bytes 6291464 | tf_op jit(solution)/shard_map/ppermute | solution.py:369
  37.3 13.6 %collective-permute-done.4 = bf16[3,16,2,8,128]{4,3,2,1,0:T(8,128)(2,1)S(1)} collective-permute-done((bf16[3,16,2,8,128]{4,3,2,1,0:T(8,128)(2,1)}, bf16[3,16,2,8,128]{4,3,2,1,0:T(8,128)(2,1)S(1)}, u32[]{:S(2)}, u32[]{:S(2)}) %collective-permute-start.4) | collective-permute-done | bytes 196640 | tf_op jit(solution)/shard_map/ppermute | solution.py:30
  50.9 0.8 add_convert_fusion
  51.7 13.1 %all-to-all-start = ((bf16[96,8,128]{2,1,0:T(8,128)(2,1)}), bf16[96,8,128]{2,1,0:T(8,128)(2,1)S(1)}, u32[]{:S(2)}, u32[]{:S(2)}) async-start(bf16[96,8,128]{2,1,0:T(8,128)(2,1)} %bitcast.5), calls=%async_computation | async-start | bytes 393216 | tf_op jit(solution)/shard_map/all_to_all | solution.py:367
  64.8 2.9 %pair.1.pairs_ref = bf16[4,256,256]{2,1,0:T(8,128)(2,1)} custom-call(bf16[256,2,256]{2,1,0:T(2,128)(2,1)} %keys_ref.3, bf16[256,2,256]{2,1,0:T(2,128)(2,1)} %values_ref.3), custom_call_target="tpu_custom_call" | custom-call | bytes 2000000 | tf_op jit(solution)/shard_map/pair/pallas_call | solution.py:139
  67.7 5.0 %collective-permute-start.1 = (bf16[4,256,256]{2,1,0:T(8,128)(2,1)}, bf16[4,256,256]{2,1,0:T(8,128)(2,1)}, u32[]{:S(2)}, u32[]{:S(2)}) collective-permute-start(bf16[4,256,256]{2,1,0:T(8,128)(2,1)} %pair.1.pairs_ref), channel_id=1, source_target_pairs={{0,4},{2,6},{4,8},{6,10},{8,12},{10,14},{12,16},{14,18},{16,20},{1... | collective-permute-start | bytes 1572872 | tf_op jit(solution)/shard_map/ppermute | solution.py:22
  72.7 0.7 constant_dynamic-slice_fusion.old_ref
  73.4 1.8 %all-to-all-done.blocks_ref = bf16[96,8,128]{2,1,0:T(8,128)(2,1)S(1)} async-done(((bf16[96,8,128]{2,1,0:T(8,128)(2,1)}), bf16[96,8,128]{2,1,0:T(8,128)(2,1)S(1)}, u32[]{:S(2)}, u32[]{:S(2)}) %all-to-all-start) | async-done | bytes 196640 | tf_op jit(solution)/shard_map/all_to_all | solution.py:367
  75.3 0.9 refresh.1
  76.2 8.6 %all-to-all-start.1 = ((bf16[96,4,256]{2,1,0:T(4,128)(2,1)}), bf16[96,4,256]{2,1,0:T(4,128)(2,1)}, u32[]{:S(2)}, u32[]{:S(2)}) async-start(bf16[96,4,256]{2,1,0:T(4,128)(2,1)} %refresh.1), calls=%async_computation.1 | async-start | bytes 393216 | tf_op jit(solution)/shard_map/all_to_all | solution.py:375
  84.8 3.4 %collective-permute-start = (bf16[4,256,256]{2,1,0:T(8,128)(2,1)}, bf16[4,256,256]{2,1,0:T(8,128)(2,1)}, u32[]{:S(2)}, u32[]{:S(2)}) collective-permute-start(bf16[4,256,256]{2,1,0:T(8,128)(2,1)} %pair.1.pairs_ref), channel_id=1, source_target_pairs={{0,2},{2,4},{4,6},{6,8},{8,10},{10,12},{12,14},{14,16},{16,18},{18... | collective-permute-start | bytes 1572872 | tf_op jit(solution)/shard_map/ppermute | solution.py:26
  88.2 1.3 collective-permute-start.2
  89.6 0.0 copy-start.1
  89.6 1.0 copy-done.1
  90.6 1.6 %own_attention.1.state_ref = f32[2,256,512]{2,1,0:T(8,128)S(1)} custom-call(s32[4]{0:T(128)S(1)} %copy-done.6, s32[384]{0:T(512)S(1)} %copy-done.5, bf16[256,2,256]{2,1,0:T(2,128)(2,1)S(1)} %copy-done.4, bf16[4,256,256]{2,1,0:T(8,128)(2,1)S(1)} %copy-done.1), custom_call_target="tpu_custom_call" | custom-call | flops 134217728 | bytes 3000000 | tf_op jit(solution)/shard_map/own_attention/pallas_call | solution.py:170
  92.2 2.7 %all-to-all-done.1 = bf16[96,4,256]{2,1,0:T(4,128)(2,1)} async-done(((bf16[96,4,256]{2,1,0:T(4,128)(2,1)}), bf16[96,4,256]{2,1,0:T(4,128)(2,1)}, u32[]{:S(2)}, u32[]{:S(2)}) %all-to-all-start.1) | async-done | bytes 196640 | tf_op jit(solution)/shard_map/all_to_all | solution.py:375
  94.9 1.7 %reshape.11 = bf16[384,256]{1,0:T(8,128)(2,1)} reshape(bf16[96,4,256]{2,1,0:T(4,128)(2,1)} %all-to-all-done.1) | data formatting | bytes 393216 | tf_op jit(solution)/shard_map/reshape | solution.py:378
  96.6 27.8 %all_gather.3.weights_ref = bf16[1536,256]{1,0:T(8,128)(2,1)S(1)} all-gather(bf16[384,256]{1,0:T(8,128)(2,1)} %reshape.11), channel_id=1, replica_groups=mesh['z'=4,'p'=96,'head'=2] {'z'}, dimensions={0}, use_global_device_ids=true | all-gather | bytes 983040 | tf_op jit(solution)/shard_map/all_gather | solution.py:378
  124.4 3.2 %features.1.own_ref = bf16[256,512]{1,0:T(8,128)(2,1)S(1)} custom-call(s32[4]{0:T(128)S(1)} %copy-done.6, s32[384]{0:T(512)S(1)} %copy-done.5, bf16[256,2,256]{2,1,0:T(2,128)(2,1)S(1)} %copy-done.4, bf16[4,256,256]{2,1,0:T(8,128)(2,1)} %collective-permute-done.near_ref, bf16[4,256,256]{2,1,0:T(8,128)(2,1)} %collective-permute-done.2.first_ref, ...), custom_call_target="tpu_custom_call" | custom-call | flops 469762048 | bytes 3000000 | tf_op jit(solution)/shard_map/features/pallas_call | solution.py:234
  127.6 7.4 %collective-permute-start.6 = (bf16[256,512]{1,0:T(8,128)(2,1)S(1)}, bf16[256,512]{1,0:T(8,128)(2,1)S(1)}, u32[]{:S(2)}, u32[]{:S(2)}) collective-permute-start(bf16[256,512]{1,0:T(8,128)(2,1)S(1)} %features.1.own_ref), channel_id=1, source_target_pairs={{0,1},{1,0},{2,3},{3,2},{4,5},{5,4},{6,7},{7,6},{8,9},{9,8},{10,11... | collective-permute-start | bytes 786440 | tf_op jit(solution)/shard_map/ppermute | solution.py:380
  135.1 0.7 own_project.1.own_ref
  135.8 0.4 collective-permute-done.6.other_ref
  136.2 2.0 %project.1 = bf16[256,2048]{1,0:T(8,128)(2,1)} custom-call(bf16[256,512]{1,0:T(8,128)(2,1)S(1)} %collective-permute-done.6.other_ref, bf16[512,2048]{1,0:T(8,128)(2,1)S(1)} %collective-permute-done.7.weight_ref, f32[256,2048]{1,0:T(8,128)S(1)} %own_project.1.own_ref), custom_call_target="tpu_custom_call" | custom-call | flops 536870912 | bytes 6000000 | tf_op jit(solution)/shard_map/project/pallas_call | solution.py:309
  (17 shorter events, 0.0 us)
Async XLA Ops:
  5.0 32.3 %collective-permute-start.3 = (bf16[3,16,2,8,128]{4,3,2,1,0:T(8,128)(2,1)}, bf16[3,16,2,8,128]{4,3,2,1,0:T(8,128)(2,1)S(1)}, u32[]{:S(2)}, u32[]{:S(2)}) collective-permute-start(bf16[3,16,2,8,128]{4,3,2,1,0:T(8,128)(2,1)} %get-tuple-element.12), channel_id=1, source_target_pairs={{0,192},{192,384},{384,576},{576,0},{1,193},{193,385},{385,577},{5... | collective-permute-start | bytes 589832 | tf_op jit(solution)/shard_map/ppermute | solution.py:30
  13.4 37.5 %collective-permute-start.4 = (bf16[3,16,2,8,128]{4,3,2,1,0:T(8,128)(2,1)}, bf16[3,16,2,8,128]{4,3,2,1,0:T(8,128)(2,1)S(1)}, u32[]{:S(2)}, u32[]{:S(2)}) collective-permute-start(bf16[3,16,2,8,128]{4,3,2,1,0:T(8,128)(2,1)} %get-tuple-element.13), channel_id=1, source_target_pairs={{0,384},{192,576},{384,0},{576,192},{1,385},{193,577},{385,1},{577... | collective-permute-start | bytes 589832 | tf_op jit(solution)/shard_map/ppermute | solution.py:30
  26.2 24.7 %collective-permute-start.5 = (bf16[3,16,2,8,128]{4,3,2,1,0:T(8,128)(2,1)}, bf16[3,16,2,8,128]{4,3,2,1,0:T(8,128)(2,1)S(1)}, u32[]{:S(2)}, u32[]{:S(2)}) collective-permute-start(bf16[3,16,2,8,128]{4,3,2,1,0:T(8,128)(2,1)} %get-tuple-element.14), channel_id=1, source_target_pairs={{0,576},{192,0},{384,192},{576,384},{1,577},{193,1},{385,193},{577... | collective-permute-start | bytes 589832 | tf_op jit(solution)/shard_map/ppermute | solution.py:30
  28.4 2.2 %copy-start = (bf16[512,4096]{1,0:T(8,128)(2,1)S(1)}, bf16[512,4096]{1,0:T(8,128)(2,1)}, u32[]{:S(2)}) copy-start(bf16[512,4096]{1,0:T(8,128)(2,1)} %theirs_in_ref.1) | copy-start | bytes 12582916
  30.6 20.3 %copy-start.7 = (bf16[3,16,2,8,128]{4,3,2,1,0:T(8,128)(2,1)S(1)}, bf16[3,16,2,8,128]{4,3,2,1,0:T(8,128)(2,1)}, u32[]{:S(2)}) copy-start(bf16[3,16,2,8,128]{4,3,2,1,0:T(8,128)(2,1)} %get-tuple-element.11) | copy-start | bytes 589828
  32.4 1.3 copy-start.2
  33.7 55.8 %copy-start.4 = (bf16[256,2,256]{2,1,0:T(2,128)(2,1)S(1)}, bf16[256,2,256]{2,1,0:T(2,128)(2,1)}, u32[]{:S(2)}) copy-start(bf16[256,2,256]{2,1,0:T(2,128)(2,1)} %queries_ref.3) | copy-start | bytes 786436
  33.7 55.8 %copy-start.5 = (s32[384]{0:T(512)S(1)}, s32[384]{0:T(512)}, u32[]{:S(2)}) copy-start(s32[384]{0:T(512)} %counts_ref.5) | copy-start | bytes 4612
  33.7 55.8 %copy-start.6 = (s32[4]{0:T(128)S(1)}, s32[4]{0:T(128)}, u32[]{:S(2)}) copy-start(s32[4]{0:T(128)} %pad_add_fusion.place_ref) | copy-start | bytes 52
  33.7 102.5 %collective-permute-start.7 = (bf16[512,2048]{1,0:T(8,128)(2,1)}, bf16[512,2048]{1,0:T(8,128)(2,1)S(1)}, u32[]{:S(2)}, u32[]{:S(2)}) collective-permute-start(bf16[512,2048]{1,0:T(8,128)(2,1)} %get-tuple-element.15), channel_id=1, source_target_pairs={{0,1},{1,0},{2,3},{3,2},{4,5},{5,4},{6,7},{7,6},{8,9},{9,8},{10,11... | collective-permute-start | bytes 6291464 | tf_op jit(solution)/shard_map/ppermute | solution.py:369
  51.7 23.6 %all-to-all-start = ((bf16[96,8,128]{2,1,0:T(8,128)(2,1)}), bf16[96,8,128]{2,1,0:T(8,128)(2,1)S(1)}, u32[]{:S(2)}, u32[]{:S(2)}) async-start(bf16[96,8,128]{2,1,0:T(8,128)(2,1)} %bitcast.5), calls=%async_computation | async-start | bytes 393216 | tf_op jit(solution)/shard_map/all_to_all | solution.py:367
  67.7 20.5 %collective-permute-start.1 = (bf16[4,256,256]{2,1,0:T(8,128)(2,1)}, bf16[4,256,256]{2,1,0:T(8,128)(2,1)}, u32[]{:S(2)}, u32[]{:S(2)}) collective-permute-start(bf16[4,256,256]{2,1,0:T(8,128)(2,1)} %pair.1.pairs_ref), channel_id=1, source_target_pairs={{0,4},{2,6},{4,8},{6,10},{8,12},{10,14},{12,16},{14,18},{16,20},{1... | collective-permute-start | bytes 1572872 | tf_op jit(solution)/shard_map/ppermute | solution.py:22
  76.2 18.7 %all-to-all-start.1 = ((bf16[96,4,256]{2,1,0:T(4,128)(2,1)}), bf16[96,4,256]{2,1,0:T(4,128)(2,1)}, u32[]{:S(2)}, u32[]{:S(2)}) async-start(bf16[96,4,256]{2,1,0:T(4,128)(2,1)} %refresh.1), calls=%async_computation.1 | async-start | bytes 393216 | tf_op jit(solution)/shard_map/all_to_all | solution.py:375
  84.8 39.6 %collective-permute-start = (bf16[4,256,256]{2,1,0:T(8,128)(2,1)}, bf16[4,256,256]{2,1,0:T(8,128)(2,1)}, u32[]{:S(2)}, u32[]{:S(2)}) collective-permute-start(bf16[4,256,256]{2,1,0:T(8,128)(2,1)} %pair.1.pairs_ref), channel_id=1, source_target_pairs={{0,2},{2,4},{4,6},{6,8},{8,10},{10,12},{12,14},{14,16},{16,18},{18... | collective-permute-start | bytes 1572872 | tf_op jit(solution)/shard_map/ppermute | solution.py:26
  88.2 36.2 %collective-permute-start.2 = (bf16[4,256,256]{2,1,0:T(8,128)(2,1)}, bf16[4,256,256]{2,1,0:T(8,128)(2,1)}, u32[]{:S(2)}, u32[]{:S(2)}) collective-permute-start(bf16[4,256,256]{2,1,0:T(8,128)(2,1)} %collective-permute-done.1.far_ref), channel_id=1, source_target_pairs={{2,0},{3,1},{194,192},{195,193},{386,384},{387,385},{578,576},{579... | collective-permute-start | bytes 1572872 | tf_op jit(solution)/shard_map/ppermute | solution.py:376
  89.6 1.0 copy-start.1
  124.4 10.7 %copy-start.3 = (bf16[512,2048]{1,0:T(8,128)(2,1)S(1)}, bf16[512,2048]{1,0:T(8,128)(2,1)}, u32[]{:S(2)}) copy-start(bf16[512,2048]{1,0:T(8,128)(2,1)} %copy-done.2) | copy-start | bytes 6291460
  127.6 8.6 %collective-permute-start.6 = (bf16[256,512]{1,0:T(8,128)(2,1)S(1)}, bf16[256,512]{1,0:T(8,128)(2,1)S(1)}, u32[]{:S(2)}, u32[]{:S(2)}) collective-permute-start(bf16[256,512]{1,0:T(8,128)(2,1)S(1)} %features.1.own_ref), channel_id=1, source_target_pairs={{0,1},{1,0},{2,3},{3,2},{4,5},{5,4},{6,7},{7,6},{8,9},{9,8},{10,11... | collective-permute-start | bytes 786440 | tf_op jit(solution)/shard_map/ppermute | solution.py:380

commit v4 on v3

v4 whole, which is shorter than its diff:
```python
import functools
import math

import jax
import jax.numpy as jnp
from jax import lax
from jax.experimental import pallas as pl
from jax.experimental.pallas import tpu as pltpu
from jax.sharding import Mesh, PartitionSpec as P


RING = 4
CTX = ("z", "p")
VMEM = pl.BlockSpec(memory_space=pltpu.VMEM)
SMEM = pl.BlockSpec(memory_space=pltpu.SMEM)
LOWEST = -1e30
VMEM_BYTES = 24 << 20


def passed_along(value, steps):
    count = lax.axis_size(CTX)
    return lax.ppermute(value, CTX, [(source, source + steps) for source in range(count - steps)])


def product(left, right, left_dim, right_dim):
    return lax.dot_general(
        left,
        right,
        (((left_dim,), (right_dim,)), ((), ())),
        preferred_element_type=jnp.float32,
    )


def place_count(counts_ref, place_ref, back_step):
    place = place_ref[0] - back_step
    return jnp.where(place >= 0, counts_ref[jnp.maximum(place, 0)], 0)


def gradient_kernel(
    place_ref, counts_ref, keys_ref, values_ref, rates_ref, weights_ref, grad_ref, pairs_ref
):
    tokens, heads, width = keys_ref.shape
    valid = lax.broadcasted_iota(jnp.int32, (tokens, 1), 0) < place_count(counts_ref, place_ref, 0)
    rates_all = jnp.concatenate(
        [rates_ref[...], jnp.zeros((8 - heads, tokens), jnp.float32)], 0
    ).T
    for head in range(heads):
        keys, values = keys_ref[:, head, :], values_ref[:, head, :]
        pairs_ref[head] = keys
        pairs_ref[heads + head] = values
        rates = jnp.where(valid, rates_all[:, head : head + 1], 0.0)
        scaled = (rates * values.astype(jnp.float32)).astype(jnp.bfloat16)
        gate_weight = weights_ref[head, 0].astype(jnp.bfloat16)
        up_weight = weights_ref[head, 1].astype(jnp.bfloat16)
        down_weight = weights_ref[head, 2].astype(jnp.bfloat16)
        gate_pre = product(keys, gate_weight, 1, 1)
        up_pre = product(keys, up_weight, 1, 1)
        back = -product(scaled, down_weight, 1, 0)
        sigmoid = jax.nn.sigmoid(gate_pre)
        gate_act = gate_pre * sigmoid
        hidden = (gate_act * up_pre).astype(jnp.bfloat16)
        slope = sigmoid * (1.0 + gate_pre * (1.0 - sigmoid))
        grad_gate = (back * up_pre * slope).astype(jnp.bfloat16)
        grad_up = (back * gate_act).astype(jnp.bfloat16)
        mats = (
            product(grad_gate, keys, 0, 0),
            product(grad_up, keys, 0, 0),
            -product(scaled, hidden, 0, 0),
        )
        for index, mat in enumerate(mats):
            first = (head * 3 + index) * width
            grad_ref[first : first + width, :] = mat.astype(jnp.bfloat16)


def local_gradient(place, counts, token_keys, token_values, step_rates, fast_weights):
    heads, mats, width, _ = fast_weights.shape
    return pl.pallas_call(
        gradient_kernel,
        out_shape=(
            jax.ShapeDtypeStruct((heads * mats * width, width), jnp.bfloat16),
            jax.ShapeDtypeStruct((2 * heads, token_keys.shape[0], width), jnp.bfloat16),
        ),
        in_specs=[SMEM, SMEM, VMEM, VMEM, VMEM, VMEM],
        out_specs=(VMEM, VMEM),
        name="gradient",
        cost_estimate=pl.CostEstimate(
            flops=14 * 256 * width * width * heads, transcendentals=131072, bytes_accessed=3000000
        ),
    )(place, counts, token_keys, token_values, step_rates.T, fast_weights)


def window_kernel(place_ref, counts_ref, queries_ref, own_ref, near_ref, far_ref, window_ref, turned_ref):
    tokens, heads, width = queries_ref.shape
    row = lax.broadcasted_iota(jnp.int32, (tokens, tokens), 0)
    column = lax.broadcasted_iota(jnp.int32, (tokens, tokens), 1)
    blocks = (
        (own_ref, (column <= row) & (column < place_count(counts_ref, place_ref, 0))),
        (near_ref, column < place_count(counts_ref, place_ref, 1)),
        (far_ref, (column > row) & (column < place_count(counts_ref, place_ref, 2))),
    )
    scale = 1.0 / math.sqrt(width)
    for head in range(heads):
        queries = queries_ref[:, head, :]
        turned_ref[head] = queries
        scores = [
            jnp.where(allowed, product(queries, block[head], 1, 1) * scale, LOWEST)
            for block, allowed in blocks
        ]
        top = jnp.max(functools.reduce(jnp.maximum, scores), axis=1, keepdims=True)
        expo = [jnp.exp(score - top) for score in scores]
        mass = jnp.sum(sum(expo), axis=1, keepdims=True)
        total = sum(
            product(part.astype(jnp.bfloat16), block[heads + head], 1, 0)
            for part, (block, _) in zip(expo, blocks)
        )
        window_ref[:, head * width : (head + 1) * width] = total / mass


def window_attention(place, counts, queries, own, near, far):
    tokens, heads, width = queries.shape
    return pl.pallas_call(
        window_kernel,
        out_shape=(
            jax.ShapeDtypeStruct((tokens, heads * width), jnp.float32),
            jax.ShapeDtypeStruct((heads, tokens, width), jnp.bfloat16),
        ),
        in_specs=[SMEM, SMEM] + [VMEM] * 4,
        out_specs=(VMEM, VMEM),
        name="window",
        compiler_params=pltpu.CompilerParams(vmem_limit_bytes=VMEM_BYTES),
        cost_estimate=pl.CostEstimate(
            flops=12 * tokens * tokens * width * heads,
            transcendentals=400000,
            bytes_accessed=3000000,
        ),
    )(place, counts, queries, own, near, far)


def feature_kernel(place_ref, counts_ref, queries_ref, window_ref, weights_ref, features_ref):
    heads, tokens, width = queries_ref.shape
    valid = lax.broadcasted_iota(jnp.int32, (tokens, 1), 0) < place_count(counts_ref, place_ref, 0)
    for head in range(heads):
        queries = queries_ref[head]
        first = head * 3 * width
        gate = product(queries, weights_ref[first : first + width, :], 1, 1)
        up = product(queries, weights_ref[first + width : first + 2 * width, :], 1, 1)
        hidden = (gate * jax.nn.sigmoid(gate) * up).astype(jnp.bfloat16)
        learned = product(hidden, weights_ref[first + 2 * width : first + 3 * width, :], 1, 1)
        columns = slice(head * width, (head + 1) * width)
        features_ref[:, columns] = jnp.where(
            valid, learned + window_ref[:, columns], 0.0
        ).astype(jnp.bfloat16)


def features_of(place, counts, queries, window, new_flat):
    heads, tokens, width = queries.shape
    return pl.pallas_call(
        feature_kernel,
        out_shape=jax.ShapeDtypeStruct((tokens, heads * width), jnp.bfloat16),
        in_specs=[SMEM, SMEM] + [VMEM] * 3,
        out_specs=VMEM,
        name="features",
        compiler_params=pltpu.CompilerParams(vmem_limit_bytes=VMEM_BYTES),
        cost_estimate=pl.CostEstimate(
            flops=6 * tokens * width * width * heads, transcendentals=131072, bytes_accessed=2000000
        ),
    )(place, counts, queries, window, new_flat)


def split_kernel(place_ref, mine_in_ref, theirs_in_ref, mine_ref, theirs_ref):
    mine_ref[...] = mine_in_ref[...]
    theirs_ref[...] = theirs_in_ref[...]


def column_halves(head_place, out_weight):
    depth, columns = out_weight.shape
    half = columns // 2
    tile = half // 2
    piece = jax.ShapeDtypeStruct((depth, half), out_weight.dtype)
    return pl.pallas_call(
        split_kernel,
        out_shape=(piece, piece),
        grid_spec=pltpu.PrefetchScalarGridSpec(
            num_scalar_prefetch=1,
            grid=(half // tile,),
            in_specs=[
                pl.BlockSpec((depth, tile), lambda step, place: (0, place[0] * 2 + step)),
                pl.BlockSpec((depth, tile), lambda step, place: (0, (1 - place[0]) * 2 + step)),
            ],
            out_specs=(
                pl.BlockSpec((depth, tile), lambda step, place: (0, step)),
                pl.BlockSpec((depth, tile), lambda step, place: (0, step)),
            ),
        ),
        name="split",
        compiler_params=pltpu.CompilerParams(vmem_limit_bytes=VMEM_BYTES),
        cost_estimate=pl.CostEstimate(flops=0, transcendentals=0, bytes_accessed=8000000),
    )(head_place, out_weight, out_weight)


def own_project_kernel(own_ref, weight_ref, out_ref):
    out_ref[...] = jnp.dot(own_ref[...], weight_ref[...], preferred_element_type=jnp.float32)


def own_projected(own, weight):
    return pl.pallas_call(
        own_project_kernel,
        out_shape=jax.ShapeDtypeStruct((own.shape[0], weight.shape[1]), jnp.float32),
        in_specs=[VMEM, VMEM],
        out_specs=VMEM,
        name="own_project",
        compiler_params=pltpu.CompilerParams(vmem_limit_bytes=VMEM_BYTES),
        cost_estimate=pl.CostEstimate(
            flops=2 * own.shape[0] * weight.size, transcendentals=0, bytes_accessed=4000000
        ),
    )(own, weight)


def project_kernel(other_ref, weight_ref, own_ref, out_ref):
    out_ref[...] = (
        own_ref[...]
        + jnp.dot(other_ref[...], weight_ref[...], preferred_element_type=jnp.float32)
    ).astype(jnp.bfloat16)


def projected(other, weight, own_product):
    tokens, depth = other.shape
    columns = weight.shape[1]
    tile = columns // 2
    return pl.pallas_call(
        project_kernel,
        out_shape=jax.ShapeDtypeStruct((tokens, columns), jnp.bfloat16),
        grid=(columns // tile,),
        in_specs=[
            pl.BlockSpec((tokens, depth), lambda step: (0, 0)),
            pl.BlockSpec((depth, tile), lambda step: (0, step)),
            pl.BlockSpec((tokens, tile), lambda step: (0, step)),
        ],
        out_specs=pl.BlockSpec((tokens, tile), lambda step: (0, step)),
        name="project",
        compiler_params=pltpu.CompilerParams(vmem_limit_bytes=VMEM_BYTES),
        cost_estimate=pl.CostEstimate(
            flops=2 * tokens * depth * columns, transcendentals=0, bytes_accessed=6000000
        ),
    )(other, weight, own_product)


def collect_kernel(blocks_ref, sums_ref):
    total = jnp.sum(blocks_ref[...].astype(jnp.float32), axis=0)
    sums_ref[...] = jnp.broadcast_to(total[None], sums_ref.shape)


def collected(copies, blocks):
    return pl.pallas_call(
        collect_kernel,
        out_shape=jax.ShapeDtypeStruct((copies, *blocks.shape[1:]), jnp.float32),
        in_specs=[VMEM],
        out_specs=VMEM,
        name="collect",
        compiler_params=pltpu.CompilerParams(vmem_limit_bytes=VMEM_BYTES),
        cost_estimate=pl.CostEstimate(flops=400000, transcendentals=0, bytes_accessed=800000),
    )(blocks)


def refresh_kernel(total, sums_ref, old_ref, rows_ref):
    gradient = jnp.sum(sums_ref[...], axis=0)
    old = old_ref[...]
    updated = old - gradient / math.sqrt(total)
    old_norm = jnp.sqrt(jnp.sum(old * old, axis=1, keepdims=True))
    fresh = updated * old_norm / jnp.sqrt(jnp.sum(updated * updated, axis=1, keepdims=True) + 1e-06)
    rows_ref[...] = jnp.broadcast_to(fresh.astype(jnp.bfloat16)[None], rows_ref.shape)


def refreshed(total, copies, sums, old_rows):
    return pl.pallas_call(
        functools.partial(refresh_kernel, total),
        out_shape=jax.ShapeDtypeStruct((copies, *old_rows.shape), jnp.bfloat16),
        in_specs=[VMEM, VMEM],
        out_specs=VMEM,
        name="refresh",
        compiler_params=pltpu.CompilerParams(vmem_limit_bytes=VMEM_BYTES),
        cost_estimate=pl.CostEstimate(flops=100000, transcendentals=0, bytes_accessed=1000000),
    )(sums, old_rows)


def shards(queries, token_keys, token_values, step_rates, counts, fast_weights, out_weight):
    tok_rows, _, head_width = queries.shape
    device_count, plane_count = lax.axis_size(CTX), lax.axis_size("p")
    plane_place, head_place = lax.axis_index("p"), lax.axis_index("head")
    place = lax.axis_index(CTX).reshape(1).astype(jnp.int32)
    local_grad, pairs = local_gradient(
        place, counts, token_keys, token_values, step_rates, fast_weights
    )
    near = passed_along(pairs, 1)
    blocks = lax.all_to_all(local_grad.reshape(plane_count, -1, head_width), "p", 0, 0, tiled=True)
    out_own, out_theirs = column_halves(
        head_place.reshape(1).astype(jnp.int32), out_weight
    )
    out_other = lax.ppermute(out_theirs, "head", [(0, 1), (1, 0)])
    sums = collected(RING, blocks)
    sums = lax.all_to_all(sums, "z", 0, 0, tiled=True)
    far = passed_along(pairs, 2)
    old_flat = fast_weights.reshape(-1, head_width)
    own_rows = old_flat.shape[0] // plane_count
    old_rows = lax.dynamic_slice_in_dim(old_flat, plane_place * own_rows, own_rows, 0)
    new_rows = refreshed(tok_rows * device_count, plane_count, sums, old_rows)
    new_flat = lax.all_to_all(new_rows, "p", 0, 0, tiled=True).reshape(-1, head_width)
    window, turned_queries = window_attention(place, counts, queries, pairs, near, far)
    features = features_of(place, counts, turned_queries, window, new_flat)
    other = lax.ppermute(features, "head", [(0, 1), (1, 0)])
    own_product = own_projected(features, out_own)
    return projected(other, out_other, own_product)


def solution(mesh):
    fine = Mesh(mesh.devices.reshape(RING, -1, 2), ("z", "p", "head"))
    in_specs = (
        P(CTX, "head", None),
        P(CTX, "head", None),
        P(CTX, "head", None),
        P(CTX, "head"),
        P(),
        P("head", None, None, None),
        P("head", None),
    )
    return jax.shard_map(
        shards, mesh=fine, in_specs=in_specs, out_specs=P(CTX, "head"), check_vma=False
    )
```

time: 139 us -> 139 us (level)
  the two profiles are of different devices: /device:TPU:1 before, /device:TPU:27 now
where the time goes in v4:
time: 139 us; the launch traced here: 138 us
  waiting for transfers between devices  43.5 us (31%)
  starting transfers between devices  38.8 us (28%)
  blocking collectives  34 us (24%)
  Pallas kernels  14.4 us (10%)
  local copies, waits for them, and re-layouts  7.47 us (5%)
    ppermute x2, waiting for transfers between devices, passed_along(): lax.ppermute(value, CTX, [(source, source + steps) for source in range(co...  34.8 us
    all_to_all x1, blocking collectives, shards(): lax.all_to_all(local_grad.reshape(plane_count, -1, head_width), 'p', 0, 0...  34 us
    all_to_all x1, starting transfers between devices, shards(): sums = lax.all_to_all(sums, 'z', 0, 0, tiled=True)  12.9 us
    all_to_all x1, starting transfers between devices, shards(): lax.all_to_all(new_rows, 'p', 0, 0, tiled=True).reshape(-1, head_width)  10.2 us
    all_to_all x1, waiting for transfers between devices, shards(): sums = lax.all_to_all(sums, 'z', 0, 0, tiled=True)  8.64 us
    ppermute x2, starting transfers between devices, passed_along(): lax.ppermute(value, CTX, [(source, source + steps) for source in range(co...  8 us
    unnamed x16, local copies, waits for them, and re-layouts  6.75 us
    ppermute x1, starting transfers between devices, shards(): out_other = lax.ppermute(out_theirs, 'head', [(0, 1), (1, 0)])  4.98 us
  transfers between devices with their start and end apart: 6, of which 3 were waited for; matrix products, arithmetic and copies ran while one was open for 1% of the time, Pallas kernels for 4%

profile of v4, /device:TPU:27, one launch (start us, length us, event | category | flops | bytes accessed | tf_op | source)
XLA Modules:
  0.0 138.2 jit_solution(15822814800147482811)
XLA Ops:
  0.0 4.9 %gradient.1 = (bf16[1536,256]{1,0:T(8,128)(2,1)}, bf16[4,256,256]{2,1,0:T(8,128)(2,1)}) custom-call(s32[1]{0:T(128)} %bitcast.place_ref, s32[384]{0:T(512)} %counts_ref.5, bf16[256,2,256]{2,1,0:T(2,128)(2,1)} %keys_ref.1, bf16[256,2,256]{2,1,0:T(2,128)(2,1)} %values_ref.1, f32[2,256]{1,0:T(2,128)} %bitcast.9, f32[2,3,256,256]{3,2,1,0:T(8,128)} %weights_ref.1), custom_call_target="tpu_custom_call" | custom-call | flops 469762048 | bytes 3000000 | tf_op jit(solution)/shard_map/gradient/pallas_call | solution.py:77
  4.9 34.0 %all_to_all.15.blocks_ref = bf16[96,16,256]{2,1,0:T(8,128)(2,1)S(1)} all-to-all(bf16[96,16,256]{2,1,0:T(8,128)(2,1)} %bitcast.8), channel_id=1, replica_groups=mesh['z'=4,'p'=96,'head'=2] {'p'}, dimensions={0} | all-to-all | bytes 1572864 | tf_op jit(solution)/shard_map/all_to_all | solution.py:295
  38.9 0.8 collect.1
  39.6 12.9 %all-to-all-start.1 = ((f32[4,16,256]{2,1,0:T(8,128)}), f32[4,16,256]{2,1,0:T(8,128)S(1)}, u32[]{:S(2)}, u32[]{:S(2)}) async-start(f32[4,16,256]{2,1,0:T(8,128)} %collect.1), calls=%async_computation.1 | async-start | bytes 131072 | tf_op jit(solution)/shard_map/all_to_all | solution.py:301
  52.5 0.7 constant_dynamic-slice_fusion.old_ref
  53.2 8.6 %all-to-all-done.1.sums_ref = f32[4,16,256]{2,1,0:T(8,128)S(1)} async-done(((f32[4,16,256]{2,1,0:T(8,128)}), f32[4,16,256]{2,1,0:T(8,128)S(1)}, u32[]{:S(2)}, u32[]{:S(2)}) %all-to-all-start.1) | async-done | bytes 65568 | tf_op jit(solution)/shard_map/all_to_all | solution.py:301
  61.9 1.0 refresh.1
  62.9 10.2 %all-to-all-start.2 = ((bf16[96,16,256]{2,1,0:T(8,128)(2,1)}), bf16[96,16,256]{2,1,0:T(8,128)(2,1)S(1)}, u32[]{:S(2)}, u32[]{:S(2)}) async-start(bf16[96,16,256]{2,1,0:T(8,128)(2,1)} %refresh.1), calls=%async_computation.2 | async-start | bytes 1572864 | tf_op jit(solution)/shard_map/all_to_all | solution.py:307
  73.2 0.0 copy-start
  73.2 2.2 %copy-done = bf16[512,4096]{1,0:T(8,128)(2,1)S(1)} copy-done((bf16[512,4096]{1,0:T(8,128)(2,1)S(1)}, bf16[512,4096]{1,0:T(8,128)(2,1)}, u32[]{:S(2)}) %copy-start) | copy-done | bytes 4194328
  75.4 1.8 %split.1 = (bf16[512,2048]{1,0:T(8,128)(2,1)S(1)}, bf16[512,2048]{1,0:T(8,128)(2,1)}) custom-call(s32[1]{0:T(128)} %bitcast.5.place_ref, bf16[512,4096]{1,0:T(8,128)(2,1)S(1)} %copy-done, bf16[512,4096]{1,0:T(8,128)(2,1)S(1)} %copy-done), custom_call_target="tpu_custom_call" | custom-call | bytes 8000000 | tf_op jit(solution)/shard_map/split/pallas_call | solution.py:180
  77.2 1.3 copy-done.1
  78.5 5.0 %collective-permute-start.3 = (bf16[512,2048]{1,0:T(8,128)(2,1)}, bf16[512,2048]{1,0:T(8,128)(2,1)S(1)}, u32[]{:S(2)}, u32[]{:S(2)}) collective-permute-start(bf16[512,2048]{1,0:T(8,128)(2,1)} %get-tuple-element.15), channel_id=1, source_target_pairs={{0,1},{1,0},{2,3},{3,2},{4,5},{5,4},{6,7},{7,6},{8,9},{9,8},{10,11... | collective-permute-start | bytes 6291464 | tf_op jit(solution)/shard_map/ppermute | solution.py:299
  83.5 0.0 copy-done.3
  83.5 3.1 %collective-permute-start = (bf16[4,256,256]{2,1,0:T(8,128)(2,1)S(1)}, bf16[4,256,256]{2,1,0:T(8,128)(2,1)S(1)}, u32[]{:S(2)}, u32[]{:S(2)}) collective-permute-start(bf16[4,256,256]{2,1,0:T(8,128)(2,1)S(1)} %copy-done.3), channel_id=1, source_target_pairs={{0,2},{2,4},{4,6},{6,8},{8,10},{10,12},{12,14},{14,16},{16,18},{18... | collective-permute-start | bytes 1572872 | tf_op jit(solution)/shard_map/ppermute | solution.py:22
  86.6 4.9 %collective-permute-start.1 = (bf16[4,256,256]{2,1,0:T(8,128)(2,1)S(1)}, bf16[4,256,256]{2,1,0:T(8,128)(2,1)S(1)}, u32[]{:S(2)}, u32[]{:S(2)}) collective-permute-start(bf16[4,256,256]{2,1,0:T(8,128)(2,1)S(1)} %copy-done.3), channel_id=1, source_target_pairs={{0,4},{2,6},{4,8},{6,10},{8,12},{10,14},{12,16},{14,18},{16,20},{1... | collective-permute-start | bytes 1572872 | tf_op jit(solution)/shard_map/ppermute | solution.py:22
  91.5 9.0 %collective-permute-done.near_ref = bf16[4,256,256]{2,1,0:T(8,128)(2,1)S(1)} collective-permute-done((bf16[4,256,256]{2,1,0:T(8,128)(2,1)S(1)}, bf16[4,256,256]{2,1,0:T(8,128)(2,1)S(1)}, u32[]{:S(2)}, u32[]{:S(2)}) %collective-permute-start) | collective-permute-done | bytes 524320 | tf_op jit(solution)/shard_map/ppermute | solution.py:22
  100.5 25.9 %collective-permute-done.1.far_ref = bf16[4,256,256]{2,1,0:T(8,128)(2,1)S(1)} collective-permute-done((bf16[4,256,256]{2,1,0:T(8,128)(2,1)S(1)}, bf16[4,256,256]{2,1,0:T(8,128)(2,1)S(1)}, u32[]{:S(2)}, u32[]{:S(2)}) %collective-permute-start.1) | collective-permute-done | bytes 524320 | tf_op jit(solution)/shard_map/ppermute | solution.py:22
  126.4 0.0 copy-done.4
  126.4 0.0 copy-done.7
  126.4 2.1 %window.1 = (f32[256,512]{1,0:T(8,128)S(1)}, bf16[2,256,256]{2,1,0:T(8,128)(2,1)S(1)}) custom-call(s32[1]{0:T(128)} %bitcast.place_ref, s32[384]{0:T(512)S(1)} %copy-done.7, bf16[256,2,256]{2,1,0:T(2,128)(2,1)S(1)} %copy-done.4, bf16[4,256,256]{2,1,0:T(8,128)(2,1)S(1)} %copy-done.3, bf16[4,256,256]{2,1,0:T(8,128)(2,1)S(1)} %collective-permute-done.near_ref, ...), custom_call_target="tpu_custom_call" | custom-call | flops 402653184 | bytes 3000000 | tf_op jit(solution)/shard_map/window/pallas_call | solution.py:121
  128.4 0.0 copy-start.5
  128.5 0.7 copy-done.5
  129.2 0.0 all-to-all-done.2
  129.2 0.9 copy-done.6
  130.1 1.1 features.1.own_ref
  131.3 2.7 %collective-permute-start.2 = (bf16[256,512]{1,0:T(8,128)(2,1)S(1)}, bf16[256,512]{1,0:T(8,128)(2,1)S(1)}, u32[]{:S(2)}, u32[]{:S(2)}) collective-permute-start(bf16[256,512]{1,0:T(8,128)(2,1)S(1)} %features.1.own_ref), channel_id=1, source_target_pairs={{0,1},{1,0},{2,3},{3,2},{4,5},{5,4},{6,7},{7,6},{8,9},{9,8},{10,11... | collective-permute-start | bytes 786440 | tf_op jit(solution)/shard_map/ppermute | solution.py:310
  133.9 1.6 %copy-done.2 = bf16[512,2048]{1,0:T(8,128)(2,1)S(1)} copy-done((bf16[512,2048]{1,0:T(8,128)(2,1)S(1)}, bf16[512,2048]{1,0:T(8,128)(2,1)}, u32[]{:S(2)}) %copy-start.2) | copy-done | bytes 2097176
  135.5 0.7 own_project.1.own_ref
  136.2 0.0 collective-permute-done.3.weight_ref
  136.2 0.0 collective-permute-done.2.other_ref
  136.3 2.0 %project.1 = bf16[256,2048]{1,0:T(8,128)(2,1)} custom-call(bf16[256,512]{1,0:T(8,128)(2,1)S(1)} %collective-permute-done.2.other_ref, bf16[512,2048]{1,0:T(8,128)(2,1)S(1)} %collective-permute-done.3.weight_ref, f32[256,2048]{1,0:T(8,128)S(1)} %own_project.1.own_ref), custom_call_target="tpu_custom_call" | custom-call | flops 536870912 | bytes 6000000 | tf_op jit(solution)/shard_map/project/pallas_call | solution.py:230
  (6 shorter events, 0.0 us)
Async XLA Ops:
  39.6 22.2 %all-to-all-start.1 = ((f32[4,16,256]{2,1,0:T(8,128)}), f32[4,16,256]{2,1,0:T(8,128)S(1)}, u32[]{:S(2)}, u32[]{:S(2)}) async-start(f32[4,16,256]{2,1,0:T(8,128)} %collect.1), calls=%async_computation.1 | async-start | bytes 131072 | tf_op jit(solution)/shard_map/all_to_all | solution.py:301
  62.9 66.2 %all-to-all-start.2 = ((bf16[96,16,256]{2,1,0:T(8,128)(2,1)}), bf16[96,16,256]{2,1,0:T(8,128)(2,1)S(1)}, u32[]{:S(2)}, u32[]{:S(2)}) async-start(bf16[96,16,256]{2,1,0:T(8,128)(2,1)} %refresh.1), calls=%async_computation.2 | async-start | bytes 1572864 | tf_op jit(solution)/shard_map/all_to_all | solution.py:307
  73.2 2.2 %copy-start = (bf16[512,4096]{1,0:T(8,128)(2,1)S(1)}, bf16[512,4096]{1,0:T(8,128)(2,1)}, u32[]{:S(2)}) copy-start(bf16[512,4096]{1,0:T(8,128)(2,1)} %theirs_in_ref.1) | copy-start | bytes 12582916
  75.4 8.2 %copy-start.3 = (bf16[4,256,256]{2,1,0:T(8,128)(2,1)S(1)}, bf16[4,256,256]{2,1,0:T(8,128)(2,1)}, u32[]{:S(2)}) copy-start(bf16[4,256,256]{2,1,0:T(8,128)(2,1)} %get-tuple-element.11.own_ref) | copy-start | bytes 1572868
  75.4 51.0 %copy-start.4 = (bf16[256,2,256]{2,1,0:T(2,128)(2,1)S(1)}, bf16[256,2,256]{2,1,0:T(2,128)(2,1)}, u32[]{:S(2)}) copy-start(bf16[256,2,256]{2,1,0:T(2,128)(2,1)} %queries_ref.1) | copy-start | bytes 786436
  75.4 51.0 %copy-start.7 = (s32[384]{0:T(512)S(1)}, s32[384]{0:T(512)}, u32[]{:S(2)}) copy-start(s32[384]{0:T(512)} %counts_ref.5) | copy-start | bytes 4612
  77.2 1.3 copy-start.1
  78.5 57.7 %collective-permute-start.3 = (bf16[512,2048]{1,0:T(8,128)(2,1)}, bf16[512,2048]{1,0:T(8,128)(2,1)S(1)}, u32[]{:S(2)}, u32[]{:S(2)}) collective-permute-start(bf16[512,2048]{1,0:T(8,128)(2,1)} %get-tuple-element.15), channel_id=1, source_target_pairs={{0,1},{1,0},{2,3},{3,2},{4,5},{5,4},{6,7},{7,6},{8,9},{9,8},{10,11... | collective-permute-start | bytes 6291464 | tf_op jit(solution)/shard_map/ppermute | solution.py:299
  83.5 17.0 %collective-permute-start = (bf16[4,256,256]{2,1,0:T(8,128)(2,1)S(1)}, bf16[4,256,256]{2,1,0:T(8,128)(2,1)S(1)}, u32[]{:S(2)}, u32[]{:S(2)}) collective-permute-start(bf16[4,256,256]{2,1,0:T(8,128)(2,1)S(1)} %copy-done.3), channel_id=1, source_target_pairs={{0,2},{2,4},{4,6},{6,8},{8,10},{10,12},{12,14},{14,16},{16,18},{18... | collective-permute-start | bytes 1572872 | tf_op jit(solution)/shard_map/ppermute | solution.py:22
  86.6 39.8 %collective-permute-start.1 = (bf16[4,256,256]{2,1,0:T(8,128)(2,1)S(1)}, bf16[4,256,256]{2,1,0:T(8,128)(2,1)S(1)}, u32[]{:S(2)}, u32[]{:S(2)}) collective-permute-start(bf16[4,256,256]{2,1,0:T(8,128)(2,1)S(1)} %copy-done.3), channel_id=1, source_target_pairs={{0,4},{2,6},{4,8},{6,10},{8,12},{10,14},{12,16},{14,18},{16,20},{1... | collective-permute-start | bytes 1572872 | tf_op jit(solution)/shard_map/ppermute | solution.py:22
  128.4 0.7 copy-start.5
  129.2 1.0 copy-start.6
  131.3 5.0 %collective-permute-start.2 = (bf16[256,512]{1,0:T(8,128)(2,1)S(1)}, bf16[256,512]{1,0:T(8,128)(2,1)S(1)}, u32[]{:S(2)}, u32[]{:S(2)}) collective-permute-start(bf16[256,512]{1,0:T(8,128)(2,1)S(1)} %features.1.own_ref), channel_id=1, source_target_pairs={{0,1},{1,0},{2,3},{3,2},{4,5},{5,4},{6,7},{7,6},{8,9},{9,8},{10,11... | collective-permute-start | bytes 786440 | tf_op jit(solution)/shard_map/ppermute | solution.py:310
  133.9 1.6 %copy-start.2 = (bf16[512,2048]{1,0:T(8,128)(2,1)S(1)}, bf16[512,2048]{1,0:T(8,128)(2,1)}, u32[]{:S(2)}) copy-start(bf16[512,2048]{1,0:T(8,128)(2,1)} %copy-done.1) | copy-start | bytes 6291460

commit v5 on v4

--- a/solution.py
+++ b/solution.py
@@ -40,19 +40,22 @@
     place_ref, counts_ref, keys_ref, values_ref, rates_ref, weights_ref, grad_ref, pairs_ref
 ):
     tokens, heads, width = keys_ref.shape
-    valid = lax.broadcasted_iota(jnp.int32, (tokens, 1), 0) < place_count(counts_ref, place_ref, 0)
-    rates_all = jnp.concatenate(
-        [rates_ref[...], jnp.zeros((8 - heads, tokens), jnp.float32)], 0
-    ).T
-    for head in range(heads):
+
+    def one_head(head):
+        valid = lax.broadcasted_iota(jnp.int32, (tokens, 1), 0) < place_count(
+            counts_ref, place_ref, 0
+        )
+        rates_all = jnp.concatenate(
+            [rates_ref[...], jnp.zeros((8 - heads, tokens), jnp.float32)], 0
+        ).T
         keys, values = keys_ref[:, head, :], values_ref[:, head, :]
-        pairs_ref[head] = keys
-        pairs_ref[heads + head] = values
+        pairs_ref[0, 0] = keys
+        pairs_ref[1, 0] = values
         rates = jnp.where(valid, rates_all[:, head : head + 1], 0.0)
         scaled = (rates * values.astype(jnp.float32)).astype(jnp.bfloat16)
-        gate_weight = weights_ref[head, 0].astype(jnp.bfloat16)
-        up_weight = weights_ref[head, 1].astype(jnp.bfloat16)
-        down_weight = weights_ref[head, 2].astype(jnp.bfloat16)
+        gate_weight = weights_ref[0, 0].astype(jnp.bfloat16)
+        up_weight = weights_ref[0, 1].astype(jnp.bfloat16)
+        down_weight = weights_ref[0, 2].astype(jnp.bfloat16)
         gate_pre = product(keys, gate_weight, 1, 1)
         up_pre = product(keys, up_weight, 1, 1)
         back = -product(scaled, down_weight, 1, 0)
@@ -68,20 +71,35 @@
             -product(scaled, hidden, 0, 0),
         )
         for index, mat in enumerate(mats):
-            first = (head * 3 + index) * width
-            grad_ref[first : first + width, :] = mat.astype(jnp.bfloat16)
+            grad_ref[index * width : (index + 1) * width, :] = mat.astype(jnp.bfloat16)
+
+    for head in range(heads):
+        pl.when(pl.program_id(0) == head)(functools.partial(one_head, head))
 
 
 def local_gradient(place, counts, token_keys, token_values, step_rates, fast_weights):
     heads, mats, width, _ = fast_weights.shape
+    tokens = token_keys.shape[0]
+    raw = pl.BlockSpec((tokens, heads, width), lambda head: (0, 0, 0))
     return pl.pallas_call(
         gradient_kernel,
         out_shape=(
             jax.ShapeDtypeStruct((heads * mats * width, width), jnp.bfloat16),
-            jax.ShapeDtypeStruct((2 * heads, token_keys.shape[0], width), jnp.bfloat16),
-        ),
-        in_specs=[SMEM, SMEM, VMEM, VMEM, VMEM, VMEM],
-        out_specs=(VMEM, VMEM),
+            jax.ShapeDtypeStruct((2, heads, tokens, width), jnp.bfloat16),
+        ),
+        grid=(heads,),
+        in_specs=[
+            SMEM,
+            SMEM,
+            raw,
+            raw,
+            pl.BlockSpec((heads, tokens), lambda head: (0, 0)),
+            pl.BlockSpec((1, mats, width, width), lambda head: (head, 0, 0, 0)),
+        ],
+        out_specs=(
+            pl.BlockSpec((mats * width, width), lambda head: (head, 0)),
+            pl.BlockSpec((2, 1, tokens, width), lambda head: (0, head, 0, 0)),
+        ),
         name="gradient",
         cost_estimate=pl.CostEstimate(
             flops=14 * 256 * width * width * heads, transcendentals=131072, bytes_accessed=3000000
@@ -103,14 +121,14 @@
         queries = queries_ref[:, head, :]
         turned_ref[head] = queries
         scores = [
-            jnp.where(allowed, product(queries, block[head], 1, 1) * scale, LOWEST)
+            jnp.where(allowed, product(queries, block[0, head], 1, 1) * scale, LOWEST)
             for block, allowed in blocks
         ]
         top = jnp.max(functools.reduce(jnp.maximum, scores), axis=1, keepdims=True)
         expo = [jnp.exp(score - top) for score in scores]
         mass = jnp.sum(sum(expo), axis=1, keepdims=True)
         total = sum(
-            product(part.astype(jnp.bfloat16), block[heads + head], 1, 0)
+            product(part.astype(jnp.bfloat16), block[1, head], 1, 0)
             for part, (block, _) in zip(expo, blocks)
         )
         window_ref[:, head * width : (head + 1) * width] = total / mass
@@ -136,19 +154,55 @@
     )(place, counts, queries, own, near, far)
 
 
-def feature_kernel(place_ref, counts_ref, queries_ref, window_ref, weights_ref, features_ref):
-    heads, tokens, width = queries_ref.shape
+def feature_kernel(
+    place_ref,
+    counts_ref,
+    queries_ref,
+    window_ref,
+    weights_ref,
+    features_ref,
+    held_queries,
+    held_window,
+    held_weights,
+    sems,
+):
+    heads, tokens, width = held_queries.shape
+    mats = 3
+    fetches = []
+    for head in range(heads):
+        fetches.append(
+            pltpu.make_async_copy(
+                queries_ref.at[head], held_queries.at[head], sems.at[len(fetches)]
+            )
+        )
+        for index in range(mats):
+            rows = pl.ds((head * mats + index) * width, width)
+            fetches.append(
+                pltpu.make_async_copy(
+                    weights_ref.at[rows], held_weights.at[rows], sems.at[len(fetches)]
+                )
+            )
+    fetches.append(pltpu.make_async_copy(window_ref, held_window, sems.at[len(fetches)]))
+    for fetch in fetches:
+        fetch.start()
     valid = lax.broadcasted_iota(jnp.int32, (tokens, 1), 0) < place_count(counts_ref, place_ref, 0)
+    learned = []
     for head in range(heads):
-        queries = queries_ref[head]
-        first = head * 3 * width
-        gate = product(queries, weights_ref[first : first + width, :], 1, 1)
-        up = product(queries, weights_ref[first + width : first + 2 * width, :], 1, 1)
+        for fetch in fetches[head * (mats + 1) : (head + 1) * (mats + 1)]:
+            fetch.wait()
+        queries = held_queries[head]
+        first = head * mats * width
+        gate = product(queries, held_weights[first : first + width, :], 1, 1)
+        up = product(queries, held_weights[first + width : first + 2 * width, :], 1, 1)
         hidden = (gate * jax.nn.sigmoid(gate) * up).astype(jnp.bfloat16)
-        learned = product(hidden, weights_ref[first + 2 * width : first + 3 * width, :], 1, 1)
+        learned.append(
+            product(hidden, held_weights[first + 2 * width : first + 3 * width, :], 1, 1)
+        )
+    fetches[-1].wait()
+    for head in range(heads):
         columns = slice(head * width, (head + 1) * width)
         features_ref[:, columns] = jnp.where(
-            valid, learned + window_ref[:, columns], 0.0
+            valid, learned[head] + held_window[:, columns], 0.0
         ).astype(jnp.bfloat16)
 
 
@@ -157,10 +211,15 @@
     return pl.pallas_call(
         feature_kernel,
         out_shape=jax.ShapeDtypeStruct((tokens, heads * width), jnp.bfloat16),
-        in_specs=[SMEM, SMEM] + [VMEM] * 3,
+        in_specs=[SMEM, SMEM] + [pl.BlockSpec(memory_space=pl.ANY)] * 3,
         out_specs=VMEM,
+        scratch_shapes=[
+            pltpu.VMEM(queries.shape, jnp.bfloat16),
+            pltpu.VMEM(window.shape, jnp.float32),
+            pltpu.VMEM(new_flat.shape, jnp.bfloat16),
+            pltpu.SemaphoreType.DMA((4 * heads + 1,)),
+        ],
         name="features",
-        compiler_params=pltpu.CompilerParams(vmem_limit_bytes=VMEM_BYTES),
         cost_estimate=pl.CostEstimate(
             flops=6 * tokens * width * width * heads, transcendentals=131072, bytes_accessed=2000000
         ),
@@ -216,27 +275,48 @@
     )(own, weight)
 
 
-def project_kernel(other_ref, weight_ref, own_ref, out_ref):
-    out_ref[...] = (
-        own_ref[...]
-        + jnp.dot(other_ref[...], weight_ref[...], preferred_element_type=jnp.float32)
-    ).astype(jnp.bfloat16)
+def project_kernel(other_ref, weight_ref, own_ref, out_ref, held_weight, held_out, sems):
+    tiles = held_out.shape[0]
+    tile = held_out.shape[2]
+    fetches = [
+        pltpu.make_async_copy(
+            weight_ref.at[:, step * tile : (step + 1) * tile], held_weight.at[step], sems.at[0, step]
+        )
+        for step in range(tiles)
+    ]
+    for fetch in fetches:
+        fetch.start()
+    stores = []
+    for step in range(tiles):
+        columns = slice(step * tile, (step + 1) * tile)
+        fetches[step].wait()
+        held_out[step] = (
+            own_ref[:, columns]
+            + jnp.dot(other_ref[...], held_weight[step], preferred_element_type=jnp.float32)
+        ).astype(jnp.bfloat16)
+        stores.append(
+            pltpu.make_async_copy(held_out.at[step], out_ref.at[:, columns], sems.at[1, step])
+        )
+        stores[step].start()
+    for store in stores:
+        store.wait()
 
 
 def projected(other, weight, own_product):
     tokens, depth = other.shape
     columns = weight.shape[1]
-    tile = columns // 2
+    tiles = 4
+    tile = columns // tiles
     return pl.pallas_call(
         project_kernel,
         out_shape=jax.ShapeDtypeStruct((tokens, columns), jnp.bfloat16),
-        grid=(columns // tile,),
-        in_specs=[
-            pl.BlockSpec((tokens, depth), lambda step: (0, 0)),
-            pl.BlockSpec((depth, tile), lambda step: (0, step)),
-            pl.BlockSpec((tokens, tile), lambda step: (0, step)),
+        in_specs=[VMEM, pl.BlockSpec(memory_space=pl.ANY), VMEM],
+        out_specs=pl.BlockSpec(memory_space=pl.ANY),
+        scratch_shapes=[
+            pltpu.VMEM((tiles, depth, tile), jnp.bfloat16),
+            pltpu.VMEM((tiles, tokens, tile), jnp.bfloat16),
+            pltpu.SemaphoreType.DMA((2, tiles)),
         ],
-        out_specs=pl.BlockSpec((tokens, tile), lambda step: (0, step)),
         name="project",
         compiler_params=pltpu.CompilerParams(vmem_limit_bytes=VMEM_BYTES),
         cost_estimate=pl.CostEstimate(
@@ -299,7 +379,7 @@
     out_other = lax.ppermute(out_theirs, "head", [(0, 1), (1, 0)])
     sums = collected(RING, blocks)
     sums = lax.all_to_all(sums, "z", 0, 0, tiled=True)
-    far = passed_along(pairs, 2)
+    far = passed_along(near, 1)
     old_flat = fast_weights.reshape(-1, head_width)
     own_rows = old_flat.shape[0] // plane_count
     old_rows = lax.dynamic_slice_in_dim(old_flat, plane_place * own_rows, own_rows, 0)

time: 139 us -> 142 us (1.022)
  the two profiles are of different devices: /device:TPU:27 before, /device:TPU:65 now
where the time goes in v5:
time: 142 us; the launch traced here: 141 us
  waiting for transfers between devices  44.2 us (31%)
  blocking collectives  35.9 us (25%)
  starting transfers between devices  34.6 us (24%)
  Pallas kernels  17 us (12%)
  local copies, waits for them, and re-layouts  9.12 us (6%)
    all_to_all x1, blocking collectives, shards(): lax.all_to_all(local_grad.reshape(plane_count, -1, head_width), 'p', 0, 0...  35.9 us
    ppermute x2, waiting for transfers between devices, passed_along(): lax.ppermute(value, CTX, [(source, source + steps) for source in range(co...  35.7 us
    all_to_all x1, starting transfers between devices, shards(): sums = lax.all_to_all(sums, 'z', 0, 0, tiled=True)  12.2 us
    all_to_all x1, starting transfers between devices, shards(): lax.all_to_all(new_rows, 'p', 0, 0, tiled=True).reshape(-1, head_width)  8.67 us
    all_to_all x1, waiting for transfers between devices, shards(): sums = lax.all_to_all(sums, 'z', 0, 0, tiled=True)  8.56 us
    unnamed x20, local copies, waits for them, and re-layouts  8.4 us
    ppermute x2, starting transfers between devices, passed_along(): lax.ppermute(value, CTX, [(source, source + steps) for source in range(co...  5.01 us
    ppermute x1, starting transfers between devices, shards(): out_other = lax.ppermute(out_theirs, 'head', [(0, 1), (1, 0)])  4.98 us
  transfers between devices with their start and end apart: 6, of which 3 were waited for; matrix products, arithmetic and copies ran while one was open for 1% of the time, Pallas kernels for 6%

profile of v5, /device:TPU:65, one launch (start us, length us, event | category | flops | bytes accessed | tf_op | source)
XLA Modules:
  0.0 140.9 jit_solution(9294660078661740239)
XLA Ops:
  0.0 4.9 %gradient.1 = (bf16[1536,256]{1,0:T(8,128)(2,1)}, bf16[2,2,256,256]{3,2,1,0:T(8,128)(2,1)}) custom-call(s32[1]{0:T(128)} %bitcast.place_ref, s32[384]{0:T(512)} %counts_ref.5, bf16[256,2,256]{2,1,0:T(2,128)(2,1)} %keys_ref.1, bf16[256,2,256]{2,1,0:T(2,128)(2,1)} %values_ref.1, f32[2,256]{1,0:T(2,128)} %bitcast.9, f32[2,3,256,256]{3,2,1,0:T(8,128)} %weights_ref.1), custom_call_target="tpu_custom_call" | custom-call | flops 469762048 | bytes 3000000 | tf_op jit(solution)/shard_map/gradient/pallas_call | solution.py:84
  4.9 35.9 %all_to_all.15.blocks_ref = bf16[96,16,256]{2,1,0:T(8,128)(2,1)S(1)} all-to-all(bf16[96,16,256]{2,1,0:T(8,128)(2,1)} %bitcast.8), channel_id=1, replica_groups=mesh['z'=4,'p'=96,'head'=2] {'p'}, dimensions={0} | all-to-all | bytes 1572864 | tf_op jit(solution)/shard_map/all_to_all | solution.py:375
  40.7 0.8 collect.1
  41.5 12.2 %all-to-all-start.1 = ((f32[4,16,256]{2,1,0:T(8,128)}), f32[4,16,256]{2,1,0:T(8,128)S(1)}, u32[]{:S(2)}, u32[]{:S(2)}) async-start(f32[4,16,256]{2,1,0:T(8,128)} %collect.1), calls=%async_computation.1 | async-start | bytes 131072 | tf_op jit(solution)/shard_map/all_to_all | solution.py:381
  53.7 0.7 constant_dynamic-slice_fusion.old_ref
  54.4 8.6 %all-to-all-done.1.sums_ref = f32[4,16,256]{2,1,0:T(8,128)S(1)} async-done(((f32[4,16,256]{2,1,0:T(8,128)}), f32[4,16,256]{2,1,0:T(8,128)S(1)}, u32[]{:S(2)}, u32[]{:S(2)}) %all-to-all-start.1) | async-done | bytes 65568 | tf_op jit(solution)/shard_map/all_to_all | solution.py:381
  63.0 1.0 refresh.1
  64.0 8.7 %all-to-all-start.2 = ((bf16[96,16,256]{2,1,0:T(8,128)(2,1)}), bf16[96,16,256]{2,1,0:T(8,128)(2,1)S(1)}, u32[]{:S(2)}, u32[]{:S(2)}) async-start(bf16[96,16,256]{2,1,0:T(8,128)(2,1)} %refresh.1), calls=%async_computation.2 | async-start | bytes 1572864 | tf_op jit(solution)/shard_map/all_to_all | solution.py:387
  72.7 0.0 copy-start
  72.7 2.2 %copy-done = bf16[512,4096]{1,0:T(8,128)(2,1)S(1)} copy-done((bf16[512,4096]{1,0:T(8,128)(2,1)S(1)}, bf16[512,4096]{1,0:T(8,128)(2,1)}, u32[]{:S(2)}) %copy-start) | copy-done | bytes 4194328
  74.9 1.9 %split.1 = (bf16[512,2048]{1,0:T(8,128)(2,1)S(1)}, bf16[512,2048]{1,0:T(8,128)(2,1)}) custom-call(s32[1]{0:T(128)} %bitcast.5.place_ref, bf16[512,4096]{1,0:T(8,128)(2,1)S(1)} %copy-done, bf16[512,4096]{1,0:T(8,128)(2,1)S(1)} %copy-done), custom_call_target="tpu_custom_call" | custom-call | bytes 8000000 | tf_op jit(solution)/shard_map/split/pallas_call | solution.py:239
  76.8 1.3 copy-done.1
  78.1 5.0 %collective-permute-start.3 = (bf16[512,2048]{1,0:T(8,128)(2,1)}, bf16[512,2048]{1,0:T(8,128)(2,1)S(1)}, u32[]{:S(2)}, u32[]{:S(2)}) collective-permute-start(bf16[512,2048]{1,0:T(8,128)(2,1)} %get-tuple-element.15), channel_id=1, source_target_pairs={{0,1},{1,0},{2,3},{3,2},{4,5},{5,4},{6,7},{7,6},{8,9},{9,8},{10,11... | collective-permute-start | bytes 6291464 | tf_op jit(solution)/shard_map/ppermute | solution.py:379
  83.1 0.0 copy-done.4
  83.1 3.1 %collective-permute-start = (bf16[2,2,256,256]{3,2,1,0:T(8,128)(2,1)S(1)}, bf16[2,2,256,256]{3,2,1,0:T(8,128)(2,1)S(1)}, u32[]{:S(2)}, u32[]{:S(2)}) collective-permute-start(bf16[2,2,256,256]{3,2,1,0:T(8,128)(2,1)S(1)} %copy-done.4), channel_id=1, source_target_pairs={{0,2},{2,4},{4,6},{6,8},{8,10},{10,12},{12,14},{14,16},{16,18},{18... | collective-permute-start | bytes 1572872 | tf_op jit(solution)/shard_map/ppermute | solution.py:22
  86.2 18.9 %collective-permute-done.near_ref = bf16[2,2,256,256]{3,2,1,0:T(8,128)(2,1)S(1)} collective-permute-done((bf16[2,2,256,256]{3,2,1,0:T(8,128)(2,1)S(1)}, bf16[2,2,256,256]{3,2,1,0:T(8,128)(2,1)S(1)}, u32[]{:S(2)}, u32[]{:S(2)}) %collective-permute-start) | collective-permute-done | bytes 524320 | tf_op jit(solution)/shard_map/ppermute | solution.py:22
  105.1 1.9 %collective-permute-start.1 = (bf16[2,2,256,256]{3,2,1,0:T(8,128)(2,1)S(1)}, bf16[2,2,256,256]{3,2,1,0:T(8,128)(2,1)S(1)}, u32[]{:S(2)}, u32[]{:S(2)}) collective-permute-start(bf16[2,2,256,256]{3,2,1,0:T(8,128)(2,1)S(1)} %collective-permute-done.near_ref), channel_id=1, source_target_pairs={{0,2},{2,4},{4,6},{6,8},{8,10},{10,12},{12,14},{14,16},{16,18},{18... | collective-permute-start | bytes 1572872 | tf_op jit(solution)/shard_map/ppermute | solution.py:22
  107.0 16.7 %collective-permute-done.1.far_ref = bf16[2,2,256,256]{3,2,1,0:T(8,128)(2,1)S(1)} collective-permute-done((bf16[2,2,256,256]{3,2,1,0:T(8,128)(2,1)S(1)}, bf16[2,2,256,256]{3,2,1,0:T(8,128)(2,1)S(1)}, u32[]{:S(2)}, u32[]{:S(2)}) %collective-permute-start.1) | collective-permute-done | bytes 524320 | tf_op jit(solution)/shard_map/ppermute | solution.py:22
  123.8 2.0 %window.1 = (f32[256,512]{1,0:T(8,128)S(1)}, bf16[2,256,256]{2,1,0:T(8,128)(2,1)S(1)}) custom-call(s32[1]{0:T(128)} %bitcast.place_ref, s32[384]{0:T(512)S(1)} %copy-done.8, bf16[256,2,256]{2,1,0:T(2,128)(2,1)S(1)} %copy-done.6, bf16[2,2,256,256]{3,2,1,0:T(8,128)(2,1)S(1)} %copy-done.4, bf16[2,2,256,256]{3,2,1,0:T(8,128)(2,1)S(1)} %collective-permute-done.near_ref, ...), custom_call_target="tpu_custom_call" | custom-call | flops 402653184 | bytes 3000000 | tf_op jit(solution)/shard_map/window/pallas_call | solution.py:139
  125.8 0.8 copy-done.5
  126.6 0.7 copy-done.7
  127.3 0.0 all-to-all-done.2
  127.3 0.9 copy-done.9
  128.2 3.4 %features.1.own_ref = bf16[256,512]{1,0:T(8,128)(2,1)} custom-call(s32[1]{0:T(128)} %bitcast.place_ref, s32[384]{0:T(512)} %counts_ref.5, bf16[2,256,256]{2,1,0:T(8,128)(2,1)} %copy-done.7, f32[256,512]{1,0:T(8,128)} %copy-done.5, bf16[1536,256]{1,0:T(8,128)(2,1)} %bitcast.6), custom_call_target="tpu_custom_call" | custom-call | flops 201326592 | bytes 2000000 | tf_op jit(solution)/shard_map/features/pallas_call | solution.py:211
  131.6 3.7 %collective-permute-start.2 = (bf16[256,512]{1,0:T(8,128)(2,1)}, bf16[256,512]{1,0:T(8,128)(2,1)S(1)}, u32[]{:S(2)}, u32[]{:S(2)}) collective-permute-start(bf16[256,512]{1,0:T(8,128)(2,1)} %features.1.own_ref), channel_id=1, source_target_pairs={{0,1},{1,0},{2,3},{3,2},{4,5},{5,4},{6,7},{7,6},{8,9},{9,8},{10,11... | collective-permute-start | bytes 786440 | tf_op jit(solution)/shard_map/ppermute | solution.py:390
  135.3 0.0 copy-start.2
  135.3 1.6 %copy-done.2 = bf16[512,2048]{1,0:T(8,128)(2,1)S(1)} copy-done((bf16[512,2048]{1,0:T(8,128)(2,1)S(1)}, bf16[512,2048]{1,0:T(8,128)(2,1)}, u32[]{:S(2)}) %copy-start.2) | copy-done | bytes 2097176
  136.9 0.9 copy-done.3
  137.8 0.7 own_project.1.own_ref
  138.6 0.0 collective-permute-done.3.weight_ref
  138.6 0.0 collective-permute-done.2.other_ref
  138.6 2.3 %project.1 = bf16[256,2048]{1,0:T(8,128)(2,1)} custom-call(bf16[256,512]{1,0:T(8,128)(2,1)S(1)} %collective-permute-done.2.other_ref, bf16[512,2048]{1,0:T(8,128)(2,1)S(1)} %collective-permute-done.3.weight_ref, f32[256,2048]{1,0:T(8,128)S(1)} %own_project.1.own_ref), custom_call_target="tpu_custom_call" | custom-call | flops 536870912 | bytes 6000000 | tf_op jit(solution)/shard_map/project/pallas_call | solution.py:310
  (10 shorter events, 0.0 us)
Async XLA Ops:
  41.5 21.5 %all-to-all-start.1 = ((f32[4,16,256]{2,1,0:T(8,128)}), f32[4,16,256]{2,1,0:T(8,128)S(1)}, u32[]{:S(2)}, u32[]{:S(2)}) async-start(f32[4,16,256]{2,1,0:T(8,128)} %collect.1), calls=%async_computation.1 | async-start | bytes 131072 | tf_op jit(solution)/shard_map/all_to_all | solution.py:381
  64.0 63.3 %all-to-all-start.2 = ((bf16[96,16,256]{2,1,0:T(8,128)(2,1)}), bf16[96,16,256]{2,1,0:T(8,128)(2,1)S(1)}, u32[]{:S(2)}, u32[]{:S(2)}) async-start(bf16[96,16,256]{2,1,0:T(8,128)(2,1)} %refresh.1), calls=%async_computation.2 | async-start | bytes 1572864 | tf_op jit(solution)/shard_map/all_to_all | solution.py:387
  72.7 2.2 %copy-start = (bf16[512,4096]{1,0:T(8,128)(2,1)S(1)}, bf16[512,4096]{1,0:T(8,128)(2,1)}, u32[]{:S(2)}) copy-start(bf16[512,4096]{1,0:T(8,128)(2,1)} %theirs_in_ref.1) | copy-start | bytes 12582916
  74.9 8.2 %copy-start.4 = (bf16[2,2,256,256]{3,2,1,0:T(8,128)(2,1)S(1)}, bf16[2,2,256,256]{3,2,1,0:T(8,128)(2,1)}, u32[]{:S(2)}) copy-start(bf16[2,2,256,256]{3,2,1,0:T(8,128)(2,1)} %get-tuple-element.11.own_ref) | copy-start | bytes 1572868
  74.9 48.9 %copy-start.6 = (bf16[256,2,256]{2,1,0:T(2,128)(2,1)S(1)}, bf16[256,2,256]{2,1,0:T(2,128)(2,1)}, u32[]{:S(2)}) copy-start(bf16[256,2,256]{2,1,0:T(2,128)(2,1)} %queries_ref.1) | copy-start | bytes 786436
  74.9 48.9 %copy-start.8 = (s32[384]{0:T(512)S(1)}, s32[384]{0:T(512)}, u32[]{:S(2)}) copy-start(s32[384]{0:T(512)} %counts_ref.5) | copy-start | bytes 4612
  76.8 1.3 copy-start.1
  78.1 60.5 %collective-permute-start.3 = (bf16[512,2048]{1,0:T(8,128)(2,1)}, bf16[512,2048]{1,0:T(8,128)(2,1)S(1)}, u32[]{:S(2)}, u32[]{:S(2)}) collective-permute-start(bf16[512,2048]{1,0:T(8,128)(2,1)} %get-tuple-element.15), channel_id=1, source_target_pairs={{0,1},{1,0},{2,3},{3,2},{4,5},{5,4},{6,7},{7,6},{8,9},{9,8},{10,11... | collective-permute-start | bytes 6291464 | tf_op jit(solution)/shard_map/ppermute | solution.py:379
  83.1 22.0 %collective-permute-start = (bf16[2,2,256,256]{3,2,1,0:T(8,128)(2,1)S(1)}, bf16[2,2,256,256]{3,2,1,0:T(8,128)(2,1)S(1)}, u32[]{:S(2)}, u32[]{:S(2)}) collective-permute-start(bf16[2,2,256,256]{3,2,1,0:T(8,128)(2,1)S(1)} %copy-done.4), channel_id=1, source_target_pairs={{0,2},{2,4},{4,6},{6,8},{8,10},{10,12},{12,14},{14,16},{16,18},{18... | collective-permute-start | bytes 1572872 | tf_op jit(solution)/shard_map/ppermute | solution.py:22
  105.1 18.7 %collective-permute-start.1 = (bf16[2,2,256,256]{3,2,1,0:T(8,128)(2,1)S(1)}, bf16[2,2,256,256]{3,2,1,0:T(8,128)(2,1)S(1)}, u32[]{:S(2)}, u32[]{:S(2)}) collective-permute-start(bf16[2,2,256,256]{3,2,1,0:T(8,128)(2,1)S(1)} %collective-permute-done.near_ref), channel_id=1, source_target_pairs={{0,2},{2,4},{4,6},{6,8},{8,10},{10,12},{12,14},{14,16},{16,18},{18... | collective-permute-start | bytes 1572872 | tf_op jit(solution)/shard_map/ppermute | solution.py:22
  125.8 0.8 copy-start.5
  126.6 0.7 copy-start.7
  127.3 0.9 copy-start.9
  131.6 7.0 %collective-permute-start.2 = (bf16[256,512]{1,0:T(8,128)(2,1)}, bf16[256,512]{1,0:T(8,128)(2,1)S(1)}, u32[]{:S(2)}, u32[]{:S(2)}) collective-permute-start(bf16[256,512]{1,0:T(8,128)(2,1)} %features.1.own_ref), channel_id=1, source_target_pairs={{0,1},{1,0},{2,3},{3,2},{4,5},{5,4},{6,7},{7,6},{8,9},{9,8},{10,11... | collective-permute-start | bytes 786440 | tf_op jit(solution)/shard_map/ppermute | solution.py:390
  135.3 1.6 %copy-start.2 = (bf16[512,2048]{1,0:T(8,128)(2,1)S(1)}, bf16[512,2048]{1,0:T(8,128)(2,1)}, u32[]{:S(2)}) copy-start(bf16[512,2048]{1,0:T(8,128)(2,1)} %copy-done.1) | copy-start | bytes 6291460
  136.9 0.9 copy-start.3

commit v6 on v5

--- a/solution.py
+++ b/solution.py
@@ -20,6 +20,10 @@
 def passed_along(value, steps):
     count = lax.axis_size(CTX)
     return lax.ppermute(value, CTX, [(source, source + steps) for source in range(count - steps)])
+
+
+def turned(value, steps):
+    return lax.ppermute(value, "z", [(place, (place + steps) % RING) for place in range(RING)])
 
 
 def product(left, right, left_dim, right_dim):
@@ -154,55 +158,19 @@
     )(place, counts, queries, own, near, far)
 
 
-def feature_kernel(
-    place_ref,
-    counts_ref,
-    queries_ref,
-    window_ref,
-    weights_ref,
-    features_ref,
-    held_queries,
-    held_window,
-    held_weights,
-    sems,
-):
-    heads, tokens, width = held_queries.shape
-    mats = 3
-    fetches = []
+def feature_kernel(place_ref, counts_ref, queries_ref, window_ref, weights_ref, features_ref):
+    heads, tokens, width = queries_ref.shape
+    valid = lax.broadcasted_iota(jnp.int32, (tokens, 1), 0) < place_count(counts_ref, place_ref, 0)
     for head in range(heads):
-        fetches.append(
-            pltpu.make_async_copy(
-                queries_ref.at[head], held_queries.at[head], sems.at[len(fetches)]
-            )
-        )
-        for index in range(mats):
-            rows = pl.ds((head * mats + index) * width, width)
-            fetches.append(
-                pltpu.make_async_copy(
-                    weights_ref.at[rows], held_weights.at[rows], sems.at[len(fetches)]
-                )
-            )
-    fetches.append(pltpu.make_async_copy(window_ref, held_window, sems.at[len(fetches)]))
-    for fetch in fetches:
-        fetch.start()
-    valid = lax.broadcasted_iota(jnp.int32, (tokens, 1), 0) < place_count(counts_ref, place_ref, 0)
-    learned = []
-    for head in range(heads):
-        for fetch in fetches[head * (mats + 1) : (head + 1) * (mats + 1)]:
-            fetch.wait()
-        queries = held_queries[head]
-        first = head * mats * width
-        gate = product(queries, held_weights[first : first + width, :], 1, 1)
-        up = product(queries, held_weights[first + width : first + 2 * width, :], 1, 1)
+        queries = queries_ref[head]
+        first = head * 3 * width
+        gate = product(queries, weights_ref[first : first + width, :], 1, 1)
+        up = product(queries, weights_ref[first + width : first + 2 * width, :], 1, 1)
         hidden = (gate * jax.nn.sigmoid(gate) * up).astype(jnp.bfloat16)
-        learned.append(
-            product(hidden, held_weights[first + 2 * width : first + 3 * width, :], 1, 1)
-        )
-    fetches[-1].wait()
-    for head in range(heads):
+        learned = product(hidden, weights_ref[first + 2 * width : first + 3 * width, :], 1, 1)
         columns = slice(head * width, (head + 1) * width)
         features_ref[:, columns] = jnp.where(
-            valid, learned[head] + held_window[:, columns], 0.0
+            valid, learned + window_ref[:, columns], 0.0
         ).astype(jnp.bfloat16)
 
 
@@ -211,15 +179,10 @@
     return pl.pallas_call(
         feature_kernel,
         out_shape=jax.ShapeDtypeStruct((tokens, heads * width), jnp.bfloat16),
-        in_specs=[SMEM, SMEM] + [pl.BlockSpec(memory_space=pl.ANY)] * 3,
+        in_specs=[SMEM, SMEM] + [VMEM] * 3,
         out_specs=VMEM,
-        scratch_shapes=[
-            pltpu.VMEM(queries.shape, jnp.bfloat16),
-            pltpu.VMEM(window.shape, jnp.float32),
-            pltpu.VMEM(new_flat.shape, jnp.bfloat16),
-            pltpu.SemaphoreType.DMA((4 * heads + 1,)),
-        ],
         name="features",
+        compiler_params=pltpu.CompilerParams(vmem_limit_bytes=VMEM_BYTES),
         cost_estimate=pl.CostEstimate(
             flops=6 * tokens * width * width * heads, transcendentals=131072, bytes_accessed=2000000
         ),
@@ -252,21 +215,39 @@
             ),
         ),
         name="split",
-        compiler_params=pltpu.CompilerParams(vmem_limit_bytes=VMEM_BYTES),
         cost_estimate=pl.CostEstimate(flops=0, transcendentals=0, bytes_accessed=8000000),
     )(head_place, out_weight, out_weight)
 
 
-def own_project_kernel(own_ref, weight_ref, out_ref):
-    out_ref[...] = jnp.dot(own_ref[...], weight_ref[...], preferred_element_type=jnp.float32)
+def own_project_kernel(own_ref, weight_ref, out_ref, held_weight, sems):
+    tiles, _, tile = held_weight.shape
+    fetches = [
+        pltpu.make_async_copy(
+            weight_ref.at[:, step * tile : (step + 1) * tile], held_weight.at[step], sems.at[step]
+        )
+        for step in range(tiles)
+    ]
+    for fetch in fetches:
+        fetch.start()
+    for step in range(tiles):
+        fetches[step].wait()
+        out_ref[:, step * tile : (step + 1) * tile] = jnp.dot(
+            own_ref[...], held_weight[step], preferred_element_type=jnp.float32
+        )
 
 
 def own_projected(own, weight):
+    depth, columns = weight.shape
+    tiles = 4
     return pl.pallas_call(
         own_project_kernel,
-        out_shape=jax.ShapeDtypeStruct((own.shape[0], weight.shape[1]), jnp.float32),
-        in_specs=[VMEM, VMEM],
+        out_shape=jax.ShapeDtypeStruct((own.shape[0], columns), jnp.float32),
+        in_specs=[VMEM, pl.BlockSpec(memory_space=pl.ANY)],
         out_specs=VMEM,
+        scratch_shapes=[
+            pltpu.VMEM((tiles, depth, columns // tiles), jnp.bfloat16),
+            pltpu.SemaphoreType.DMA((tiles,)),
+        ],
         name="own_project",
         compiler_params=pltpu.CompilerParams(vmem_limit_bytes=VMEM_BYTES),
         cost_estimate=pl.CostEstimate(
@@ -326,14 +307,13 @@
 
 
 def collect_kernel(blocks_ref, sums_ref):
-    total = jnp.sum(blocks_ref[...].astype(jnp.float32), axis=0)
-    sums_ref[...] = jnp.broadcast_to(total[None], sums_ref.shape)
-
-
-def collected(copies, blocks):
+    sums_ref[...] = jnp.sum(blocks_ref[...].astype(jnp.float32), axis=0)
+
+
+def collected(blocks):
     return pl.pallas_call(
         collect_kernel,
-        out_shape=jax.ShapeDtypeStruct((copies, *blocks.shape[1:]), jnp.float32),
+        out_shape=jax.ShapeDtypeStruct(blocks.shape[1:], jnp.float32),
         in_specs=[VMEM],
         out_specs=VMEM,
         name="collect",
@@ -342,8 +322,8 @@
     )(blocks)
 
 
-def refresh_kernel(total, sums_ref, old_ref, rows_ref):
-    gradient = jnp.sum(sums_ref[...], axis=0)
+def refresh_kernel(total, own_ref, behind_ref, opposite_ref, ahead_ref, old_ref, rows_ref):
+    gradient = (own_ref[...] + opposite_ref[...]) + (behind_ref[...] + ahead_ref[...])
     old = old_ref[...]
     updated = old - gradient / math.sqrt(total)
     old_norm = jnp.sqrt(jnp.sum(old * old, axis=1, keepdims=True))
@@ -351,16 +331,16 @@
     rows_ref[...] = jnp.broadcast_to(fresh.astype(jnp.bfloat16)[None], rows_ref.shape)
 
 
-def refreshed(total, copies, sums, old_rows):
+def refreshed(total, copies, parts, old_rows):
     return pl.pallas_call(
         functools.partial(refresh_kernel, total),
         out_shape=jax.ShapeDtypeStruct((copies, *old_rows.shape), jnp.bfloat16),
-        in_specs=[VMEM, VMEM],
+        in_specs=[VMEM] * (RING + 1),
         out_specs=VMEM,
         name="refresh",
         compiler_params=pltpu.CompilerParams(vmem_limit_bytes=VMEM_BYTES),
         cost_estimate=pl.CostEstimate(flops=100000, transcendentals=0, bytes_accessed=1000000),
-    )(sums, old_rows)
+    )(*parts, old_rows)
 
 
 def shards(queries, token_keys, token_values, step_rates, counts, fast_weights, out_weight):
@@ -377,19 +357,24 @@
         head_place.reshape(1).astype(jnp.int32), out_weight
     )
     out_other = lax.ppermute(out_theirs, "head", [(0, 1), (1, 0)])
-    sums = collected(RING, blocks)
-    sums = lax.all_to_all(sums, "z", 0, 0, tiled=True)
+    parts = [collected(blocks)]
+    for steps in range(1, RING):
+        parts.append(turned(parts[0], steps))
     far = passed_along(near, 1)
     old_flat = fast_weights.reshape(-1, head_width)
     own_rows = old_flat.shape[0] // plane_count
     old_rows = lax.dynamic_slice_in_dim(old_flat, plane_place * own_rows, own_rows, 0)
-    new_rows = refreshed(tok_rows * device_count, plane_count, sums, old_rows)
+    new_rows = refreshed(tok_rows * device_count, plane_count, parts, old_rows)
     new_flat = lax.all_to_all(new_rows, "p", 0, 0, tiled=True).reshape(-1, head_width)
     window, turned_queries = window_attention(place, counts, queries, pairs, near, far)
     features = features_of(place, counts, turned_queries, window, new_flat)
     other = lax.ppermute(features, "head", [(0, 1), (1, 0)])
-    own_product = own_projected(features, out_own)
-    return projected(other, out_other, own_product)
+    own_product = own_projected(
+        features, pltpu.with_memory_space_constraint(out_own, pltpu.MemorySpace.HBM)
+    )
+    return projected(
+        other, pltpu.with_memory_space_constraint(out_other, pltpu.MemorySpace.HBM), own_product
+    )
 
 
 def solution(mesh):

time: 142 us -> 138 us (0.972)
  blocking collectives: 35.9 us -> 0 us
  starting transfers between devices: 34.6 us -> 54.7 us
  waiting for transfers between devices: 44.2 us -> 63.3 us
  local copies, waits for them, and re-layouts: 9.12 us -> 0.74 us
    all_to_all x1 -> x0, blocking collectives: 35.9 us -> none  [shards(): lax.all_to_all(local_grad.reshape(plane_count, -1, head_width), 'p', 0, 0...]
    ppermute x0 -> x3, starting transfers between devices: none -> 20.5 us  [turned(): lax.ppermute(value, 'z', [(place, (place + steps) % RING) for place in ra...]
    all_to_all x1, waiting for transfers between devices: 8.56 us -> 22.6 us  [shards(): lax.all_to_all(local_grad.reshape(plane_count, -1, head_width), 'p', 0, 0...]
    unnamed x20 -> x6, local copies, waits for them, and re-layouts: 8.4 us -> 0.02 us
    ppermute x0 -> x3, waiting for transfers between devices: none -> 4.05 us  [turned(): lax.ppermute(value, 'z', [(place, (place + steps) % RING) for place in ra...]
    pallas_call x1, Pallas kernels: 3.41 us -> 1.14 us  [features_of(): pl.pallas_call(feature_kernel, out_shape=jax.ShapeDtypeStruct((tokens, he...]
    pallas_call x1, Pallas kernels: 1.85 us -> 3.76 us  [column_halves(): pl.pallas_call(split_kernel, out_shape=(piece, piece), grid_spec=pltpu.Pr...]
    pallas_call x1, Pallas kernels: 0.7 us -> 2.29 us  [own_projected(): pl.pallas_call(own_project_kernel, out_shape=jax.ShapeDtypeStruct((own.sh...]
  transfers between devices with their start and end apart: 6 -> 9, of which waited for: 3 -> 4; matrix products, arithmetic and copies ran while one was open for 1% -> 1% of each run, Pallas kernels for 6% -> 7%
where the time goes in v6:
time: 138 us; the launch traced here: 137 us
  waiting for transfers between devices  63.3 us (46%)
  starting transfers between devices  54.7 us (40%)
  Pallas kernels  18.3 us (13%)
    ppermute x2, waiting for transfers between devices, passed_along(): lax.ppermute(value, CTX, [(source, source + steps) for source in range(co...  36.7 us
    all_to_all x1, waiting for transfers between devices, shards(): lax.all_to_all(local_grad.reshape(plane_count, -1, head_width), 'p', 0, 0...  22.6 us
    ppermute x3, starting transfers between devices, turned(): lax.ppermute(value, 'z', [(place, (place + steps) % RING) for place in ra...  20.5 us
    all_to_all x1, starting transfers between devices, shards(): lax.all_to_all(local_grad.reshape(plane_count, -1, head_width), 'p', 0, 0...  13.3 us
    all_to_all x1, starting transfers between devices, shards(): lax.all_to_all(new_rows, 'p', 0, 0, tiled=True).reshape(-1, head_width)  7.28 us
    ppermute x2, starting transfers between devices, passed_along(): lax.ppermute(value, CTX, [(source, source + steps) for source in range(co...  5.01 us
    ppermute x1, starting transfers between devices, shards(): out_other = lax.ppermute(out_theirs, 'head', [(0, 1), (1, 0)])  4.95 us
    pallas_call x1, Pallas kernels, local_gradient(): pl.pallas_call(gradient_kernel, out_shape=(jax.ShapeDtypeStruct((heads *...  4.85 us
  transfers between devices with their start and end apart: 9, of which 4 were waited for; matrix products, arithmetic and copies ran while one was open for 1% of the time, Pallas kernels for 7%

profile of v6, /device:TPU:65, one launch (start us, length us, event | category | flops | bytes accessed | tf_op | source)
XLA Modules:
  0.0 137.3 jit_solution(15934970685377536404)
XLA Ops:
  0.0 4.8 %gradient.1 = (bf16[1536,256]{1,0:T(8,128)(2,1)}, bf16[2,2,256,256]{3,2,1,0:T(8,128)(2,1)}) custom-call(s32[1]{0:T(128)} %bitcast.place_ref, s32[384]{0:T(512)} %counts_ref.5, bf16[256,2,256]{2,1,0:T(2,128)(2,1)} %keys_ref.1, bf16[256,2,256]{2,1,0:T(2,128)(2,1)} %values_ref.1, f32[2,256]{1,0:T(2,128)} %bitcast.9, f32[2,3,256,256]{3,2,1,0:T(8,128)} %weights_ref.1), custom_call_target="tpu_custom_call" | custom-call | flops 469762048 | bytes 3000000 | tf_op jit(solution)/shard_map/gradient/pallas_call | solution.py:88
  4.9 13.3 %all-to-all-start = ((bf16[96,16,256]{2,1,0:T(8,128)(2,1)}), bf16[96,16,256]{2,1,0:T(8,128)(2,1)S(1)}, u32[]{:S(2)}, u32[]{:S(2)}) async-start(bf16[96,16,256]{2,1,0:T(8,128)(2,1)} %bitcast.8), calls=%async_computation | async-start | bytes 1572864 | tf_op jit(solution)/shard_map/all_to_all | solution.py:355
  18.2 22.6 %all-to-all-done.blocks_ref = bf16[96,16,256]{2,1,0:T(8,128)(2,1)S(1)} async-done(((bf16[96,16,256]{2,1,0:T(8,128)(2,1)}), bf16[96,16,256]{2,1,0:T(8,128)(2,1)S(1)}, u32[]{:S(2)}, u32[]{:S(2)}) %all-to-all-start) | async-done | bytes 786464 | tf_op jit(solution)/shard_map/all_to_all | solution.py:355
  40.7 0.2 collect.1.own_ref
  40.9 9.8 %collective-permute-start.2 = (f32[16,256]{1,0:T(8,128)S(1)}, f32[16,256]{1,0:T(8,128)S(1)}, u32[]{:S(2)}, u32[]{:S(2)}) collective-permute-start(f32[16,256]{1,0:T(8,128)S(1)} %collect.1.own_ref), channel_id=1, source_target_pairs={{0,192},{192,384},{384,576},{576,0},{1,193},{193,385},{385,577},{5... | collective-permute-start | bytes 49160 | tf_op jit(solution)/shard_map/ppermute | solution.py:26
  50.8 7.9 %collective-permute-start.3 = (f32[16,256]{1,0:T(8,128)S(1)}, f32[16,256]{1,0:T(8,128)S(1)}, u32[]{:S(2)}, u32[]{:S(2)}) collective-permute-start(f32[16,256]{1,0:T(8,128)S(1)} %collect.1.own_ref), channel_id=1, source_target_pairs={{0,384},{192,576},{384,0},{576,192},{1,385},{193,577},{385,1},{577... | collective-permute-start | bytes 49160 | tf_op jit(solution)/shard_map/ppermute | solution.py:26
  58.7 2.7 %collective-permute-start.4 = (f32[16,256]{1,0:T(8,128)S(1)}, f32[16,256]{1,0:T(8,128)S(1)}, u32[]{:S(2)}, u32[]{:S(2)}) collective-permute-start(f32[16,256]{1,0:T(8,128)S(1)} %collect.1.own_ref), channel_id=1, source_target_pairs={{0,576},{192,0},{384,192},{576,384},{1,577},{193,1},{385,193},{577... | collective-permute-start | bytes 49160 | tf_op jit(solution)/shard_map/ppermute | solution.py:26
  61.4 0.7 constant_dynamic-slice_fusion.old_ref
  62.1 0.0 collective-permute-done.2.behind_ref
  62.2 0.0 collective-permute-done.3.opposite_ref
  62.2 4.0 %collective-permute-done.4.ahead_ref = f32[16,256]{1,0:T(8,128)S(1)} collective-permute-done((f32[16,256]{1,0:T(8,128)S(1)}, f32[16,256]{1,0:T(8,128)S(1)}, u32[]{:S(2)}, u32[]{:S(2)}) %collective-permute-start.4) | collective-permute-done | bytes 16416 | tf_op jit(solution)/shard_map/ppermute | solution.py:26
  66.2 1.0 refresh.1
  67.2 7.3 %all-to-all-start.1 = ((bf16[96,16,256]{2,1,0:T(8,128)(2,1)}), bf16[96,16,256]{2,1,0:T(8,128)(2,1)S(1)}, u32[]{:S(2)}, u32[]{:S(2)}) async-start(bf16[96,16,256]{2,1,0:T(8,128)(2,1)} %refresh.1), calls=%async_computation.1 | async-start | bytes 1572864 | tf_op jit(solution)/shard_map/all_to_all | solution.py:368
  74.5 0.0 copy-start
  74.5 0.0 copy-start.1
  74.5 0.0 copy-start.2
  74.6 3.8 %split.1 = (bf16[512,2048]{1,0:T(8,128)(2,1)}, bf16[512,2048]{1,0:T(8,128)(2,1)}) custom-call(s32[1]{0:T(128)} %bitcast.5.place_ref, bf16[512,4096]{1,0:T(8,128)(2,1)} %theirs_in_ref.1, bf16[512,4096]{1,0:T(8,128)(2,1)} %theirs_in_ref.1), custom_call_target="tpu_custom_call" | custom-call | bytes 8000000 | tf_op jit(solution)/shard_map/split/pallas_call | solution.py:202
  78.3 5.0 %collective-permute-start.6 = (bf16[512,2048]{1,0:T(8,128)(2,1)}, bf16[512,2048]{1,0:T(8,128)(2,1)}, u32[]{:S(2)}, u32[]{:S(2)}) collective-permute-start(bf16[512,2048]{1,0:T(8,128)(2,1)} %get-tuple-element.15), channel_id=1, source_target_pairs={{0,1},{1,0},{2,3},{3,2},{4,5},{5,4},{6,7},{7,6},{8,9},{9,8},{10,11... | collective-permute-start | bytes 6291464 | tf_op jit(solution)/shard_map/ppermute | solution.py:359
  83.3 0.0 copy-done
  83.3 3.1 %collective-permute-start = (bf16[2,2,256,256]{3,2,1,0:T(8,128)(2,1)S(1)}, bf16[2,2,256,256]{3,2,1,0:T(8,128)(2,1)S(1)}, u32[]{:S(2)}, u32[]{:S(2)}) collective-permute-start(bf16[2,2,256,256]{3,2,1,0:T(8,128)(2,1)S(1)} %copy-done), channel_id=1, source_target_pairs={{0,2},{2,4},{4,6},{6,8},{8,10},{10,12},{12,14},{14,16},{16,18},{18... | collective-permute-start | bytes 1572872 | tf_op jit(solution)/shard_map/ppermute | solution.py:22
  86.4 20.0 %collective-permute-done.near_ref = bf16[2,2,256,256]{3,2,1,0:T(8,128)(2,1)S(1)} collective-permute-done((bf16[2,2,256,256]{3,2,1,0:T(8,128)(2,1)S(1)}, bf16[2,2,256,256]{3,2,1,0:T(8,128)(2,1)S(1)}, u32[]{:S(2)}, u32[]{:S(2)}) %collective-permute-start) | collective-permute-done | bytes 524320 | tf_op jit(solution)/shard_map/ppermute | solution.py:22
  106.4 1.9 %collective-permute-start.1 = (bf16[2,2,256,256]{3,2,1,0:T(8,128)(2,1)S(1)}, bf16[2,2,256,256]{3,2,1,0:T(8,128)(2,1)S(1)}, u32[]{:S(2)}, u32[]{:S(2)}) collective-permute-start(bf16[2,2,256,256]{3,2,1,0:T(8,128)(2,1)S(1)} %collective-permute-done.near_ref), channel_id=1, source_target_pairs={{0,2},{2,4},{4,6},{6,8},{8,10},{10,12},{12,14},{14,16},{16,18},{18... | collective-permute-start | bytes 1572872 | tf_op jit(solution)/shard_map/ppermute | solution.py:22
  108.3 16.7 %collective-permute-done.1.far_ref = bf16[2,2,256,256]{3,2,1,0:T(8,128)(2,1)S(1)} collective-permute-done((bf16[2,2,256,256]{3,2,1,0:T(8,128)(2,1)S(1)}, bf16[2,2,256,256]{3,2,1,0:T(8,128)(2,1)S(1)}, u32[]{:S(2)}, u32[]{:S(2)}) %collective-permute-start.1) | collective-permute-done | bytes 524320 | tf_op jit(solution)/shard_map/ppermute | solution.py:22
  125.0 0.0 copy-done.2
  125.0 2.0 %window.1 = (f32[256,512]{1,0:T(8,128)S(1)}, bf16[2,256,256]{2,1,0:T(8,128)(2,1)S(1)}) custom-call(s32[1]{0:T(128)} %bitcast.place_ref, s32[384]{0:T(512)S(1)} %copy-done.2, bf16[256,2,256]{2,1,0:T(2,128)(2,1)S(1)} %copy-done.1, bf16[2,2,256,256]{3,2,1,0:T(8,128)(2,1)S(1)} %copy-done, bf16[2,2,256,256]{3,2,1,0:T(8,128)(2,1)S(1)} %collective-permute-done.near_ref, ...), custom_call_target="tpu_custom_call" | custom-call | flops 402653184 | bytes 3000000 | tf_op jit(solution)/shard_map/window/pallas_call | solution.py:143
  127.0 0.0 all-to-all-done.1
  127.0 1.1 features.1.own_ref
  128.2 3.7 %collective-permute-start.5 = (bf16[256,512]{1,0:T(8,128)(2,1)S(1)}, bf16[256,512]{1,0:T(8,128)(2,1)S(1)}, u32[]{:S(2)}, u32[]{:S(2)}) collective-permute-start(bf16[256,512]{1,0:T(8,128)(2,1)S(1)} %features.1.own_ref), channel_id=1, source_target_pairs={{0,1},{1,0},{2,3},{3,2},{4,5},{5,4},{6,7},{7,6},{8,9},{9,8},{10,11... | collective-permute-start | bytes 786440 | tf_op jit(solution)/shard_map/ppermute | solution.py:371
  131.9 2.3 %own_project.1.own_ref = f32[256,2048]{1,0:T(8,128)S(1)} custom-call(bf16[256,512]{1,0:T(8,128)(2,1)S(1)} %features.1.own_ref, bf16[512,2048]{1,0:T(8,128)(2,1)} %get-tuple-element.16.weight_ref), custom_call_target="tpu_custom_call" | custom-call | flops 536870912 | bytes 4000000 | tf_op jit(solution)/shard_map/own_project/pallas_call | solution.py:242
  134.2 0.0 collective-permute-done.6.weight_ref
  134.2 0.0 collective-permute-done.5.other_ref
  134.2 3.0 %project.1 = bf16[256,2048]{1,0:T(8,128)(2,1)} custom-call(bf16[256,512]{1,0:T(8,128)(2,1)S(1)} %collective-permute-done.5.other_ref, bf16[512,2048]{1,0:T(8,128)(2,1)} %collective-permute-done.6.weight_ref, f32[256,2048]{1,0:T(8,128)S(1)} %own_project.1.own_ref), custom_call_target="tpu_custom_call" | custom-call | flops 536870912 | bytes 6000000 | tf_op jit(solution)/shard_map/project/pallas_call | solution.py:291
  (1 shorter events, 0.0 us)
Async XLA Ops:
  4.9 35.9 %all-to-all-start = ((bf16[96,16,256]{2,1,0:T(8,128)(2,1)}), bf16[96,16,256]{2,1,0:T(8,128)(2,1)S(1)}, u32[]{:S(2)}, u32[]{:S(2)}) async-start(bf16[96,16,256]{2,1,0:T(8,128)(2,1)} %bitcast.8), calls=%async_computation | async-start | bytes 1572864 | tf_op jit(solution)/shard_map/all_to_all | solution.py:355
  40.9 21.2 %collective-permute-start.2 = (f32[16,256]{1,0:T(8,128)S(1)}, f32[16,256]{1,0:T(8,128)S(1)}, u32[]{:S(2)}, u32[]{:S(2)}) collective-permute-start(f32[16,256]{1,0:T(8,128)S(1)} %collect.1.own_ref), channel_id=1, source_target_pairs={{0,192},{192,384},{384,576},{576,0},{1,193},{193,385},{385,577},{5... | collective-permute-start | bytes 49160 | tf_op jit(solution)/shard_map/ppermute | solution.py:26
  50.8 11.4 %collective-permute-start.3 = (f32[16,256]{1,0:T(8,128)S(1)}, f32[16,256]{1,0:T(8,128)S(1)}, u32[]{:S(2)}, u32[]{:S(2)}) collective-permute-start(f32[16,256]{1,0:T(8,128)S(1)} %collect.1.own_ref), channel_id=1, source_target_pairs={{0,384},{192,576},{384,0},{576,192},{1,385},{193,577},{385,1},{577... | collective-permute-start | bytes 49160 | tf_op jit(solution)/shard_map/ppermute | solution.py:26
  58.7 7.5 %collective-permute-start.4 = (f32[16,256]{1,0:T(8,128)S(1)}, f32[16,256]{1,0:T(8,128)S(1)}, u32[]{:S(2)}, u32[]{:S(2)}) collective-permute-start(f32[16,256]{1,0:T(8,128)S(1)} %collect.1.own_ref), channel_id=1, source_target_pairs={{0,576},{192,0},{384,192},{576,384},{1,577},{193,1},{385,193},{577... | collective-permute-start | bytes 49160 | tf_op jit(solution)/shard_map/ppermute | solution.py:26
  67.2 59.8 %all-to-all-start.1 = ((bf16[96,16,256]{2,1,0:T(8,128)(2,1)}), bf16[96,16,256]{2,1,0:T(8,128)(2,1)S(1)}, u32[]{:S(2)}, u32[]{:S(2)}) async-start(bf16[96,16,256]{2,1,0:T(8,128)(2,1)} %refresh.1), calls=%async_computation.1 | async-start | bytes 1572864 | tf_op jit(solution)/shard_map/all_to_all | solution.py:368
  74.5 8.8 %copy-start = (bf16[2,2,256,256]{3,2,1,0:T(8,128)(2,1)S(1)}, bf16[2,2,256,256]{3,2,1,0:T(8,128)(2,1)}, u32[]{:S(2)}) copy-start(bf16[2,2,256,256]{3,2,1,0:T(8,128)(2,1)} %get-tuple-element.11.own_ref) | copy-start | bytes 1572868
  74.5 50.5 %copy-start.1 = (bf16[256,2,256]{2,1,0:T(2,128)(2,1)S(1)}, bf16[256,2,256]{2,1,0:T(2,128)(2,1)}, u32[]{:S(2)}) copy-start(bf16[256,2,256]{2,1,0:T(2,128)(2,1)} %queries_ref.1) | copy-start | bytes 786436
  74.5 50.5 %copy-start.2 = (s32[384]{0:T(512)S(1)}, s32[384]{0:T(512)}, u32[]{:S(2)}) copy-start(s32[384]{0:T(512)} %counts_ref.5) | copy-start | bytes 4612
  78.3 55.9 %collective-permute-start.6 = (bf16[512,2048]{1,0:T(8,128)(2,1)}, bf16[512,2048]{1,0:T(8,128)(2,1)}, u32[]{:S(2)}, u32[]{:S(2)}) collective-permute-start(bf16[512,2048]{1,0:T(8,128)(2,1)} %get-tuple-element.15), channel_id=1, source_target_pairs={{0,1},{1,0},{2,3},{3,2},{4,5},{5,4},{6,7},{7,6},{8,9},{9,8},{10,11... | collective-permute-start | bytes 6291464 | tf_op jit(solution)/shard_map/ppermute | solution.py:359
  83.3 23.1 %collective-permute-start = (bf16[2,2,256,256]{3,2,1,0:T(8,128)(2,1)S(1)}, bf16[2,2,256,256]{3,2,1,0:T(8,128)(2,1)S(1)}, u32[]{:S(2)}, u32[]{:S(2)}) collective-permute-start(bf16[2,2,256,256]{3,2,1,0:T(8,128)(2,1)S(1)} %copy-done), channel_id=1, source_target_pairs={{0,2},{2,4},{4,6},{6,8},{8,10},{10,12},{12,14},{14,16},{16,18},{18... | collective-permute-start | bytes 1572872 | tf_op jit(solution)/shard_map/ppermute | solution.py:22
  106.4 18.7 %collective-permute-start.1 = (bf16[2,2,256,256]{3,2,1,0:T(8,128)(2,1)S(1)}, bf16[2,2,256,256]{3,2,1,0:T(8,128)(2,1)S(1)}, u32[]{:S(2)}, u32[]{:S(2)}) collective-permute-start(bf16[2,2,256,256]{3,2,1,0:T(8,128)(2,1)S(1)} %collective-permute-done.near_ref), channel_id=1, source_target_pairs={{0,2},{2,4},{4,6},{6,8},{8,10},{10,12},{12,14},{14,16},{16,18},{18... | collective-permute-start | bytes 1572872 | tf_op jit(solution)/shard_map/ppermute | solution.py:22
  128.2 6.0 %collective-permute-start.5 = (bf16[256,512]{1,0:T(8,128)(2,1)S(1)}, bf16[256,512]{1,0:T(8,128)(2,1)S(1)}, u32[]{:S(2)}, u32[]{:S(2)}) collective-permute-start(bf16[256,512]{1,0:T(8,128)(2,1)S(1)} %features.1.own_ref), channel_id=1, source_target_pairs={{0,1},{1,0},{2,3},{3,2},{4,5},{5,4},{6,7},{7,6},{8,9},{9,8},{10,11... | collective-permute-start | bytes 786440 | tf_op jit(solution)/shard_map/ppermute | solution.py:371

commit v7 on v6

--- a/solution.py
+++ b/solution.py
@@ -10,6 +10,7 @@
 
 
 RING = 4
+TILES = 4
 CTX = ("z", "p")
 VMEM = pl.BlockSpec(memory_space=pltpu.VMEM)
 SMEM = pl.BlockSpec(memory_space=pltpu.SMEM)
@@ -20,10 +21,6 @@
 def passed_along(value, steps):
     count = lax.axis_size(CTX)
     return lax.ppermute(value, CTX, [(source, source + steps) for source in range(count - steps)])
-
-
-def turned(value, steps):
-    return lax.ppermute(value, "z", [(place, (place + steps) % RING) for place in range(RING)])
 
 
 def product(left, right, left_dim, right_dim):
@@ -190,29 +187,26 @@
 
 
 def split_kernel(place_ref, mine_in_ref, theirs_in_ref, mine_ref, theirs_ref):
-    mine_ref[...] = mine_in_ref[...]
-    theirs_ref[...] = theirs_in_ref[...]
+    mine_ref[0] = mine_in_ref[...]
+    theirs_ref[0] = theirs_in_ref[...]
 
 
 def column_halves(head_place, out_weight):
     depth, columns = out_weight.shape
-    half = columns // 2
-    tile = half // 2
-    piece = jax.ShapeDtypeStruct((depth, half), out_weight.dtype)
+    tile = columns // 2 // TILES
+    piece = jax.ShapeDtypeStruct((TILES, depth, tile), out_weight.dtype)
+    out_spec = pl.BlockSpec((1, depth, tile), lambda step, place: (step, 0, 0))
     return pl.pallas_call(
         split_kernel,
         out_shape=(piece, piece),
         grid_spec=pltpu.PrefetchScalarGridSpec(
             num_scalar_prefetch=1,
-            grid=(half // tile,),
+            grid=(TILES,),
             in_specs=[
-                pl.BlockSpec((depth, tile), lambda step, place: (0, place[0] * 2 + step)),
-                pl.BlockSpec((depth, tile), lambda step, place: (0, (1 - place[0]) * 2 + step)),
+                pl.BlockSpec((depth, tile), lambda step, place: (0, place[0] * TILES + step)),
+                pl.BlockSpec((depth, tile), lambda step, place: (0, (1 - place[0]) * TILES + step)),
             ],
-            out_specs=(
-                pl.BlockSpec((depth, tile), lambda step, place: (0, step)),
-                pl.BlockSpec((depth, tile), lambda step, place: (0, step)),
-            ),
+            out_specs=(out_spec, out_spec),
         ),
         name="split",
         cost_estimate=pl.CostEstimate(flops=0, transcendentals=0, bytes_accessed=8000000),
@@ -220,16 +214,14 @@
 
 
 def own_project_kernel(own_ref, weight_ref, out_ref, held_weight, sems):
-    tiles, _, tile = held_weight.shape
     fetches = [
-        pltpu.make_async_copy(
-            weight_ref.at[:, step * tile : (step + 1) * tile], held_weight.at[step], sems.at[step]
-        )
-        for step in range(tiles)
+        pltpu.make_async_copy(weight_ref.at[step], held_weight.at[step], sems.at[step])
+        for step in range(TILES)
     ]
     for fetch in fetches:
         fetch.start()
-    for step in range(tiles):
+    tile = held_weight.shape[2]
+    for step in range(TILES):
         fetches[step].wait()
         out_ref[:, step * tile : (step + 1) * tile] = jnp.dot(
             own_ref[...], held_weight[step], preferred_element_type=jnp.float32
@@ -237,17 +229,12 @@
 
 
 def own_projected(own, weight):
-    depth, columns = weight.shape
-    tiles = 4
     return pl.pallas_call(
         own_project_kernel,
-        out_shape=jax.ShapeDtypeStruct((own.shape[0], columns), jnp.float32),
+        out_shape=jax.ShapeDtypeStruct((own.shape[0], TILES * weight.shape[2]), jnp.float32),
         in_specs=[VMEM, pl.BlockSpec(memory_space=pl.ANY)],
         out_specs=VMEM,
-        scratch_shapes=[
-            pltpu.VMEM((tiles, depth, columns // tiles), jnp.bfloat16),
-            pltpu.SemaphoreType.DMA((tiles,)),
-        ],
+        scratch_shapes=[pltpu.VMEM(weight.shape, jnp.bfloat16), pltpu.SemaphoreType.DMA((TILES,))],
         name="own_project",
         compiler_params=pltpu.CompilerParams(vmem_limit_bytes=VMEM_BYTES),
         cost_estimate=pl.CostEstimate(
@@ -257,18 +244,15 @@
 
 
 def project_kernel(other_ref, weight_ref, own_ref, out_ref, held_weight, held_out, sems):
-    tiles = held_out.shape[0]
-    tile = held_out.shape[2]
     fetches = [
-        pltpu.make_async_copy(
-            weight_ref.at[:, step * tile : (step + 1) * tile], held_weight.at[step], sems.at[0, step]
-        )
-        for step in range(tiles)
+        pltpu.make_async_copy(weight_ref.at[step], held_weight.at[step], sems.at[0, step])
+        for step in range(TILES)
     ]
     for fetch in fetches:
         fetch.start()
+    tile = held_weight.shape[2]
     stores = []
-    for step in range(tiles):
+    for step in range(TILES):
         columns = slice(step * tile, (step + 1) * tile)
         fetches[step].wait()
         held_out[step] = (
@@ -284,36 +268,35 @@
 
 
 def projected(other, weight, own_product):
-    tokens, depth = other.shape
-    columns = weight.shape[1]
-    tiles = 4
-    tile = columns // tiles
+    tokens = other.shape[0]
+    tile = weight.shape[2]
     return pl.pallas_call(
         project_kernel,
-        out_shape=jax.ShapeDtypeStruct((tokens, columns), jnp.bfloat16),
+        out_shape=jax.ShapeDtypeStruct((tokens, TILES * tile), jnp.bfloat16),
         in_specs=[VMEM, pl.BlockSpec(memory_space=pl.ANY), VMEM],
         out_specs=pl.BlockSpec(memory_space=pl.ANY),
         scratch_shapes=[
-            pltpu.VMEM((tiles, depth, tile), jnp.bfloat16),
-            pltpu.VMEM((tiles, tokens, tile), jnp.bfloat16),
-            pltpu.SemaphoreType.DMA((2, tiles)),
+            pltpu.VMEM(weight.shape, jnp.bfloat16),
+            pltpu.VMEM((TILES, tokens, tile), jnp.bfloat16),
+            pltpu.SemaphoreType.DMA((2, TILES)),
         ],
         name="project",
         compiler_params=pltpu.CompilerParams(vmem_limit_bytes=VMEM_BYTES),
         cost_estimate=pl.CostEstimate(
-            flops=2 * tokens * depth * columns, transcendentals=0, bytes_accessed=6000000
+            flops=2 * tokens * weight.size, transcendentals=0, bytes_accessed=6000000
         ),
     )(other, weight, own_product)
 
 
 def collect_kernel(blocks_ref, sums_ref):
-    sums_ref[...] = jnp.sum(blocks_ref[...].astype(jnp.float32), axis=0)
-
-
-def collected(blocks):
+    total = jnp.sum(blocks_ref[...].astype(jnp.float32), axis=0)
+    sums_ref[...] = jnp.broadcast_to(total[None], sums_ref.shape)
+
+
+def collected(copies, blocks):
     return pl.pallas_call(
         collect_kernel,
-        out_shape=jax.ShapeDtypeStruct(blocks.shape[1:], jnp.float32),
+        out_shape=jax.ShapeDtypeStruct((copies, *blocks.shape[1:]), jnp.float32),
         in_specs=[VMEM],
         out_specs=VMEM,
         name="collect",
@@ -322,8 +305,8 @@
     )(blocks)
 
 
-def refresh_kernel(total, own_ref, behind_ref, opposite_ref, ahead_ref, old_ref, rows_ref):
-    gradient = (own_ref[...] + opposite_ref[...]) + (behind_ref[...] + ahead_ref[...])
+def refresh_kernel(total, sums_ref, old_ref, rows_ref):
+    gradient = jnp.sum(sums_ref[...], axis=0)
     old = old_ref[...]
     updated = old - gradient / math.sqrt(total)
     old_norm = jnp.sqrt(jnp.sum(old * old, axis=1, keepdims=True))
@@ -331,16 +314,16 @@
     rows_ref[...] = jnp.broadcast_to(fresh.astype(jnp.bfloat16)[None], rows_ref.shape)
 
 
-def refreshed(total, copies, parts, old_rows):
+def refreshed(total, copies, sums, old_rows):
     return pl.pallas_call(
         functools.partial(refresh_kernel, total),
         out_shape=jax.ShapeDtypeStruct((copies, *old_rows.shape), jnp.bfloat16),
-        in_specs=[VMEM] * (RING + 1),
+        in_specs=[VMEM, VMEM],
         out_specs=VMEM,
         name="refresh",
         compiler_params=pltpu.CompilerParams(vmem_limit_bytes=VMEM_BYTES),
         cost_estimate=pl.CostEstimate(flops=100000, transcendentals=0, bytes_accessed=1000000),
-    )(*parts, old_rows)
+    )(sums, old_rows)
 
 
 def shards(queries, token_keys, token_values, step_rates, counts, fast_weights, out_weight):
@@ -357,14 +340,13 @@
         head_place.reshape(1).astype(jnp.int32), out_weight
     )
     out_other = lax.ppermute(out_theirs, "head", [(0, 1), (1, 0)])
-    parts = [collected(blocks)]
-    for steps in range(1, RING):
-        parts.append(turned(parts[0], steps))
+    sums = collected(RING, blocks)
+    sums = lax.all_to_all(sums, "z", 0, 0, tiled=True)
     far = passed_along(near, 1)
     old_flat = fast_weights.reshape(-1, head_width)
     own_rows = old_flat.shape[0] // plane_count
     old_rows = lax.dynamic_slice_in_dim(old_flat, plane_place * own_rows, own_rows, 0)
-    new_rows = refreshed(tok_rows * device_count, plane_count, parts, old_rows)
+    new_rows = refreshed(tok_rows * device_count, plane_count, sums, old_rows)
     new_flat = lax.all_to_all(new_rows, "p", 0, 0, tiled=True).reshape(-1, head_width)
     window, turned_queries = window_attention(place, counts, queries, pairs, near, far)
     features = features_of(place, counts, turned_queries, window, new_flat)

time: 138 us -> 136 us (0.986)
  blocking collectives: 0 us -> 35.9 us
  starting transfers between devices: 54.7 us -> 34.5 us
  waiting for transfers between devices: 63.3 us -> 44.6 us
  Pallas kernels: 18.3 us -> 20 us
    all_to_all x0 -> x1, blocking collectives: none -> 35.9 us  [shards(): lax.all_to_all(local_grad.reshape(plane_count, -1, head_width), 'p', 0, 0...]
    ppermute x3 -> x0, starting transfers between devices: 20.5 us -> none  [turned(): lax.ppermute(value, 'z', [(place, (place + steps) % RING) for place in ra...]
    all_to_all x1, waiting for transfers between devices: 22.6 us -> 8.56 us  [shards(): sums = lax.all_to_all(sums, 'z', 0, 0, tiled=True)]
    ppermute x3 -> x0, waiting for transfers between devices: 4.05 us -> none  [turned(): lax.ppermute(value, 'z', [(place, (place + steps) % RING) for place in ra...]
    all_to_all x1, starting transfers between devices: 7.28 us -> 8.67 us  [shards(): lax.all_to_all(new_rows, 'p', 0, 0, tiled=True).reshape(-1, head_width)]
  transfers between devices with their start and end apart: 9 -> 6, of which waited for: 4 -> 3; matrix products, arithmetic and copies ran while one was open for 1% -> 1% of each run, Pallas kernels for 7% -> 8%
where the time goes in v7:
time: 136 us
  waiting for transfers between devices  44.6 us (33%)
  blocking collectives  35.9 us (26%)
  starting transfers between devices  34.5 us (25%)
  Pallas kernels  20 us (15%)
    ppermute x2, waiting for transfers between devices, passed_along(): lax.ppermute(value, CTX, [(source, source + steps) for source in range(co...  36 us
    all_to_all x1, blocking collectives, shards(): lax.all_to_all(local_grad.reshape(plane_count, -1, head_width), 'p', 0, 0...  35.9 us
    all_to_all x1, starting transfers between devices, shards(): sums = lax.all_to_all(sums, 'z', 0, 0, tiled=True)  12.2 us
    all_to_all x1, starting transfers between devices, shards(): lax.all_to_all(new_rows, 'p', 0, 0, tiled=True).reshape(-1, head_width)  8.67 us
    all_to_all x1, waiting for transfers between devices, shards(): sums = lax.all_to_all(sums, 'z', 0, 0, tiled=True)  8.56 us
    ppermute x2, starting transfers between devices, passed_along(): lax.ppermute(value, CTX, [(source, source + steps) for source in range(co...  5.01 us
    ppermute x1, starting transfers between devices, shards(): out_other = lax.ppermute(out_theirs, 'head', [(0, 1), (1, 0)])  4.98 us
    pallas_call x1, Pallas kernels, local_gradient(): pl.pallas_call(gradient_kernel, out_shape=(jax.ShapeDtypeStruct((heads *...  4.86 us
  transfers between devices with their start and end apart: 6, of which 3 were waited for; matrix products, arithmetic and copies ran while one was open for 1% of the time, Pallas kernels for 8%

profile of v7, /device:TPU:65, one launch (start us, length us, event | category | flops | bytes accessed | tf_op | source)
XLA Modules:
  0.0 135.8 jit_solution(13168210929080844043)
XLA Ops:
  0.0 4.9 %gradient.1 = (bf16[1536,256]{1,0:T(8,128)(2,1)}, bf16[2,2,256,256]{3,2,1,0:T(8,128)(2,1)}) custom-call(s32[1]{0:T(128)} %bitcast.place_ref, s32[384]{0:T(512)} %counts_ref.5, bf16[256,2,256]{2,1,0:T(2,128)(2,1)} %keys_ref.1, bf16[256,2,256]{2,1,0:T(2,128)(2,1)} %values_ref.1, f32[2,256]{1,0:T(2,128)} %bitcast.9, f32[2,3,256,256]{3,2,1,0:T(8,128)} %weights_ref.1), custom_call_target="tpu_custom_call" | custom-call | flops 469762048 | bytes 3000000 | tf_op jit(solution)/shard_map/gradient/pallas_call | solution.py:85
  4.9 35.9 %all_to_all.15.blocks_ref = bf16[96,16,256]{2,1,0:T(8,128)(2,1)S(1)} all-to-all(bf16[96,16,256]{2,1,0:T(8,128)(2,1)} %bitcast.8), channel_id=1, replica_groups=mesh['z'=4,'p'=96,'head'=2] {'p'}, dimensions={0} | all-to-all | bytes 1572864 | tf_op jit(solution)/shard_map/all_to_all | solution.py:338
  40.7 0.8 collect.1
  41.5 12.2 %all-to-all-start.1 = ((f32[4,16,256]{2,1,0:T(8,128)}), f32[4,16,256]{2,1,0:T(8,128)S(1)}, u32[]{:S(2)}, u32[]{:S(2)}) async-start(f32[4,16,256]{2,1,0:T(8,128)} %collect.1), calls=%async_computation.1 | async-start | bytes 131072 | tf_op jit(solution)/shard_map/all_to_all | solution.py:344
  53.7 0.7 constant_dynamic-slice_fusion.old_ref
  54.4 8.6 %all-to-all-done.1.sums_ref = f32[4,16,256]{2,1,0:T(8,128)S(1)} async-done(((f32[4,16,256]{2,1,0:T(8,128)}), f32[4,16,256]{2,1,0:T(8,128)S(1)}, u32[]{:S(2)}, u32[]{:S(2)}) %all-to-all-start.1) | async-done | bytes 65568 | tf_op jit(solution)/shard_map/all_to_all | solution.py:344
  63.0 1.0 refresh.1
  64.0 8.7 %all-to-all-start.2 = ((bf16[96,16,256]{2,1,0:T(8,128)(2,1)}), bf16[96,16,256]{2,1,0:T(8,128)(2,1)S(1)}, u32[]{:S(2)}, u32[]{:S(2)}) async-start(bf16[96,16,256]{2,1,0:T(8,128)(2,1)} %refresh.1), calls=%async_computation.2 | async-start | bytes 1572864 | tf_op jit(solution)/shard_map/all_to_all | solution.py:350
  72.7 0.0 copy-start
  72.7 0.0 copy-start.1
  72.7 0.0 copy-start.2
  72.7 4.8 %split.1 = (bf16[4,512,512]{2,1,0:T(8,128)(2,1)}, bf16[4,512,512]{2,1,0:T(8,128)(2,1)}) custom-call(s32[1]{0:T(128)} %bitcast.5.place_ref, bf16[512,4096]{1,0:T(8,128)(2,1)} %theirs_in_ref.1, bf16[512,4096]{1,0:T(8,128)(2,1)} %theirs_in_ref.1), custom_call_target="tpu_custom_call" | custom-call | bytes 8000000 | tf_op jit(solution)/shard_map/split/pallas_call | solution.py:199
  77.5 5.0 %collective-permute-start.3 = (bf16[4,512,512]{2,1,0:T(8,128)(2,1)}, bf16[4,512,512]{2,1,0:T(8,128)(2,1)}, u32[]{:S(2)}, u32[]{:S(2)}) collective-permute-start(bf16[4,512,512]{2,1,0:T(8,128)(2,1)} %get-tuple-element.15), channel_id=1, source_target_pairs={{0,1},{1,0},{2,3},{3,2},{4,5},{5,4},{6,7},{7,6},{8,9},{9,8},{10,11... | collective-permute-start | bytes 6291464 | tf_op jit(solution)/shard_map/ppermute | solution.py:342
  82.5 0.0 copy-done
  82.5 3.1 %collective-permute-start = (bf16[2,2,256,256]{3,2,1,0:T(8,128)(2,1)S(1)}, bf16[2,2,256,256]{3,2,1,0:T(8,128)(2,1)S(1)}, u32[]{:S(2)}, u32[]{:S(2)}) collective-permute-start(bf16[2,2,256,256]{3,2,1,0:T(8,128)(2,1)S(1)} %copy-done), channel_id=1, source_target_pairs={{0,2},{2,4},{4,6},{6,8},{8,10},{10,12},{12,14},{14,16},{16,18},{18... | collective-permute-start | bytes 1572872 | tf_op jit(solution)/shard_map/ppermute | solution.py:23
  85.6 19.2 %collective-permute-done.near_ref = bf16[2,2,256,256]{3,2,1,0:T(8,128)(2,1)S(1)} collective-permute-done((bf16[2,2,256,256]{3,2,1,0:T(8,128)(2,1)S(1)}, bf16[2,2,256,256]{3,2,1,0:T(8,128)(2,1)S(1)}, u32[]{:S(2)}, u32[]{:S(2)}) %collective-permute-start) | collective-permute-done | bytes 524320 | tf_op jit(solution)/shard_map/ppermute | solution.py:23
  104.9 1.9 %collective-permute-start.1 = (bf16[2,2,256,256]{3,2,1,0:T(8,128)(2,1)S(1)}, bf16[2,2,256,256]{3,2,1,0:T(8,128)(2,1)S(1)}, u32[]{:S(2)}, u32[]{:S(2)}) collective-permute-start(bf16[2,2,256,256]{3,2,1,0:T(8,128)(2,1)S(1)} %collective-permute-done.near_ref), channel_id=1, source_target_pairs={{0,2},{2,4},{4,6},{6,8},{8,10},{10,12},{12,14},{14,16},{16,18},{18... | collective-permute-start | bytes 1572872 | tf_op jit(solution)/shard_map/ppermute | solution.py:23
  106.8 16.7 %collective-permute-done.1.far_ref = bf16[2,2,256,256]{3,2,1,0:T(8,128)(2,1)S(1)} collective-permute-done((bf16[2,2,256,256]{3,2,1,0:T(8,128)(2,1)S(1)}, bf16[2,2,256,256]{3,2,1,0:T(8,128)(2,1)S(1)}, u32[]{:S(2)}, u32[]{:S(2)}) %collective-permute-start.1) | collective-permute-done | bytes 524320 | tf_op jit(solution)/shard_map/ppermute | solution.py:23
  123.5 0.0 copy-done.1
  123.5 0.0 copy-done.2
  123.5 2.0 %window.1 = (f32[256,512]{1,0:T(8,128)S(1)}, bf16[2,256,256]{2,1,0:T(8,128)(2,1)S(1)}) custom-call(s32[1]{0:T(128)} %bitcast.place_ref, s32[384]{0:T(512)S(1)} %copy-done.2, bf16[256,2,256]{2,1,0:T(2,128)(2,1)S(1)} %copy-done.1, bf16[2,2,256,256]{3,2,1,0:T(8,128)(2,1)S(1)} %copy-done, bf16[2,2,256,256]{3,2,1,0:T(8,128)(2,1)S(1)} %collective-permute-done.near_ref, ...), custom_call_target="tpu_custom_call" | custom-call | flops 402653184 | bytes 3000000 | tf_op jit(solution)/shard_map/window/pallas_call | solution.py:140
  125.6 0.0 all-to-all-done.2
  125.6 1.1 features.1.own_ref
  126.7 3.7 %collective-permute-start.2 = (bf16[256,512]{1,0:T(8,128)(2,1)S(1)}, bf16[256,512]{1,0:T(8,128)(2,1)S(1)}, u32[]{:S(2)}, u32[]{:S(2)}) collective-permute-start(bf16[256,512]{1,0:T(8,128)(2,1)S(1)} %features.1.own_ref), channel_id=1, source_target_pairs={{0,1},{1,0},{2,3},{3,2},{4,5},{5,4},{6,7},{7,6},{8,9},{9,8},{10,11... | collective-permute-start | bytes 786440 | tf_op jit(solution)/shard_map/ppermute | solution.py:353
  130.4 2.3 %own_project.1.own_ref = f32[256,2048]{1,0:T(8,128)S(1)} custom-call(bf16[256,512]{1,0:T(8,128)(2,1)S(1)} %features.1.own_ref, bf16[4,512,512]{2,1,0:T(8,128)(2,1)} %get-tuple-element.16.weight_ref), custom_call_target="tpu_custom_call" | custom-call | flops 536870912 | bytes 4000000 | tf_op jit(solution)/shard_map/own_project/pallas_call | solution.py:232
  132.7 0.0 collective-permute-done.3.weight_ref
  132.7 0.0 collective-permute-done.2.other_ref
  132.7 3.0 %project.1 = bf16[256,2048]{1,0:T(8,128)(2,1)} custom-call(bf16[256,512]{1,0:T(8,128)(2,1)S(1)} %collective-permute-done.2.other_ref, bf16[4,512,512]{2,1,0:T(8,128)(2,1)} %collective-permute-done.3.weight_ref, f32[256,2048]{1,0:T(8,128)S(1)} %own_project.1.own_ref), custom_call_target="tpu_custom_call" | custom-call | flops 536870912 | bytes 6000000 | tf_op jit(solution)/shard_map/project/pallas_call | solution.py:273
Async XLA Ops:
  41.5 21.5 %all-to-all-start.1 = ((f32[4,16,256]{2,1,0:T(8,128)}), f32[4,16,256]{2,1,0:T(8,128)S(1)}, u32[]{:S(2)}, u32[]{:S(2)}) async-start(f32[4,16,256]{2,1,0:T(8,128)} %collect.1), calls=%async_computation.1 | async-start | bytes 131072 | tf_op jit(solution)/shard_map/all_to_all | solution.py:344
  64.0 61.5 %all-to-all-start.2 = ((bf16[96,16,256]{2,1,0:T(8,128)(2,1)}), bf16[96,16,256]{2,1,0:T(8,128)(2,1)S(1)}, u32[]{:S(2)}, u32[]{:S(2)}) async-start(bf16[96,16,256]{2,1,0:T(8,128)(2,1)} %refresh.1), calls=%async_computation.2 | async-start | bytes 1572864 | tf_op jit(solution)/shard_map/all_to_all | solution.py:350
  72.7 9.8 %copy-start = (bf16[2,2,256,256]{3,2,1,0:T(8,128)(2,1)S(1)}, bf16[2,2,256,256]{3,2,1,0:T(8,128)(2,1)}, u32[]{:S(2)}) copy-start(bf16[2,2,256,256]{3,2,1,0:T(8,128)(2,1)} %get-tuple-element.11.own_ref) | copy-start | bytes 1572868
  72.7 50.8 %copy-start.1 = (bf16[256,2,256]{2,1,0:T(2,128)(2,1)S(1)}, bf16[256,2,256]{2,1,0:T(2,128)(2,1)}, u32[]{:S(2)}) copy-start(bf16[256,2,256]{2,1,0:T(2,128)(2,1)} %queries_ref.1) | copy-start | bytes 786436
  72.7 50.8 %copy-start.2 = (s32[384]{0:T(512)S(1)}, s32[384]{0:T(512)}, u32[]{:S(2)}) copy-start(s32[384]{0:T(512)} %counts_ref.5) | copy-start | bytes 4612
  77.5 55.2 %collective-permute-start.3 = (bf16[4,512,512]{2,1,0:T(8,128)(2,1)}, bf16[4,512,512]{2,1,0:T(8,128)(2,1)}, u32[]{:S(2)}, u32[]{:S(2)}) collective-permute-start(bf16[4,512,512]{2,1,0:T(8,128)(2,1)} %get-tuple-element.15), channel_id=1, source_target_pairs={{0,1},{1,0},{2,3},{3,2},{4,5},{5,4},{6,7},{7,6},{8,9},{9,8},{10,11... | collective-permute-start | bytes 6291464 | tf_op jit(solution)/shard_map/ppermute | solution.py:342
  82.5 22.3 %collective-permute-start = (bf16[2,2,256,256]{3,2,1,0:T(8,128)(2,1)S(1)}, bf16[2,2,256,256]{3,2,1,0:T(8,128)(2,1)S(1)}, u32[]{:S(2)}, u32[]{:S(2)}) collective-permute-start(bf16[2,2,256,256]{3,2,1,0:T(8,128)(2,1)S(1)} %copy-done), channel_id=1, source_target_pairs={{0,2},{2,4},{4,6},{6,8},{8,10},{10,12},{12,14},{14,16},{16,18},{18... | collective-permute-start | bytes 1572872 | tf_op jit(solution)/shard_map/ppermute | solution.py:23
  104.9 18.7 %collective-permute-start.1 = (bf16[2,2,256,256]{3,2,1,0:T(8,128)(2,1)S(1)}, bf16[2,2,256,256]{3,2,1,0:T(8,128)(2,1)S(1)}, u32[]{:S(2)}, u32[]{:S(2)}) collective-permute-start(bf16[2,2,256,256]{3,2,1,0:T(8,128)(2,1)S(1)} %collective-permute-done.near_ref), channel_id=1, source_target_pairs={{0,2},{2,4},{4,6},{6,8},{8,10},{10,12},{12,14},{14,16},{16,18},{18... | collective-permute-start | bytes 1572872 | tf_op jit(solution)/shard_map/ppermute | solution.py:23
  126.7 6.0 %collective-permute-start.2 = (bf16[256,512]{1,0:T(8,128)(2,1)S(1)}, bf16[256,512]{1,0:T(8,128)(2,1)S(1)}, u32[]{:S(2)}, u32[]{:S(2)}) collective-permute-start(bf16[256,512]{1,0:T(8,128)(2,1)S(1)} %features.1.own_ref), channel_id=1, source_target_pairs={{0,1},{1,0},{2,3},{3,2},{4,5},{5,4},{6,7},{7,6},{8,9},{9,8},{10,11... | collective-permute-start | bytes 786440 | tf_op jit(solution)/shard_map/ppermute | solution.py:353

commit v8 on v7

--- a/solution.py
+++ b/solution.py
@@ -23,6 +23,10 @@
     return lax.ppermute(value, CTX, [(source, source + steps) for source in range(count - steps)])
 
 
+def resting(value):
+    return pltpu.with_memory_space_constraint(value, pltpu.MemorySpace.HBM)
+
+
 def product(left, right, left_dim, right_dim):
     return lax.dot_general(
         left,
@@ -38,74 +42,112 @@
 
 
 def gradient_kernel(
-    place_ref, counts_ref, keys_ref, values_ref, rates_ref, weights_ref, grad_ref, pairs_ref
+    place_ref,
+    counts_ref,
+    rates_ref,
+    keys_ref,
+    values_ref,
+    weights_ref,
+    grad_ref,
+    pairs_ref,
+    held_keys,
+    held_values,
+    held_weights,
+    held_grad,
+    held_pairs,
+    load_sems,
+    store_sems,
 ):
-    tokens, heads, width = keys_ref.shape
-
-    def one_head(head):
-        valid = lax.broadcasted_iota(jnp.int32, (tokens, 1), 0) < place_count(
-            counts_ref, place_ref, 0
+    tokens, heads, width = held_keys.shape
+    mats = held_weights.shape[1]
+
+    def weight_load(head, index):
+        return pltpu.make_async_copy(
+            weights_ref.at[head, index],
+            held_weights.at[head, index],
+            load_sems.at[2 + head * mats + index],
         )
-        rates_all = jnp.concatenate(
-            [rates_ref[...], jnp.zeros((8 - heads, tokens), jnp.float32)], 0
-        ).T
-        keys, values = keys_ref[:, head, :], values_ref[:, head, :]
-        pairs_ref[0, 0] = keys
-        pairs_ref[1, 0] = values
+
+    keys_load = pltpu.make_async_copy(keys_ref, held_keys, load_sems.at[0])
+    values_load = pltpu.make_async_copy(values_ref, held_values, load_sems.at[1])
+    keys_load.start()
+    weight_load(0, 0).start()
+    weight_load(0, 1).start()
+    values_load.start()
+    weight_load(0, 2).start()
+    for head in range(1, heads):
+        for index in range(mats):
+            weight_load(head, index).start()
+    valid = lax.broadcasted_iota(jnp.int32, (tokens, 1), 0) < place_count(counts_ref, place_ref, 0)
+    rates_all = jnp.concatenate(
+        [rates_ref[...], jnp.zeros((8 - heads, tokens), jnp.float32)], 0
+    ).T
+    stores = []
+
+    def store(source, target):
+        stores.append(pltpu.make_async_copy(source, target, store_sems.at[len(stores)]))
+        stores[-1].start()
+
+    keys_load.wait()
+    head_keys = []
+    for head in range(heads):
+        head_keys.append(held_keys[:, head, :])
+        held_pairs[0, head] = head_keys[head]
+        store(held_pairs.at[0, head], pairs_ref.at[0, head])
+    for head in range(heads):
+        keys = head_keys[head]
+        weight_load(head, 0).wait()
+        gate_pre = product(keys, held_weights[head, 0].astype(jnp.bfloat16), 1, 1)
+        weight_load(head, 1).wait()
+        up_pre = product(keys, held_weights[head, 1].astype(jnp.bfloat16), 1, 1)
+        if head == 0:
+            values_load.wait()
+        values = held_values[:, head, :]
+        held_pairs[1, head] = values
+        store(held_pairs.at[1, head], pairs_ref.at[1, head])
         rates = jnp.where(valid, rates_all[:, head : head + 1], 0.0)
         scaled = (rates * values.astype(jnp.float32)).astype(jnp.bfloat16)
-        gate_weight = weights_ref[0, 0].astype(jnp.bfloat16)
-        up_weight = weights_ref[0, 1].astype(jnp.bfloat16)
-        down_weight = weights_ref[0, 2].astype(jnp.bfloat16)
-        gate_pre = product(keys, gate_weight, 1, 1)
-        up_pre = product(keys, up_weight, 1, 1)
-        back = -product(scaled, down_weight, 1, 0)
+        weight_load(head, 2).wait()
+        back = -product(scaled, held_weights[head, 2].astype(jnp.bfloat16), 1, 0)
         sigmoid = jax.nn.sigmoid(gate_pre)
         gate_act = gate_pre * sigmoid
         hidden = (gate_act * up_pre).astype(jnp.bfloat16)
         slope = sigmoid * (1.0 + gate_pre * (1.0 - sigmoid))
         grad_gate = (back * up_pre * slope).astype(jnp.bfloat16)
         grad_up = (back * gate_act).astype(jnp.bfloat16)
-        mats = (
-            product(grad_gate, keys, 0, 0),
-            product(grad_up, keys, 0, 0),
-            -product(scaled, hidden, 0, 0),
-        )
-        for index, mat in enumerate(mats):
-            grad_ref[index * width : (index + 1) * width, :] = mat.astype(jnp.bfloat16)
-
-    for head in range(heads):
-        pl.when(pl.program_id(0) == head)(functools.partial(one_head, head))
+        factors = ((grad_gate, keys, 1.0), (grad_up, keys, 1.0), (scaled, hidden, -1.0))
+        for index, (left, right, sign) in enumerate(factors):
+            rows = pl.ds((head * mats + index) * width, width)
+            held_grad[rows] = (sign * product(left, right, 0, 0)).astype(jnp.bfloat16)
+            store(held_grad.at[rows], grad_ref.at[rows])
+    for started in stores:
+        started.wait()
 
 
 def local_gradient(place, counts, token_keys, token_values, step_rates, fast_weights):
     heads, mats, width, _ = fast_weights.shape
-    tokens = token_keys.shape[0]
-    raw = pl.BlockSpec((tokens, heads, width), lambda head: (0, 0, 0))
+    grad = jax.ShapeDtypeStruct((heads * mats * width, width), jnp.bfloat16)
+    pairs = jax.ShapeDtypeStruct((2, heads, token_keys.shape[0], width), jnp.bfloat16)
+    apart = pl.BlockSpec(memory_space=pl.ANY)
     return pl.pallas_call(
         gradient_kernel,
-        out_shape=(
-            jax.ShapeDtypeStruct((heads * mats * width, width), jnp.bfloat16),
-            jax.ShapeDtypeStruct((2, heads, tokens, width), jnp.bfloat16),
-        ),
-        grid=(heads,),
-        in_specs=[
-            SMEM,
-            SMEM,
-            raw,
-            raw,
-            pl.BlockSpec((heads, tokens), lambda head: (0, 0)),
-            pl.BlockSpec((1, mats, width, width), lambda head: (head, 0, 0, 0)),
+        out_shape=(grad, pairs),
+        in_specs=[SMEM, SMEM, VMEM, apart, apart, apart],
+        out_specs=(apart, apart),
+        scratch_shapes=[
+            pltpu.VMEM(token_keys.shape, jnp.bfloat16),
+            pltpu.VMEM(token_values.shape, jnp.bfloat16),
+            pltpu.VMEM(fast_weights.shape, jnp.float32),
+            pltpu.VMEM(grad.shape, jnp.bfloat16),
+            pltpu.VMEM(pairs.shape, jnp.bfloat16),
+            pltpu.SemaphoreType.DMA((2 + heads * mats,)),
+            pltpu.SemaphoreType.DMA(((2 + mats) * heads,)),
         ],
-        out_specs=(
-            pl.BlockSpec((mats * width, width), lambda head: (head, 0)),
-            pl.BlockSpec((2, 1, tokens, width), lambda head: (0, head, 0, 0)),
-        ),
         name="gradient",
         cost_estimate=pl.CostEstimate(
             flops=14 * 256 * width * width * heads, transcendentals=131072, bytes_accessed=3000000
         ),
-    )(place, counts, token_keys, token_values, step_rates.T, fast_weights)
+    )(place, counts, step_rates.T, token_keys, token_values, fast_weights)
 
 
 def window_kernel(place_ref, counts_ref, queries_ref, own_ref, near_ref, far_ref, window_ref, turned_ref):
@@ -155,7 +197,19 @@
     )(place, counts, queries, own, near, far)
 
 
-def feature_kernel(place_ref, counts_ref, queries_ref, window_ref, weights_ref, features_ref):
+def feature_kernel(
+    place_ref,
+    counts_ref,
+    queries_ref,
+    window_ref,
+    weights_ref,
+    own_weight_ref,
+    features_ref,
+    brought_ref,
+    sem,
+):
+    brought = pltpu.make_async_copy(own_weight_ref, brought_ref, sem)
+    brought.start()
     heads, tokens, width = queries_ref.shape
     valid = lax.broadcasted_iota(jnp.int32, (tokens, 1), 0) < place_count(counts_ref, place_ref, 0)
     for head in range(heads):
@@ -169,21 +223,26 @@
         features_ref[:, columns] = jnp.where(
             valid, learned + window_ref[:, columns], 0.0
         ).astype(jnp.bfloat16)
-
-
-def features_of(place, counts, queries, window, new_flat):
+    brought.wait()
+
+
+def features_of(place, counts, queries, window, new_flat, own_weight):
     heads, tokens, width = queries.shape
     return pl.pallas_call(
         feature_kernel,
-        out_shape=jax.ShapeDtypeStruct((tokens, heads * width), jnp.bfloat16),
-        in_specs=[SMEM, SMEM] + [VMEM] * 3,
-        out_specs=VMEM,
+        out_shape=(
+            jax.ShapeDtypeStruct((tokens, heads * width), jnp.bfloat16),
+            jax.ShapeDtypeStruct(own_weight.shape, jnp.bfloat16),
+        ),
+        in_specs=[SMEM, SMEM] + [VMEM] * 3 + [pl.BlockSpec(memory_space=pl.ANY)],
+        out_specs=(VMEM, VMEM),
+        scratch_shapes=[pltpu.SemaphoreType.DMA],
         name="features",
         compiler_params=pltpu.CompilerParams(vmem_limit_bytes=VMEM_BYTES),
         cost_estimate=pl.CostEstimate(
             flops=6 * tokens * width * width * heads, transcendentals=131072, bytes_accessed=2000000
         ),
-    )(place, counts, queries, window, new_flat)
+    )(place, counts, queries, window, new_flat, own_weight)
 
 
 def split_kernel(place_ref, mine_in_ref, theirs_in_ref, mine_ref, theirs_ref):
@@ -213,54 +272,46 @@
     )(head_place, out_weight, out_weight)
 
 
-def own_project_kernel(own_ref, weight_ref, out_ref, held_weight, sems):
-    fetches = [
-        pltpu.make_async_copy(weight_ref.at[step], held_weight.at[step], sems.at[step])
-        for step in range(TILES)
-    ]
-    for fetch in fetches:
-        fetch.start()
-    tile = held_weight.shape[2]
+def own_project_kernel(own_ref, weight_ref, theirs_ref, out_ref, brought_ref, sem):
+    brought = pltpu.make_async_copy(theirs_ref, brought_ref, sem)
+    brought.start()
+    tile = weight_ref.shape[2]
     for step in range(TILES):
-        fetches[step].wait()
         out_ref[:, step * tile : (step + 1) * tile] = jnp.dot(
-            own_ref[...], held_weight[step], preferred_element_type=jnp.float32
+            own_ref[...], weight_ref[step], preferred_element_type=jnp.float32
         )
-
-
-def own_projected(own, weight):
+    brought.wait()
+
+
+def own_projected(own, weight, theirs):
     return pl.pallas_call(
         own_project_kernel,
-        out_shape=jax.ShapeDtypeStruct((own.shape[0], TILES * weight.shape[2]), jnp.float32),
-        in_specs=[VMEM, pl.BlockSpec(memory_space=pl.ANY)],
-        out_specs=VMEM,
-        scratch_shapes=[pltpu.VMEM(weight.shape, jnp.bfloat16), pltpu.SemaphoreType.DMA((TILES,))],
+        out_shape=(
+            jax.ShapeDtypeStruct((own.shape[0], TILES * weight.shape[2]), jnp.float32),
+            jax.ShapeDtypeStruct(theirs.shape, jnp.bfloat16),
+        ),
+        in_specs=[VMEM, VMEM, pl.BlockSpec(memory_space=pl.ANY)],
+        out_specs=(VMEM, VMEM),
+        scratch_shapes=[pltpu.SemaphoreType.DMA],
         name="own_project",
         compiler_params=pltpu.CompilerParams(vmem_limit_bytes=VMEM_BYTES),
         cost_estimate=pl.CostEstimate(
-            flops=2 * own.shape[0] * weight.size, transcendentals=0, bytes_accessed=4000000
-        ),
-    )(own, weight)
-
-
-def project_kernel(other_ref, weight_ref, own_ref, out_ref, held_weight, held_out, sems):
-    fetches = [
-        pltpu.make_async_copy(weight_ref.at[step], held_weight.at[step], sems.at[0, step])
-        for step in range(TILES)
-    ]
-    for fetch in fetches:
-        fetch.start()
-    tile = held_weight.shape[2]
+            flops=2 * own.shape[0] * theirs.size, transcendentals=0, bytes_accessed=4000000
+        ),
+    )(own, weight, theirs)
+
+
+def project_kernel(other_ref, weight_ref, own_ref, out_ref, held_out, sems):
+    tile = held_out.shape[2]
     stores = []
     for step in range(TILES):
         columns = slice(step * tile, (step + 1) * tile)
-        fetches[step].wait()
         held_out[step] = (
             own_ref[:, columns]
-            + jnp.dot(other_ref[...], held_weight[step], preferred_element_type=jnp.float32)
+            + jnp.dot(other_ref[...], weight_ref[step], preferred_element_type=jnp.float32)
         ).astype(jnp.bfloat16)
         stores.append(
-            pltpu.make_async_copy(held_out.at[step], out_ref.at[:, columns], sems.at[1, step])
+            pltpu.make_async_copy(held_out.at[step], out_ref.at[:, columns], sems.at[step])
         )
         stores[step].start()
     for store in stores:
@@ -273,12 +324,11 @@
     return pl.pallas_call(
         project_kernel,
         out_shape=jax.ShapeDtypeStruct((tokens, TILES * tile), jnp.bfloat16),
-        in_specs=[VMEM, pl.BlockSpec(memory_space=pl.ANY), VMEM],
+        in_specs=[VMEM, VMEM, VMEM],
         out_specs=pl.BlockSpec(memory_space=pl.ANY),
         scratch_shapes=[
-            pltpu.VMEM(weight.shape, jnp.bfloat16),
             pltpu.VMEM((TILES, tokens, tile), jnp.bfloat16),
-            pltpu.SemaphoreType.DMA((2, TILES)),
+            pltpu.SemaphoreType.DMA((TILES,)),
         ],
         name="project",
         compiler_params=pltpu.CompilerParams(vmem_limit_bytes=VMEM_BYTES),
@@ -349,14 +399,12 @@
     new_rows = refreshed(tok_rows * device_count, plane_count, sums, old_rows)
     new_flat = lax.all_to_all(new_rows, "p", 0, 0, tiled=True).reshape(-1, head_width)
     window, turned_queries = window_attention(place, counts, queries, pairs, near, far)
-    features = features_of(place, counts, turned_queries, window, new_flat)
+    features, own_weight = features_of(
+        place, counts, turned_queries, window, new_flat, resting(out_own)
+    )
     other = lax.ppermute(features, "head", [(0, 1), (1, 0)])
-    own_product = own_projected(
-        features, pltpu.with_memory_space_constraint(out_own, pltpu.MemorySpace.HBM)
-    )
-    return projected(
-        other, pltpu.with_memory_space_constraint(out_other, pltpu.MemorySpace.HBM), own_product
-    )
+    own_product, brought = own_projected(features, own_weight, resting(out_other))
+    return projected(other, brought, own_product)
 
 
 def solution(mesh):

time: 136 us -> 136 us (level)
    pallas_call x1, Pallas kernels: 3.03 us -> 1.45 us  [projected(): pl.pallas_call(project_kernel, out_shape=jax.ShapeDtypeStruct((tokens, TI...]
    pallas_call x3, Pallas kernels: 8.29 us -> 9.73 us  [the longest x1 5.94 us: local_gradient(): pl.pallas_call(gradient_kernel, out_shape=(grad, pairs), in_specs=[SMEM,...]
where the time goes in v8:
time: 136 us
  waiting for transfers between devices  44.6 us (33%)
  blocking collectives  35.9 us (26%)
  starting transfers between devices  34.6 us (25%)
  Pallas kernels  19.8 us (15%)
    ppermute x2, waiting for transfers between devices, passed_along(): lax.ppermute(value, CTX, [(source, source + steps) for source in range(co...  36 us
    all_to_all x1, blocking collectives, shards(): lax.all_to_all(local_grad.reshape(plane_count, -1, head_width), 'p', 0, 0...  35.9 us
    all_to_all x1, starting transfers between devices, shards(): sums = lax.all_to_all(sums, 'z', 0, 0, tiled=True)  12.2 us
    all_to_all x1, starting transfers between devices, shards(): lax.all_to_all(new_rows, 'p', 0, 0, tiled=True).reshape(-1, head_width)  8.67 us
    all_to_all x1, waiting for transfers between devices, shards(): sums = lax.all_to_all(sums, 'z', 0, 0, tiled=True)  8.56 us
    pallas_call x1, Pallas kernels, local_gradient(): pl.pallas_call(gradient_kernel, out_shape=(grad, pairs), in_specs=[SMEM,...  5.94 us
    ppermute x2, starting transfers between devices, passed_along(): lax.ppermute(value, CTX, [(source, source + steps) for source in range(co...  5.01 us
    ppermute x1, starting transfers between devices, shards(): out_other = lax.ppermute(out_theirs, 'head', [(0, 1), (1, 0)])  4.98 us
  transfers between devices with their start and end apart: 6, of which 3 were waited for; matrix products, arithmetic and copies ran while one was open for 1% of the time, Pallas kernels for 8%

profile of v8, /device:TPU:65, one launch (start us, length us, event | category | flops | bytes accessed | tf_op | source)
XLA Modules:
  0.0 135.7 jit_solution(3213172821465920956)
XLA Ops:
  0.0 5.9 %gradient.1 = (bf16[1536,256]{1,0:T(8,128)(2,1)}, bf16[2,2,256,256]{3,2,1,0:T(8,128)(2,1)}) custom-call(s32[1]{0:T(128)} %bitcast.place_ref, s32[384]{0:T(512)} %counts_ref.5, f32[2,256]{1,0:T(2,128)} %bitcast.9, bf16[256,2,256]{2,1,0:T(2,128)(2,1)} %keys_ref.1, bf16[256,2,256]{2,1,0:T(2,128)(2,1)} %values_ref.1, f32[2,3,256,256]{3,2,1,0:T(8,128)} %weights_ref.1), custom_call_target="tpu_custom_call" | custom-call | flops 469762048 | bytes 3000000 | tf_op jit(solution)/shard_map/gradient/pallas_call | solution.py:132
  5.9 35.9 %all_to_all.15.blocks_ref = bf16[96,16,256]{2,1,0:T(8,128)(2,1)S(1)} all-to-all(bf16[96,16,256]{2,1,0:T(8,128)(2,1)} %bitcast.8), channel_id=1, replica_groups=mesh['z'=4,'p'=96,'head'=2] {'p'}, dimensions={0} | all-to-all | bytes 1572864 | tf_op jit(solution)/shard_map/all_to_all | solution.py:388
  41.8 0.8 collect.1
  42.6 12.2 %all-to-all-start.1 = ((f32[4,16,256]{2,1,0:T(8,128)}), f32[4,16,256]{2,1,0:T(8,128)S(1)}, u32[]{:S(2)}, u32[]{:S(2)}) async-start(f32[4,16,256]{2,1,0:T(8,128)} %collect.1), calls=%async_computation.1 | async-start | bytes 131072 | tf_op jit(solution)/shard_map/all_to_all | solution.py:394
  54.8 0.7 constant_dynamic-slice_fusion.old_ref
  55.5 8.6 %all-to-all-done.1.sums_ref = f32[4,16,256]{2,1,0:T(8,128)S(1)} async-done(((f32[4,16,256]{2,1,0:T(8,128)}), f32[4,16,256]{2,1,0:T(8,128)S(1)}, u32[]{:S(2)}, u32[]{:S(2)}) %all-to-all-start.1) | async-done | bytes 65568 | tf_op jit(solution)/shard_map/all_to_all | solution.py:394
  64.1 1.0 refresh.1
  65.1 8.7 %all-to-all-start.2 = ((bf16[96,16,256]{2,1,0:T(8,128)(2,1)}), bf16[96,16,256]{2,1,0:T(8,128)(2,1)S(1)}, u32[]{:S(2)}, u32[]{:S(2)}) async-start(bf16[96,16,256]{2,1,0:T(8,128)(2,1)} %refresh.1), calls=%async_computation.2 | async-start | bytes 1572864 | tf_op jit(solution)/shard_map/all_to_all | solution.py:400
  73.8 0.0 copy-start
  73.8 0.0 copy-start.1
  73.8 0.0 copy-start.2
  73.8 4.8 %split.1 = (bf16[4,512,512]{2,1,0:T(8,128)(2,1)}, bf16[4,512,512]{2,1,0:T(8,128)(2,1)}) custom-call(s32[1]{0:T(128)} %bitcast.5.place_ref, bf16[512,4096]{1,0:T(8,128)(2,1)} %theirs_in_ref.1, bf16[512,4096]{1,0:T(8,128)(2,1)} %theirs_in_ref.1), custom_call_target="tpu_custom_call" | custom-call | bytes 8000000 | tf_op jit(solution)/shard_map/split/pallas_call | solution.py:258
  78.6 5.0 %collective-permute-start.3 = (bf16[4,512,512]{2,1,0:T(8,128)(2,1)}, bf16[4,512,512]{2,1,0:T(8,128)(2,1)}, u32[]{:S(2)}, u32[]{:S(2)}) collective-permute-start(bf16[4,512,512]{2,1,0:T(8,128)(2,1)} %get-tuple-element.22), channel_id=1, source_target_pairs={{0,1},{1,0},{2,3},{3,2},{4,5},{5,4},{6,7},{7,6},{8,9},{9,8},{10,11... | collective-permute-start | bytes 6291464 | tf_op jit(solution)/shard_map/ppermute | solution.py:392
  83.6 0.0 copy-done
  83.6 3.1 %collective-permute-start = (bf16[2,2,256,256]{3,2,1,0:T(8,128)(2,1)S(1)}, bf16[2,2,256,256]{3,2,1,0:T(8,128)(2,1)S(1)}, u32[]{:S(2)}, u32[]{:S(2)}) collective-permute-start(bf16[2,2,256,256]{3,2,1,0:T(8,128)(2,1)S(1)} %copy-done), channel_id=1, source_target_pairs={{0,2},{2,4},{4,6},{6,8},{8,10},{10,12},{12,14},{14,16},{16,18},{18... | collective-permute-start | bytes 1572872 | tf_op jit(solution)/shard_map/ppermute | solution.py:23
  86.7 19.2 %collective-permute-done.near_ref = bf16[2,2,256,256]{3,2,1,0:T(8,128)(2,1)S(1)} collective-permute-done((bf16[2,2,256,256]{3,2,1,0:T(8,128)(2,1)S(1)}, bf16[2,2,256,256]{3,2,1,0:T(8,128)(2,1)S(1)}, u32[]{:S(2)}, u32[]{:S(2)}) %collective-permute-start) | collective-permute-done | bytes 524320 | tf_op jit(solution)/shard_map/ppermute | solution.py:23
  106.0 1.9 %collective-permute-start.1 = (bf16[2,2,256,256]{3,2,1,0:T(8,128)(2,1)S(1)}, bf16[2,2,256,256]{3,2,1,0:T(8,128)(2,1)S(1)}, u32[]{:S(2)}, u32[]{:S(2)}) collective-permute-start(bf16[2,2,256,256]{3,2,1,0:T(8,128)(2,1)S(1)} %collective-permute-done.near_ref), channel_id=1, source_target_pairs={{0,2},{2,4},{4,6},{6,8},{8,10},{10,12},{12,14},{14,16},{16,18},{18... | collective-permute-start | bytes 1572872 | tf_op jit(solution)/shard_map/ppermute | solution.py:23
  107.9 16.7 %collective-permute-done.1.far_ref = bf16[2,2,256,256]{3,2,1,0:T(8,128)(2,1)S(1)} collective-permute-done((bf16[2,2,256,256]{3,2,1,0:T(8,128)(2,1)S(1)}, bf16[2,2,256,256]{3,2,1,0:T(8,128)(2,1)S(1)}, u32[]{:S(2)}, u32[]{:S(2)}) %collective-permute-start.1) | collective-permute-done | bytes 524320 | tf_op jit(solution)/shard_map/ppermute | solution.py:23
  124.6 0.0 copy-done.1
  124.6 0.0 copy-done.2
  124.6 2.0 %window.1 = (f32[256,512]{1,0:T(8,128)S(1)}, bf16[2,256,256]{2,1,0:T(8,128)(2,1)S(1)}) custom-call(s32[1]{0:T(128)} %bitcast.place_ref, s32[384]{0:T(512)S(1)} %copy-done.2, bf16[256,2,256]{2,1,0:T(2,128)(2,1)S(1)} %copy-done.1, bf16[2,2,256,256]{3,2,1,0:T(8,128)(2,1)S(1)} %copy-done, bf16[2,2,256,256]{3,2,1,0:T(8,128)(2,1)S(1)} %collective-permute-done.near_ref, ...), custom_call_target="tpu_custom_call" | custom-call | flops 402653184 | bytes 3000000 | tf_op jit(solution)/shard_map/window/pallas_call | solution.py:182
  126.7 0.0 all-to-all-done.2
  126.7 2.2 %features.1 = (bf16[256,512]{1,0:T(8,128)(2,1)S(1)}, bf16[4,512,512]{2,1,0:T(8,128)(2,1)S(1)}) custom-call(s32[1]{0:T(128)} %bitcast.place_ref, s32[384]{0:T(512)S(1)} %copy-done.2, bf16[2,256,256]{2,1,0:T(8,128)(2,1)S(1)} %get-tuple-element.16.queries_ref, f32[256,512]{1,0:T(8,128)S(1)} %get-tuple-element.17.window_ref, bf16[1536,256]{1,0:T(8,128)(2,1)S(1)} %bitcast.6, ...), custom_call_target="tpu_custom_call" | custom-call | flops 201326592 | bytes 2000000 | tf_op jit(solution)/shard_map/features/pallas_call | solution.py:231
  128.9 3.7 %collective-permute-start.2 = (bf16[256,512]{1,0:T(8,128)(2,1)S(1)}, bf16[256,512]{1,0:T(8,128)(2,1)S(1)}, u32[]{:S(2)}, u32[]{:S(2)}) collective-permute-start(bf16[256,512]{1,0:T(8,128)(2,1)S(1)} %get-tuple-element.20.own_ref), channel_id=1, source_target_pairs={{0,1},{1,0},{2,3},{3,2},{4,5},{5,4},{6,7},{7,6},{8,9},{9,8},{10,11... | collective-permute-start | bytes 786440 | tf_op jit(solution)/shard_map/ppermute | solution.py:405
  132.6 0.0 collective-permute-done.3.theirs_ref
  132.6 1.6 %own_project.1 = (f32[256,2048]{1,0:T(8,128)S(1)}, bf16[4,512,512]{2,1,0:T(8,128)(2,1)S(1)}) custom-call(bf16[256,512]{1,0:T(8,128)(2,1)S(1)} %get-tuple-element.20.own_ref, bf16[4,512,512]{2,1,0:T(8,128)(2,1)S(1)} %get-tuple-element.21.weight_ref, bf16[4,512,512]{2,1,0:T(8,128)(2,1)} %collective-permute-done.3.theirs_ref), custom_call_target="tpu_custom_call" | custom-call | flops 536870912 | bytes 4000000 | tf_op jit(solution)/shard_map/own_project/pallas_call | solution.py:287
  134.2 0.0 collective-permute-done.2.other_ref
  134.2 1.5 %project.1 = bf16[256,2048]{1,0:T(8,128)(2,1)} custom-call(bf16[256,512]{1,0:T(8,128)(2,1)S(1)} %collective-permute-done.2.other_ref, bf16[4,512,512]{2,1,0:T(8,128)(2,1)S(1)} %get-tuple-element.23.weight_ref, f32[256,2048]{1,0:T(8,128)S(1)} %get-tuple-element.24.own_ref), custom_call_target="tpu_custom_call" | custom-call | flops 536870912 | bytes 6000000 | tf_op jit(solution)/shard_map/project/pallas_call | solution.py:324
Async XLA Ops:
  42.6 21.5 %all-to-all-start.1 = ((f32[4,16,256]{2,1,0:T(8,128)}), f32[4,16,256]{2,1,0:T(8,128)S(1)}, u32[]{:S(2)}, u32[]{:S(2)}) async-start(f32[4,16,256]{2,1,0:T(8,128)} %collect.1), calls=%async_computation.1 | async-start | bytes 131072 | tf_op jit(solution)/shard_map/all_to_all | solution.py:394
  65.1 61.5 %all-to-all-start.2 = ((bf16[96,16,256]{2,1,0:T(8,128)(2,1)}), bf16[96,16,256]{2,1,0:T(8,128)(2,1)S(1)}, u32[]{:S(2)}, u32[]{:S(2)}) async-start(bf16[96,16,256]{2,1,0:T(8,128)(2,1)} %refresh.1), calls=%async_computation.2 | async-start | bytes 1572864 | tf_op jit(solution)/shard_map/all_to_all | solution.py:400
  73.8 9.8 %copy-start = (bf16[2,2,256,256]{3,2,1,0:T(8,128)(2,1)S(1)}, bf16[2,2,256,256]{3,2,1,0:T(8,128)(2,1)}, u32[]{:S(2)}) copy-start(bf16[2,2,256,256]{3,2,1,0:T(8,128)(2,1)} %get-tuple-element.15.own_ref) | copy-start | bytes 1572868
  73.8 50.8 %copy-start.1 = (bf16[256,2,256]{2,1,0:T(2,128)(2,1)S(1)}, bf16[256,2,256]{2,1,0:T(2,128)(2,1)}, u32[]{:S(2)}) copy-start(bf16[256,2,256]{2,1,0:T(2,128)(2,1)} %queries_ref.1) | copy-start | bytes 786436
  73.8 50.8 %copy-start.2 = (s32[384]{0:T(512)S(1)}, s32[384]{0:T(512)}, u32[]{:S(2)}) copy-start(s32[384]{0:T(512)} %counts_ref.5) | copy-start | bytes 4612
  78.6 53.9 %collective-permute-start.3 = (bf16[4,512,512]{2,1,0:T(8,128)(2,1)}, bf16[4,512,512]{2,1,0:T(8,128)(2,1)}, u32[]{:S(2)}, u32[]{:S(2)}) collective-permute-start(bf16[4,512,512]{2,1,0:T(8,128)(2,1)} %get-tuple-element.22), channel_id=1, source_target_pairs={{0,1},{1,0},{2,3},{3,2},{4,5},{5,4},{6,7},{7,6},{8,9},{9,8},{10,11... | collective-permute-start | bytes 6291464 | tf_op jit(solution)/shard_map/ppermute | solution.py:392
  83.6 22.3 %collective-permute-start = (bf16[2,2,256,256]{3,2,1,0:T(8,128)(2,1)S(1)}, bf16[2,2,256,256]{3,2,1,0:T(8,128)(2,1)S(1)}, u32[]{:S(2)}, u32[]{:S(2)}) collective-permute-start(bf16[2,2,256,256]{3,2,1,0:T(8,128)(2,1)S(1)} %copy-done), channel_id=1, source_target_pairs={{0,2},{2,4},{4,6},{6,8},{8,10},{10,12},{12,14},{14,16},{16,18},{18... | collective-permute-start | bytes 1572872 | tf_op jit(solution)/shard_map/ppermute | solution.py:23
  106.0 18.7 %collective-permute-start.1 = (bf16[2,2,256,256]{3,2,1,0:T(8,128)(2,1)S(1)}, bf16[2,2,256,256]{3,2,1,0:T(8,128)(2,1)S(1)}, u32[]{:S(2)}, u32[]{:S(2)}) collective-permute-start(bf16[2,2,256,256]{3,2,1,0:T(8,128)(2,1)S(1)} %collective-permute-done.near_ref), channel_id=1, source_target_pairs={{0,2},{2,4},{4,6},{6,8},{8,10},{10,12},{12,14},{14,16},{16,18},{18... | collective-permute-start | bytes 1572872 | tf_op jit(solution)/shard_map/ppermute | solution.py:23
  128.9 5.3 %collective-permute-start.2 = (bf16[256,512]{1,0:T(8,128)(2,1)S(1)}, bf16[256,512]{1,0:T(8,128)(2,1)S(1)}, u32[]{:S(2)}, u32[]{:S(2)}) collective-permute-start(bf16[256,512]{1,0:T(8,128)(2,1)S(1)} %get-tuple-element.20.own_ref), channel_id=1, source_target_pairs={{0,1},{1,0},{2,3},{3,2},{4,5},{5,4},{6,7},{7,6},{8,9},{9,8},{10,11... | collective-permute-start | bytes 786440 | tf_op jit(solution)/shard_map/ppermute | solution.py:405

commit v9 on v7

--- a/solution.py
+++ b/solution.py
@@ -21,6 +21,10 @@
 def passed_along(value, steps):
     count = lax.axis_size(CTX)
     return lax.ppermute(value, CTX, [(source, source + steps) for source in range(count - steps)])
+
+
+def resting(value):
+    return pltpu.with_memory_space_constraint(value, pltpu.MemorySpace.HBM)
 
 
 def product(left, right, left_dim, right_dim):
@@ -155,7 +159,19 @@
     )(place, counts, queries, own, near, far)
 
 
-def feature_kernel(place_ref, counts_ref, queries_ref, window_ref, weights_ref, features_ref):
+def feature_kernel(
+    place_ref,
+    counts_ref,
+    queries_ref,
+    window_ref,
+    weights_ref,
+    own_weight_ref,
+    features_ref,
+    brought_ref,
+    sem,
+):
+    brought = pltpu.make_async_copy(own_weight_ref, brought_ref, sem)
+    brought.start()
     heads, tokens, width = queries_ref.shape
     valid = lax.broadcasted_iota(jnp.int32, (tokens, 1), 0) < place_count(counts_ref, place_ref, 0)
     for head in range(heads):
@@ -169,21 +185,26 @@
         features_ref[:, columns] = jnp.where(
             valid, learned + window_ref[:, columns], 0.0
         ).astype(jnp.bfloat16)
-
-
-def features_of(place, counts, queries, window, new_flat):
+    brought.wait()
+
+
+def features_of(place, counts, queries, window, new_flat, own_weight):
     heads, tokens, width = queries.shape
     return pl.pallas_call(
         feature_kernel,
-        out_shape=jax.ShapeDtypeStruct((tokens, heads * width), jnp.bfloat16),
-        in_specs=[SMEM, SMEM] + [VMEM] * 3,
-        out_specs=VMEM,
+        out_shape=(
+            jax.ShapeDtypeStruct((tokens, heads * width), jnp.bfloat16),
+            jax.ShapeDtypeStruct(own_weight.shape, jnp.bfloat16),
+        ),
+        in_specs=[SMEM, SMEM] + [VMEM] * 3 + [pl.BlockSpec(memory_space=pl.ANY)],
+        out_specs=(VMEM, VMEM),
+        scratch_shapes=[pltpu.SemaphoreType.DMA],
         name="features",
         compiler_params=pltpu.CompilerParams(vmem_limit_bytes=VMEM_BYTES),
         cost_estimate=pl.CostEstimate(
             flops=6 * tokens * width * width * heads, transcendentals=131072, bytes_accessed=2000000
         ),
-    )(place, counts, queries, window, new_flat)
+    )(place, counts, queries, window, new_flat, own_weight)
 
 
 def split_kernel(place_ref, mine_in_ref, theirs_in_ref, mine_ref, theirs_ref):
@@ -213,54 +234,46 @@
     )(head_place, out_weight, out_weight)
 
 
-def own_project_kernel(own_ref, weight_ref, out_ref, held_weight, sems):
-    fetches = [
-        pltpu.make_async_copy(weight_ref.at[step], held_weight.at[step], sems.at[step])
-        for step in range(TILES)
-    ]
-    for fetch in fetches:
-        fetch.start()
-    tile = held_weight.shape[2]
+def own_project_kernel(own_ref, weight_ref, theirs_ref, out_ref, brought_ref, sem):
+    brought = pltpu.make_async_copy(theirs_ref, brought_ref, sem)
+    brought.start()
+    tile = weight_ref.shape[2]
     for step in range(TILES):
-        fetches[step].wait()
         out_ref[:, step * tile : (step + 1) * tile] = jnp.dot(
-            own_ref[...], held_weight[step], preferred_element_type=jnp.float32
-        )
-
-
-def own_projected(own, weight):
+            own_ref[...], weight_ref[step], preferred_element_type=jnp.float32
+        )
+    brought.wait()
+
+
+def own_projected(own, weight, theirs):
     return pl.pallas_call(
         own_project_kernel,
-        out_shape=jax.ShapeDtypeStruct((own.shape[0], TILES * weight.shape[2]), jnp.float32),
-        in_specs=[VMEM, pl.BlockSpec(memory_space=pl.ANY)],
-        out_specs=VMEM,
-        scratch_shapes=[pltpu.VMEM(weight.shape, jnp.bfloat16), pltpu.SemaphoreType.DMA((TILES,))],
+        out_shape=(
+            jax.ShapeDtypeStruct((own.shape[0], TILES * weight.shape[2]), jnp.float32),
+            jax.ShapeDtypeStruct(theirs.shape, jnp.bfloat16),
+        ),
+        in_specs=[VMEM, VMEM, pl.BlockSpec(memory_space=pl.ANY)],
+        out_specs=(VMEM, VMEM),
+        scratch_shapes=[pltpu.SemaphoreType.DMA],
         name="own_project",
         compiler_params=pltpu.CompilerParams(vmem_limit_bytes=VMEM_BYTES),
         cost_estimate=pl.CostEstimate(
-            flops=2 * own.shape[0] * weight.size, transcendentals=0, bytes_accessed=4000000
-        ),
-    )(own, weight)
-
-
-def project_kernel(other_ref, weight_ref, own_ref, out_ref, held_weight, held_out, sems):
-    fetches = [
-        pltpu.make_async_copy(weight_ref.at[step], held_weight.at[step], sems.at[0, step])
-        for step in range(TILES)
-    ]
-    for fetch in fetches:
-        fetch.start()
-    tile = held_weight.shape[2]
+            flops=2 * own.shape[0] * theirs.size, transcendentals=0, bytes_accessed=4000000
+        ),
+    )(own, weight, theirs)
+
+
+def project_kernel(other_ref, weight_ref, own_ref, out_ref, held_out, sems):
+    tile = held_out.shape[2]
     stores = []
     for step in range(TILES):
         columns = slice(step * tile, (step + 1) * tile)
-        fetches[step].wait()
         held_out[step] = (
             own_ref[:, columns]
-            + jnp.dot(other_ref[...], held_weight[step], preferred_element_type=jnp.float32)
+            + jnp.dot(other_ref[...], weight_ref[step], preferred_element_type=jnp.float32)
         ).astype(jnp.bfloat16)
         stores.append(
-            pltpu.make_async_copy(held_out.at[step], out_ref.at[:, columns], sems.at[1, step])
+            pltpu.make_async_copy(held_out.at[step], out_ref.at[:, columns], sems.at[step])
         )
         stores[step].start()
     for store in stores:
@@ -273,12 +286,11 @@
     return pl.pallas_call(
         project_kernel,
         out_shape=jax.ShapeDtypeStruct((tokens, TILES * tile), jnp.bfloat16),
-        in_specs=[VMEM, pl.BlockSpec(memory_space=pl.ANY), VMEM],
+        in_specs=[VMEM, VMEM, VMEM],
         out_specs=pl.BlockSpec(memory_space=pl.ANY),
         scratch_shapes=[
-            pltpu.VMEM(weight.shape, jnp.bfloat16),
             pltpu.VMEM((TILES, tokens, tile), jnp.bfloat16),
-            pltpu.SemaphoreType.DMA((2, TILES)),
+            pltpu.SemaphoreType.DMA((TILES,)),
         ],
         name="project",
         compiler_params=pltpu.CompilerParams(vmem_limit_bytes=VMEM_BYTES),
@@ -349,14 +361,12 @@
     new_rows = refreshed(tok_rows * device_count, plane_count, sums, old_rows)
     new_flat = lax.all_to_all(new_rows, "p", 0, 0, tiled=True).reshape(-1, head_width)
     window, turned_queries = window_attention(place, counts, queries, pairs, near, far)
-    features = features_of(place, counts, turned_queries, window, new_flat)
+    features, own_weight = features_of(
+        place, counts, turned_queries, window, new_flat, resting(out_own)
+    )
     other = lax.ppermute(features, "head", [(0, 1), (1, 0)])
-    own_product = own_projected(
-        features, pltpu.with_memory_space_constraint(out_own, pltpu.MemorySpace.HBM)
-    )
-    return projected(
-        other, pltpu.with_memory_space_constraint(out_other, pltpu.MemorySpace.HBM), own_product
-    )
+    own_product, brought = own_projected(features, own_weight, resting(out_other))
+    return projected(other, brought, own_product)
 
 
 def solution(mesh):

time: 136 us -> 135 us (level)
    pallas_call x1, Pallas kernels: 3.03 us -> 1.45 us  [projected(): pl.pallas_call(project_kernel, out_shape=jax.ShapeDtypeStruct((tokens, TI...]
where the time goes in v9:
time: 135 us
  waiting for transfers between devices  44.6 us (33%)
  blocking collectives  35.9 us (27%)
  starting transfers between devices  34.5 us (26%)
  Pallas kernels  18.7 us (14%)
    ppermute x2, waiting for transfers between devices, passed_along(): lax.ppermute(value, CTX, [(source, source + steps) for source in range(co...  36 us
    all_to_all x1, blocking collectives, shards(): lax.all_to_all(local_grad.reshape(plane_count, -1, head_width), 'p', 0, 0...  35.9 us
    all_to_all x1, starting transfers between devices, shards(): sums = lax.all_to_all(sums, 'z', 0, 0, tiled=True)  12.2 us
    all_to_all x1, starting transfers between devices, shards(): lax.all_to_all(new_rows, 'p', 0, 0, tiled=True).reshape(-1, head_width)  8.67 us
    all_to_all x1, waiting for transfers between devices, shards(): sums = lax.all_to_all(sums, 'z', 0, 0, tiled=True)  8.56 us
    ppermute x2, starting transfers between devices, passed_along(): lax.ppermute(value, CTX, [(source, source + steps) for source in range(co...  5.01 us
    ppermute x1, starting transfers between devices, shards(): out_other = lax.ppermute(out_theirs, 'head', [(0, 1), (1, 0)])  4.98 us
    pallas_call x1, Pallas kernels, local_gradient(): pl.pallas_call(gradient_kernel, out_shape=(jax.ShapeDtypeStruct((heads *...  4.85 us
  transfers between devices with their start and end apart: 6, of which 3 were waited for; matrix products, arithmetic and copies ran while one was open for 1% of the time, Pallas kernels for 8%

profile of v9, /device:TPU:65, one launch (start us, length us, event | category | flops | bytes accessed | tf_op | source)
XLA Modules:
  0.0 134.6 jit_solution(16465437694502727064)
XLA Ops:
  0.0 4.8 %gradient.1 = (bf16[1536,256]{1,0:T(8,128)(2,1)}, bf16[2,2,256,256]{3,2,1,0:T(8,128)(2,1)}) custom-call(s32[1]{0:T(128)} %bitcast.place_ref, s32[384]{0:T(512)} %counts_ref.5, bf16[256,2,256]{2,1,0:T(2,128)(2,1)} %keys_ref.1, bf16[256,2,256]{2,1,0:T(2,128)(2,1)} %values_ref.1, f32[2,256]{1,0:T(2,128)} %bitcast.9, f32[2,3,256,256]{3,2,1,0:T(8,128)} %weights_ref.1), custom_call_target="tpu_custom_call" | custom-call | flops 469762048 | bytes 3000000 | tf_op jit(solution)/shard_map/gradient/pallas_call | solution.py:89
  4.8 35.9 %all_to_all.15.blocks_ref = bf16[96,16,256]{2,1,0:T(8,128)(2,1)S(1)} all-to-all(bf16[96,16,256]{2,1,0:T(8,128)(2,1)} %bitcast.8), channel_id=1, replica_groups=mesh['z'=4,'p'=96,'head'=2] {'p'}, dimensions={0} | all-to-all | bytes 1572864 | tf_op jit(solution)/shard_map/all_to_all | solution.py:350
  40.7 0.8 collect.1
  41.5 12.2 %all-to-all-start.1 = ((f32[4,16,256]{2,1,0:T(8,128)}), f32[4,16,256]{2,1,0:T(8,128)S(1)}, u32[]{:S(2)}, u32[]{:S(2)}) async-start(f32[4,16,256]{2,1,0:T(8,128)} %collect.1), calls=%async_computation.1 | async-start | bytes 131072 | tf_op jit(solution)/shard_map/all_to_all | solution.py:356
  53.7 0.7 constant_dynamic-slice_fusion.old_ref
  54.4 8.6 %all-to-all-done.1.sums_ref = f32[4,16,256]{2,1,0:T(8,128)S(1)} async-done(((f32[4,16,256]{2,1,0:T(8,128)}), f32[4,16,256]{2,1,0:T(8,128)S(1)}, u32[]{:S(2)}, u32[]{:S(2)}) %all-to-all-start.1) | async-done | bytes 65568 | tf_op jit(solution)/shard_map/all_to_all | solution.py:356
  63.0 1.0 refresh.1
  64.0 8.7 %all-to-all-start.2 = ((bf16[96,16,256]{2,1,0:T(8,128)(2,1)}), bf16[96,16,256]{2,1,0:T(8,128)(2,1)S(1)}, u32[]{:S(2)}, u32[]{:S(2)}) async-start(bf16[96,16,256]{2,1,0:T(8,128)(2,1)} %refresh.1), calls=%async_computation.2 | async-start | bytes 1572864 | tf_op jit(solution)/shard_map/all_to_all | solution.py:362
  72.7 0.0 copy-start
  72.7 0.0 copy-start.1
  72.7 0.0 copy-start.2
  72.7 4.8 %split.1 = (bf16[4,512,512]{2,1,0:T(8,128)(2,1)}, bf16[4,512,512]{2,1,0:T(8,128)(2,1)}) custom-call(s32[1]{0:T(128)} %bitcast.5.place_ref, bf16[512,4096]{1,0:T(8,128)(2,1)} %theirs_in_ref.1, bf16[512,4096]{1,0:T(8,128)(2,1)} %theirs_in_ref.1), custom_call_target="tpu_custom_call" | custom-call | bytes 8000000 | tf_op jit(solution)/shard_map/split/pallas_call | solution.py:220
  77.5 5.0 %collective-permute-start.3 = (bf16[4,512,512]{2,1,0:T(8,128)(2,1)}, bf16[4,512,512]{2,1,0:T(8,128)(2,1)}, u32[]{:S(2)}, u32[]{:S(2)}) collective-permute-start(bf16[4,512,512]{2,1,0:T(8,128)(2,1)} %get-tuple-element.22), channel_id=1, source_target_pairs={{0,1},{1,0},{2,3},{3,2},{4,5},{5,4},{6,7},{7,6},{8,9},{9,8},{10,11... | collective-permute-start | bytes 6291464 | tf_op jit(solution)/shard_map/ppermute | solution.py:354
  82.5 0.0 copy-done
  82.5 3.1 %collective-permute-start = (bf16[2,2,256,256]{3,2,1,0:T(8,128)(2,1)S(1)}, bf16[2,2,256,256]{3,2,1,0:T(8,128)(2,1)S(1)}, u32[]{:S(2)}, u32[]{:S(2)}) collective-permute-start(bf16[2,2,256,256]{3,2,1,0:T(8,128)(2,1)S(1)} %copy-done), channel_id=1, source_target_pairs={{0,2},{2,4},{4,6},{6,8},{8,10},{10,12},{12,14},{14,16},{16,18},{18... | collective-permute-start | bytes 1572872 | tf_op jit(solution)/shard_map/ppermute | solution.py:23
  85.6 19.2 %collective-permute-done.near_ref = bf16[2,2,256,256]{3,2,1,0:T(8,128)(2,1)S(1)} collective-permute-done((bf16[2,2,256,256]{3,2,1,0:T(8,128)(2,1)S(1)}, bf16[2,2,256,256]{3,2,1,0:T(8,128)(2,1)S(1)}, u32[]{:S(2)}, u32[]{:S(2)}) %collective-permute-start) | collective-permute-done | bytes 524320 | tf_op jit(solution)/shard_map/ppermute | solution.py:23
  104.9 1.9 %collective-permute-start.1 = (bf16[2,2,256,256]{3,2,1,0:T(8,128)(2,1)S(1)}, bf16[2,2,256,256]{3,2,1,0:T(8,128)(2,1)S(1)}, u32[]{:S(2)}, u32[]{:S(2)}) collective-permute-start(bf16[2,2,256,256]{3,2,1,0:T(8,128)(2,1)S(1)} %collective-permute-done.near_ref), channel_id=1, source_target_pairs={{0,2},{2,4},{4,6},{6,8},{8,10},{10,12},{12,14},{14,16},{16,18},{18... | collective-permute-start | bytes 1572872 | tf_op jit(solution)/shard_map/ppermute | solution.py:23
  106.8 16.7 %collective-permute-done.1.far_ref = bf16[2,2,256,256]{3,2,1,0:T(8,128)(2,1)S(1)} collective-permute-done((bf16[2,2,256,256]{3,2,1,0:T(8,128)(2,1)S(1)}, bf16[2,2,256,256]{3,2,1,0:T(8,128)(2,1)S(1)}, u32[]{:S(2)}, u32[]{:S(2)}) %collective-permute-start.1) | collective-permute-done | bytes 524320 | tf_op jit(solution)/shard_map/ppermute | solution.py:23
  123.5 0.0 copy-done.1
  123.5 0.0 copy-done.2
  123.5 2.0 %window.1 = (f32[256,512]{1,0:T(8,128)S(1)}, bf16[2,256,256]{2,1,0:T(8,128)(2,1)S(1)}) custom-call(s32[1]{0:T(128)} %bitcast.place_ref, s32[384]{0:T(512)S(1)} %copy-done.2, bf16[256,2,256]{2,1,0:T(2,128)(2,1)S(1)} %copy-done.1, bf16[2,2,256,256]{3,2,1,0:T(8,128)(2,1)S(1)} %copy-done, bf16[2,2,256,256]{3,2,1,0:T(8,128)(2,1)S(1)} %collective-permute-done.near_ref, ...), custom_call_target="tpu_custom_call" | custom-call | flops 402653184 | bytes 3000000 | tf_op jit(solution)/shard_map/window/pallas_call | solution.py:144
  125.6 0.0 all-to-all-done.2
  125.6 2.2 %features.1 = (bf16[256,512]{1,0:T(8,128)(2,1)S(1)}, bf16[4,512,512]{2,1,0:T(8,128)(2,1)S(1)}) custom-call(s32[1]{0:T(128)} %bitcast.place_ref, s32[384]{0:T(512)S(1)} %copy-done.2, bf16[2,256,256]{2,1,0:T(8,128)(2,1)S(1)} %get-tuple-element.16.queries_ref, f32[256,512]{1,0:T(8,128)S(1)} %get-tuple-element.17.window_ref, bf16[1536,256]{1,0:T(8,128)(2,1)S(1)} %bitcast.6, ...), custom_call_target="tpu_custom_call" | custom-call | flops 201326592 | bytes 2000000 | tf_op jit(solution)/shard_map/features/pallas_call | solution.py:193
  127.8 3.7 %collective-permute-start.2 = (bf16[256,512]{1,0:T(8,128)(2,1)S(1)}, bf16[256,512]{1,0:T(8,128)(2,1)S(1)}, u32[]{:S(2)}, u32[]{:S(2)}) collective-permute-start(bf16[256,512]{1,0:T(8,128)(2,1)S(1)} %get-tuple-element.20.own_ref), channel_id=1, source_target_pairs={{0,1},{1,0},{2,3},{3,2},{4,5},{5,4},{6,7},{7,6},{8,9},{9,8},{10,11... | collective-permute-start | bytes 786440 | tf_op jit(solution)/shard_map/ppermute | solution.py:367
  131.4 0.0 collective-permute-done.3.theirs_ref
  131.5 1.6 %own_project.1 = (f32[256,2048]{1,0:T(8,128)S(1)}, bf16[4,512,512]{2,1,0:T(8,128)(2,1)S(1)}) custom-call(bf16[256,512]{1,0:T(8,128)(2,1)S(1)} %get-tuple-element.20.own_ref, bf16[4,512,512]{2,1,0:T(8,128)(2,1)S(1)} %get-tuple-element.21.weight_ref, bf16[4,512,512]{2,1,0:T(8,128)(2,1)} %collective-permute-done.3.theirs_ref), custom_call_target="tpu_custom_call" | custom-call | flops 536870912 | bytes 4000000 | tf_op jit(solution)/shard_map/own_project/pallas_call | solution.py:249
  133.1 0.0 collective-permute-done.2.other_ref
  133.1 1.5 %project.1 = bf16[256,2048]{1,0:T(8,128)(2,1)} custom-call(bf16[256,512]{1,0:T(8,128)(2,1)S(1)} %collective-permute-done.2.other_ref, bf16[4,512,512]{2,1,0:T(8,128)(2,1)S(1)} %get-tuple-element.23.weight_ref, f32[256,2048]{1,0:T(8,128)S(1)} %get-tuple-element.24.own_ref), custom_call_target="tpu_custom_call" | custom-call | flops 536870912 | bytes 6000000 | tf_op jit(solution)/shard_map/project/pallas_call | solution.py:286
Async XLA Ops:
  41.5 21.5 %all-to-all-start.1 = ((f32[4,16,256]{2,1,0:T(8,128)}), f32[4,16,256]{2,1,0:T(8,128)S(1)}, u32[]{:S(2)}, u32[]{:S(2)}) async-start(f32[4,16,256]{2,1,0:T(8,128)} %collect.1), calls=%async_computation.1 | async-start | bytes 131072 | tf_op jit(solution)/shard_map/all_to_all | solution.py:356
  64.0 61.5 %all-to-all-start.2 = ((bf16[96,16,256]{2,1,0:T(8,128)(2,1)}), bf16[96,16,256]{2,1,0:T(8,128)(2,1)S(1)}, u32[]{:S(2)}, u32[]{:S(2)}) async-start(bf16[96,16,256]{2,1,0:T(8,128)(2,1)} %refresh.1), calls=%async_computation.2 | async-start | bytes 1572864 | tf_op jit(solution)/shard_map/all_to_all | solution.py:362
  72.7 9.8 %copy-start = (bf16[2,2,256,256]{3,2,1,0:T(8,128)(2,1)S(1)}, bf16[2,2,256,256]{3,2,1,0:T(8,128)(2,1)}, u32[]{:S(2)}) copy-start(bf16[2,2,256,256]{3,2,1,0:T(8,128)(2,1)} %get-tuple-element.15.own_ref) | copy-start | bytes 1572868
  72.7 50.8 %copy-start.1 = (bf16[256,2,256]{2,1,0:T(2,128)(2,1)S(1)}, bf16[256,2,256]{2,1,0:T(2,128)(2,1)}, u32[]{:S(2)}) copy-start(bf16[256,2,256]{2,1,0:T(2,128)(2,1)} %queries_ref.1) | copy-start | bytes 786436
  72.7 50.8 %copy-start.2 = (s32[384]{0:T(512)S(1)}, s32[384]{0:T(512)}, u32[]{:S(2)}) copy-start(s32[384]{0:T(512)} %counts_ref.5) | copy-start | bytes 4612
  77.5 53.9 %collective-permute-start.3 = (bf16[4,512,512]{2,1,0:T(8,128)(2,1)}, bf16[4,512,512]{2,1,0:T(8,128)(2,1)}, u32[]{:S(2)}, u32[]{:S(2)}) collective-permute-start(bf16[4,512,512]{2,1,0:T(8,128)(2,1)} %get-tuple-element.22), channel_id=1, source_target_pairs={{0,1},{1,0},{2,3},{3,2},{4,5},{5,4},{6,7},{7,6},{8,9},{9,8},{10,11... | collective-permute-start | bytes 6291464 | tf_op jit(solution)/shard_map/ppermute | solution.py:354
  82.5 22.3 %collective-permute-start = (bf16[2,2,256,256]{3,2,1,0:T(8,128)(2,1)S(1)}, bf16[2,2,256,256]{3,2,1,0:T(8,128)(2,1)S(1)}, u32[]{:S(2)}, u32[]{:S(2)}) collective-permute-start(bf16[2,2,256,256]{3,2,1,0:T(8,128)(2,1)S(1)} %copy-done), channel_id=1, source_target_pairs={{0,2},{2,4},{4,6},{6,8},{8,10},{10,12},{12,14},{14,16},{16,18},{18... | collective-permute-start | bytes 1572872 | tf_op jit(solution)/shard_map/ppermute | solution.py:23
  104.9 18.7 %collective-permute-start.1 = (bf16[2,2,256,256]{3,2,1,0:T(8,128)(2,1)S(1)}, bf16[2,2,256,256]{3,2,1,0:T(8,128)(2,1)S(1)}, u32[]{:S(2)}, u32[]{:S(2)}) collective-permute-start(bf16[2,2,256,256]{3,2,1,0:T(8,128)(2,1)S(1)} %collective-permute-done.near_ref), channel_id=1, source_target_pairs={{0,2},{2,4},{4,6},{6,8},{8,10},{10,12},{12,14},{14,16},{16,18},{18... | collective-permute-start | bytes 1572872 | tf_op jit(solution)/shard_map/ppermute | solution.py:23
  127.8 5.3 %collective-permute-start.2 = (bf16[256,512]{1,0:T(8,128)(2,1)S(1)}, bf16[256,512]{1,0:T(8,128)(2,1)S(1)}, u32[]{:S(2)}, u32[]{:S(2)}) collective-permute-start(bf16[256,512]{1,0:T(8,128)(2,1)S(1)} %get-tuple-element.20.own_ref), channel_id=1, source_target_pairs={{0,1},{1,0},{2,3},{3,2},{4,5},{5,4},{6,7},{7,6},{8,9},{9,8},{10,11... | collective-permute-start | bytes 786440 | tf_op jit(solution)/shard_map/ppermute | solution.py:367
